TPU v7x, 32 devices: a whole 2x2x4 slice. The times are simulated.
32 devices in a mesh: ep: 8 (over z, y), tp: 4 (over x, core).
Axes of the slice: x: 2, y: 2, z: 4, core: 2. Of those that a mesh axis runs over, the one named last changes fastest.
Arguments:
- tokens: bfloat16 [3072, 2048], P('ep'), may hold values from -6 to 6
- first_gain: bfloat16 [2048], P('ep'), may hold values from 0.5 to 1.5
- query_weight: bfloat16 [2048, 2048], P('ep', 'tp'), may hold values from -0.125 to 0.125
- key_weight: bfloat16 [2048, 2048], P('ep', 'tp'), may hold values from -0.125 to 0.125
- value_weight: bfloat16 [2048, 2048], P('ep', 'tp'), may hold values from -0.125 to 0.125
- output_weight: bfloat16 [2048, 2048], P('tp', 'ep'), may hold values from -1.5 to 1.5
- second_gain: bfloat16 [2048], P('ep'), may hold values from 0.5 to 1.5
- shared_logit: bfloat16 [2048], P('ep'), may hold values from -0.125 to 0.125
- shared_gate: bfloat16 [2048, 5632], P('ep', 'tp'), may hold values from -0.125 to 0.125
- shared_up: bfloat16 [2048, 5632], P('ep', 'tp'), may hold values from -0.125 to 0.125
- shared_down: bfloat16 [5632, 2048], P('tp', 'ep'), may hold values from -0.078125 to 0.078125
- routed_gate_weight: bfloat16 [8, 2048, 1408], P('ep', None, 'tp'), may hold values from -0.125 to 0.125
- routed_up_weight: bfloat16 [8, 2048, 1408], P('ep', None, 'tp'), may hold values from -0.125 to 0.125
- expert_down: bfloat16 [8, 1408, 2048], P('ep', 'tp'), may hold values from -0.15625 to 0.15625
- route_ids: int32 [3072, 4], P('ep'), may hold values from 0 to 7, all different within a row; in each aligned block of 384 rows (0 to 383, 384 to 767, ...) at most 384 rows name the same one
- route_gates: float32 [3072, 4], P('ep'), may hold values from 0.15 to 0.4
- piece_start: int32 [8], P('ep'), may hold values from 0 to 256, as said below
- piece_length: int32 [8], P('ep'), may hold values from 128 to 256, as said below
- block_grad: bfloat16 [3072, 2048], P('ep'), may hold values from -6 to 6
Outputs:
- block_out: bfloat16 [3072, 2048], P('ep')
- tokens_grad: float32 [3072, 2048], P('ep')
- first_gain_grad: float32 [2048], P('ep')
- query_grad: float32 [2048, 2048], P('ep', 'tp')
- key_grad: float32 [2048, 2048], P('ep', 'tp')
- value_grad: float32 [2048, 2048], P('ep', 'tp')
- output_grad: float32 [2048, 2048], P('tp', 'ep')
- second_gain_grad: float32 [2048], P('ep')
- shared_logit_grad: float32 [2048], P('ep')
- shared_gate_grad: float32 [2048, 5632], P('ep', 'tp')
- shared_up_grad: float32 [2048, 5632], P('ep', 'tp')
- shared_down_grad: float32 [5632, 2048], P('tp', 'ep')
- expert_gate_grad: float32 [8, 2048, 1408], P('ep', None, 'tp')
- expert_up_grad: float32 [8, 2048, 1408], P('ep', None, 'tp')
- expert_down_grad: float32 [8, 1408, 2048], P('ep', 'tp')
- rms_values: float32 [8, 3], P('ep')
Inputs may be any that keep to these rules, and one draw needn't show every extreme that they name: `route_ids`: each token names 4 different experts; among the 384 tokens of one sequence no expert is named by more than 384 tokens, and one expert by exactly 384. piece_start + piece_length <= 384 in every sequence. `piece_length`: some sequence has a piece of exactly 256 tokens.
All inputs are finite; a program needn't handle non-finite values.
Results may differ from a plain program's by a relative error of at most 0.014.
Values may be sent and summed in bfloat16 or wider, within the bound.
No kernel may reach another device: no remote copies, remote signals or barrier semaphores. Data moves between devices by JAX's collectives and lax.ppermute only.
A program may use at most 256 MiB of HBM per device.

v0:
```python
import jax
import jax.numpy as jnp
from jax import lax
from jax.sharding import PartitionSpec as P

HD = 128


EPS = 1e-06


def matrix_product(left, right):
    return jnp.dot(left, right, preferred_element_type=jnp.float32)


def left_matrix_product(left, right):
    return lax.dot_general(
        left, right, (((0,), (0,)), ((), ())), preferred_element_type=jnp.float32
    )


def right_product(left, right):
    return lax.dot_general(
        left, right, (((1,), (1,)), ((), ())), preferred_element_type=jnp.float32
    )


def slot_index(route_rows, experts, capacity):
    count, chosen_count = route_rows.shape
    chosen = route_rows.reshape(count * chosen_count)
    onehot = (chosen[:, None] == jnp.arange(experts, dtype=jnp.int32)[None, :]).astype(jnp.int32)
    earlier = jnp.cumsum(onehot, axis=0) - onehot
    placed = jnp.sum(earlier * onehot, axis=1)
    return chosen * capacity + placed


def rms_scale(values):
    return lax.rsqrt(jnp.mean(values * values, axis=-1, keepdims=True) + EPS)


def norm_back(grad, values, scale, gain):
    weighted = grad * gain
    inner = jnp.mean(values * weighted, axis=-1, keepdims=True)
    return (scale * weighted - values * scale**3 * inner, jnp.sum(grad * values * scale, axis=0))


def gated_back(grad_hidden, gate_val, up_val):
    squash = jax.nn.sigmoid(gate_val)
    grad_gate = grad_hidden * up_val * squash * (1.0 + gate_val * (1.0 - squash))
    grad_up = grad_hidden * gate_val * squash
    return (grad_gate.astype(jnp.bfloat16), grad_up.astype(jnp.bfloat16))


def masked_scores(query, key, visible, factor):
    scores = jnp.einsum("qhd,khd->hqk", query, key, preferred_element_type=jnp.float32) * factor
    return jnp.where(visible[None], scores, -1e30)


def expert_leading_rows(token_rows, gate_w, up_weight_matrix):
    expert_gate_product = matrix_product(token_rows, gate_w)
    expert_up_product = matrix_product(token_rows, up_weight_matrix)
    return (
        expert_gate_product,
        expert_up_product,
        (jax.nn.silu(expert_gate_product) * expert_up_product).astype(jnp.bfloat16),
    )


def on_device(
    tokens,
    first_gain,
    query_weight,
    key_weight,
    value_weight,
    output_weight,
    second_gain,
    shared_logit,
    shared_gate,
    shared_up,
    shared_down,
    routed_gate_weight,
    routed_up_weight,
    expert_down,
    route_ids,
    route_gates,
    piece_start,
    piece_length,
    block_grad,
):
    groups = lax.axis_size("ep")
    count, width = tokens.shape
    chosen_count = route_ids.shape[1]
    capacity = 2 * count * chosen_count // groups
    local_heads = query_weight.shape[1] // HD
    factor = HD ** (-0.5)
    gathered = (
        lax.all_gather(first_gain, "ep", axis=0, tiled=True),
        lax.all_gather(query_weight, "ep", axis=0, tiled=True),
        lax.all_gather(key_weight, "ep", axis=0, tiled=True),
        lax.all_gather(value_weight, "ep", axis=0, tiled=True),
        lax.all_gather(output_weight, "ep", axis=1, tiled=True),
        lax.all_gather(second_gain, "ep", axis=0, tiled=True),
        lax.all_gather(shared_logit, "ep", axis=0, tiled=True),
        lax.all_gather(shared_gate, "ep", axis=0, tiled=True),
        lax.all_gather(shared_up, "ep", axis=0, tiled=True),
        lax.all_gather(shared_down, "ep", axis=1, tiled=True),
    )
    gain_one, w_query, w_key, w_value, w_output, gain_two, logit_vec, s_gate, s_up, s_down = (
        gathered
    )
    gain_one32 = gain_one.astype(jnp.float32)
    gain_two32 = gain_two.astype(jnp.float32)
    inputs32 = tokens.astype(jnp.float32)
    scale_one = rms_scale(inputs32)
    act1 = (inputs32 * scale_one * gain_one32).astype(jnp.bfloat16)
    query = matrix_product(act1, w_query).astype(jnp.bfloat16).reshape(count, local_heads, HD)
    key = matrix_product(act1, w_key).astype(jnp.bfloat16).reshape(count, local_heads, HD)
    value = matrix_product(act1, w_value).astype(jnp.bfloat16).reshape(count, local_heads, HD)
    positions = jnp.arange(count, dtype=jnp.int32)
    start = piece_start[0]
    inside = (positions >= start) & (positions < start + piece_length[0])
    visible = (positions[None, :] <= positions[:, None]) | inside[:, None] & inside[None, :]
    scores = masked_scores(query, key, visible, factor)
    highest = jnp.max(scores, axis=-1, keepdims=True)
    lse = highest + jnp.log(jnp.sum(jnp.exp(scores - highest), axis=-1, keepdims=True))
    probs = jnp.exp(scores - lse)
    attn_mix = (
        jnp.einsum(
            "hqk,khd->qhd", probs.astype(jnp.bfloat16), value, preferred_element_type=jnp.float32
        )
        .astype(jnp.bfloat16)
        .reshape(count, local_heads * HD)
    )
    attn_branch = lax.psum(matrix_product(attn_mix, w_output), "tp")
    resid = inputs32 + attn_branch
    scale_two = rms_scale(resid)
    act2 = (resid * scale_two * gain_two32).astype(jnp.bfloat16)
    shared_score = jax.nn.sigmoid(jnp.dot(act2, logit_vec, preferred_element_type=jnp.float32))
    sgate = matrix_product(act2, s_gate)
    sup = matrix_product(act2, s_up)
    shidden = (jax.nn.silu(sgate) * sup).astype(jnp.bfloat16)
    shared_part = matrix_product(shidden, s_down)
    slots = slot_index(route_ids, groups, capacity)
    pair_rows = jnp.repeat(act2, chosen_count, axis=0)
    send = jnp.zeros((groups * capacity, width), jnp.bfloat16).at[slots].set(pair_rows)
    send = send.reshape(groups, capacity, width)
    received_rows = lax.all_to_all(send, "ep", split_axis=0, concat_axis=0, tiled=True).reshape(
        groups * capacity, width
    )
    expert_gate_product, expert_up_product, expert_hidden_state = expert_leading_rows(
        received_rows, routed_gate_weight[0], routed_up_weight[0]
    )
    epart = matrix_product(expert_hidden_state, expert_down[0]).astype(jnp.bfloat16)
    returned = lax.all_to_all(
        epart.reshape(groups, capacity, width), "ep", split_axis=0, concat_axis=0, tiled=True
    ).reshape(groups * capacity, width)
    picked = returned[slots].reshape(count, chosen_count, width).astype(jnp.float32)
    routed_local = jnp.sum(route_gates[:, :, None] * picked, axis=1)
    ffn_branch = lax.psum(
        (routed_local + shared_score[:, None] * shared_part).astype(jnp.bfloat16), "tp"
    ).astype(jnp.float32)
    block_out = resid + ffn_branch
    squares = jnp.stack(
        [
            jnp.sum(attn_branch * attn_branch),
            jnp.sum(ffn_branch * ffn_branch),
            jnp.sum(block_out * block_out),
        ]
    )
    rms_values = jnp.sqrt(squares / (count * width))[None, :]
    back_weights = (
        lax.all_gather(first_gain, "ep", axis=0, tiled=True),
        lax.all_gather(query_weight, "ep", axis=0, tiled=True),
        lax.all_gather(key_weight, "ep", axis=0, tiled=True),
        lax.all_gather(value_weight, "ep", axis=0, tiled=True),
        lax.all_gather(output_weight, "ep", axis=1, tiled=True),
        lax.all_gather(second_gain, "ep", axis=0, tiled=True),
        lax.all_gather(shared_logit, "ep", axis=0, tiled=True),
        lax.all_gather(shared_gate, "ep", axis=0, tiled=True),
        lax.all_gather(shared_up, "ep", axis=0, tiled=True),
        lax.all_gather(shared_down, "ep", axis=1, tiled=True),
    )
    gain_one, w_query, w_key, w_value, w_output, gain_two, logit_vec, s_gate, s_up, s_down = (
        back_weights
    )
    gout = block_grad.astype(jnp.float32)
    pair_grads = (route_gates[:, :, None] * gout[:, None, :]).reshape(count * chosen_count, width)
    grad_send = (
        jnp.zeros((groups * capacity, width), jnp.bfloat16)
        .at[slots]
        .set(pair_grads.astype(jnp.bfloat16))
    )
    grad_send = grad_send.reshape(groups, capacity, width)
    gpart = lax.all_to_all(grad_send, "ep", split_axis=0, concat_axis=0, tiled=True).reshape(
        groups * capacity, width
    )
    token_rows_back = lax.all_to_all(send, "ep", split_axis=0, concat_axis=0, tiled=True).reshape(
        groups * capacity, width
    )
    gate_back, up_back, hidden_back = expert_leading_rows(
        token_rows_back, routed_gate_weight[0], routed_up_weight[0]
    )
    down_grad = left_matrix_product(hidden_back, gpart)
    grad_hidden = right_product(gpart, expert_down[0])
    dgate, shared_up_product = gated_back(grad_hidden, gate_back, up_back)
    egate_grad = left_matrix_product(token_rows_back, dgate)
    expert_up_product_grad = left_matrix_product(token_rows_back, shared_up_product)
    grow = (
        right_product(dgate, routed_gate_weight[0])
        + right_product(shared_up_product, routed_up_weight[0])
    ).astype(jnp.bfloat16)
    grad_back = lax.all_to_all(
        grow.reshape(groups, capacity, width), "ep", split_axis=0, concat_axis=0, tiled=True
    ).reshape(groups * capacity, width)
    groute_local = jnp.sum(
        grad_back[slots].reshape(count, chosen_count, width), axis=1, dtype=jnp.float32
    )
    gshared = (shared_score[:, None] * gout).astype(jnp.bfloat16)
    sdown_grad = left_matrix_product(shidden, gshared)
    grad_sh = right_product(gshared, s_down)
    dsgate, dsup = gated_back(grad_sh, sgate, sup)
    sgate_grad = left_matrix_product(act2, dsgate)
    sup_grad = left_matrix_product(act2, dsup)
    gact2_part = groute_local + right_product(dsgate, s_gate) + right_product(dsup, s_up)
    score_part = jnp.sum(gout * shared_part, axis=1)
    gact2_sum, score_sum = lax.psum((gact2_part, score_part), "tp")
    gscore = shared_score * (1.0 - shared_score) * score_sum
    logit_grad = jnp.dot(gscore, act2, preferred_element_type=jnp.float32)
    gact2 = gact2_sum + gscore[:, None] * logit_vec.astype(jnp.float32)[None, :]
    resid_part, gain_two_grad = norm_back(gact2, resid, scale_two, gain_two.astype(jnp.float32))
    gresid = gout + resid_part
    gattn = gresid.astype(jnp.bfloat16)
    output_grad = left_matrix_product(attn_mix, gattn)
    gmix = right_product(gattn, w_output).astype(jnp.bfloat16).reshape(count, local_heads, HD)
    scores = masked_scores(query, key, visible, factor)
    probs = jnp.exp(scores - lse)
    gprob = jnp.einsum("qhd,khd->hqk", gmix, value, preferred_element_type=jnp.float32)
    gvalue = jnp.einsum(
        "hqk,qhd->khd", probs.astype(jnp.bfloat16), gmix, preferred_element_type=jnp.float32
    ).astype(jnp.bfloat16)
    inner = jnp.sum(probs * gprob, axis=-1, keepdims=True)
    gscores = (probs * (gprob - inner)).astype(jnp.bfloat16)
    gquery = (
        jnp.einsum("hqk,khd->qhd", gscores, key, preferred_element_type=jnp.float32) * factor
    ).astype(jnp.bfloat16)
    gkey = (
        jnp.einsum("hqk,qhd->khd", gscores, query, preferred_element_type=jnp.float32) * factor
    ).astype(jnp.bfloat16)
    gquery = gquery.reshape(count, local_heads * HD)
    gkey = gkey.reshape(count, local_heads * HD)
    gvalue = gvalue.reshape(count, local_heads * HD)
    query_grad = left_matrix_product(act1, gquery)
    key_grad = left_matrix_product(act1, gkey)
    value_grad = left_matrix_product(act1, gvalue)
    gact1_part = (
        right_product(gquery, w_query) + right_product(gkey, w_key) + right_product(gvalue, w_value)
    )
    gact1 = lax.psum(gact1_part, "tp")
    input_part, gain_one_grad = norm_back(gact1, inputs32, scale_one, gain_one.astype(jnp.float32))
    tokens_grad = gresid + input_part
    summed = (
        lax.psum_scatter(gain_one_grad, "ep", scatter_dimension=0, tiled=True),
        lax.psum_scatter(query_grad, "ep", scatter_dimension=0, tiled=True),
        lax.psum_scatter(key_grad, "ep", scatter_dimension=0, tiled=True),
        lax.psum_scatter(value_grad, "ep", scatter_dimension=0, tiled=True),
        lax.psum_scatter(output_grad, "ep", scatter_dimension=1, tiled=True),
        lax.psum_scatter(gain_two_grad, "ep", scatter_dimension=0, tiled=True),
        lax.psum_scatter(logit_grad, "ep", scatter_dimension=0, tiled=True),
        lax.psum_scatter(sgate_grad, "ep", scatter_dimension=0, tiled=True),
        lax.psum_scatter(sup_grad, "ep", scatter_dimension=0, tiled=True),
        lax.psum_scatter(sdown_grad, "ep", scatter_dimension=1, tiled=True),
    )
    return (
        block_out.astype(jnp.bfloat16),
        tokens_grad,
        summed[0],
        summed[1],
        summed[2],
        summed[3],
        summed[4],
        summed[5],
        summed[6],
        summed[7],
        summed[8],
        summed[9],
        egate_grad[None],
        expert_up_product_grad[None],
        down_grad[None],
        rms_values,
    )


def solution(mesh):
    in_specs = (
        P("ep", None),
        P("ep"),
        P("ep", "tp"),
        P("ep", "tp"),
        P("ep", "tp"),
        P("tp", "ep"),
        P("ep"),
        P("ep"),
        P("ep", "tp"),
        P("ep", "tp"),
        P("tp", "ep"),
        P("ep", None, "tp"),
        P("ep", None, "tp"),
        P("ep", "tp", None),
        P("ep", None),
        P("ep", None),
        P("ep"),
        P("ep"),
        P("ep", None),
    )
    out_specs = (
        P("ep", None),
        P("ep", None),
        P("ep"),
        P("ep", "tp"),
        P("ep", "tp"),
        P("ep", "tp"),
        P("tp", "ep"),
        P("ep"),
        P("ep"),
        P("ep", "tp"),
        P("ep", "tp"),
        P("tp", "ep"),
        P("ep", None, "tp"),
        P("ep", None, "tp"),
        P("ep", "tp", None),
        P("ep", None),
    )
    return jax.shard_map(
        on_device, mesh=mesh, in_specs=in_specs, out_specs=out_specs, check_vma=False
    )
```

profile of v0, /device:TPU:0, one launch (start us, length us, event | category | flops | bytes accessed | tf_op | source)
XLA Modules:
  0.0 2921.5 jit_solution(7038120062021359784)
XLA Ops:
  12.0 22.5 all-gather
  37.1 25.1 all-gather.13.cloned.1.call-done
  67.4 44.6 %all-gather.15.cloned.1.call-done = bf16[2048,512]{1,0:T(8,128)(2,1)} async-done(((bf16[256,512]{1,0:T(8,128)(2,1)}), bf16[2048,512]{1,0:T(8,128)(2,1)}) %all-gather.15.cloned.1.call-update) | async-done | bytes 2097168 | tf_op jit(solution)/shard_map/all_gather | solution.py:99
  121.4 40.3 %all-gather.11.cloned.1.call-done = bf16[2048,512]{1,0:T(8,128)(2,1)} async-done(((bf16[256,512]{1,0:T(8,128)(2,1)}), bf16[2048,512]{1,0:T(8,128)(2,1)}) %all-gather.11.cloned.1.call-update) | async-done | bytes 2097168 | tf_op jit(solution)/shard_map/all_gather | solution.py:100
  166.2 46.4 %all-gather.17.cloned.1.call-done = bf16[512,2048]{1,0:T(8,128)(2,1)} async-done(((bf16[512,256]{1,0:T(8,128)(2,1)}), bf16[512,2048]{1,0:T(8,128)(2,1)}) %all-gather.17.cloned.1.call-update) | async-done | bytes 2097168 | tf_op jit(solution)/shard_map/all_gather | solution.py:101
  219.9 17.9 all-gather.1
  241.0 42.6 %all-reduce.9.cloned.1.call-done = f32[384,2048]{1,0:T(8,128)} async-done(((f32[384,2048]{1,0:T(8,128)}), f32[384,2048]{1,0:T(8,128)}) %all-reduce.9.cloned.1.call-update) | async-done | bytes 3145744 | tf_op jit(solution)/shard_map/psum | solution.py:134
  294.4 9.7 reshape.334
  304.0 17.5 scatter_custom_fusion
  327.4 7.8 mul.303
  335.2 14.7 mul.304
  349.8 18.3 scatter_custom_fusion.1
  368.2 231.7 %all-to-all-done = bf16[8,384,2048]{2,1,0:T(8,128)(2,1)} async-done(((bf16[8,384,2048]{2,1,0:T(8,128)(2,1)}), bf16[8,384,2048]{2,1,0:T(8,128)(2,1)}, u32[]{:S(2)}, u32[]{:S(2)}) %all-to-all-start) | async-done | bytes 12582944 | tf_op jit(solution)/shard_map/all_to_all | solution.py:147
  605.7 11.8 fusion.21
  617.4 9.7 fusion.25
  627.1 250.4 %all-to-all-done.2 = bf16[8,384,2048]{2,1,0:T(8,128)(2,1)} async-done(((bf16[8,384,2048]{2,1,0:T(8,128)(2,1)}), bf16[8,384,2048]{2,1,0:T(8,128)(2,1)}, u32[]{:S(2)}, u32[]{:S(2)}) %all-to-all-start.2) | async-done | bytes 12582944 | tf_op jit(solution)/shard_map/all_to_all | solution.py:194
  877.5 17.0 multiply_convert_fusion.2
  894.6 9.8 convolution_convert_fusion
  911.2 13.8 fusion.23
  925.0 15.4 add_convert_fusion
  940.4 368.3 %all-to-all-done.1 = bf16[8,384,2048]{2,1,0:T(8,128)(2,1)} async-done(((bf16[8,384,2048]{2,1,0:T(8,128)(2,1)}), bf16[8,384,2048]{2,1,0:T(8,128)(2,1)}, u32[]{:S(2)}, u32[]{:S(2)}) %all-to-all-start.1) | async-done | bytes 12582944 | tf_op jit(solution)/shard_map/all_to_all | solution.py:154
  1315.0 239.7 %all-gather.2 = bf16[8,1,256]{2,1,0:T(2,128)(2,1)S(1)} all-gather(bf16[1,1,256]{2,1,0:T(2,128)(2,1)S(1)} %reshape.350), channel_id=1, replica_groups=mesh['ep'=8,'tp'=4] {'ep'}, dimensions={0}, use_global_device_ids=true | all-gather | bytes 4608 | tf_op jit(solution)/shard_map/all_gather | solution.py:103
  1555.2 6.8 fusion.63
  1562.0 6.6 fusion.62
  1568.6 99.9 %all-gather.23.cloned.1.call-done = bf16[1408,2048]{1,0:T(8,128)(2,1)} async-done(((bf16[1408,256]{1,0:T(8,128)(2,1)}), bf16[1408,2048]{1,0:T(8,128)(2,1)}) %all-gather.23.cloned.1.call-update) | async-done | bytes 5767184 | tf_op jit(solution)/shard_map/all_gather | solution.py:106
  1668.5 8.8 multiply_convert_fusion.8
  1681.7 19.3 gather_fusion
  1701.0 12.1 reshape.312
  1713.1 11.2 multiply_reduce_fusion
  1724.3 6.6 multiply_reduce_fusion.5
  1730.9 18.9 gather_fusion.1
  1749.8 12.0 reshape.313
  1761.8 12.0 reduce_sum.143
  1773.8 9.0 add_add_fusion.1
  1782.9 6.4 psum.38
  1789.3 74.4 %all-reduce.13.cloned.1.call-done = f32[384,2048]{1,0:T(8,128)} async-done(((f32[384,2048]{1,0:T(8,128)}), f32[384,2048]{1,0:T(8,128)}) %all-reduce.13.cloned.1.call-update) | async-done | bytes 3145744 | tf_op jit(solution)/shard_map/psum | solution.py:226
  1895.8 6.4 fusion.68
  1930.9 11.7 convolution_bitcast_fusion.2
  1942.6 9.6 convolution_bitcast_fusion
  1952.3 9.3 convolution_bitcast_fusion.1
  1967.2 39.5 %all-reduce.3 = (f32[2048]{0:T(1024)S(1)}, f32[2048]{0:T(1024)S(1)}, f32[2048]{0:T(1024)S(1)}) all-reduce(f32[2048]{0:T(1024)S(1)} %get-tuple-element.18, f32[2048]{0:T(1024)S(1)} %get-tuple-element.16, f32[2048]{0:T(1024)S(1)} %bitcast.177), channel_id=2, replica_groups=mesh['ep'=8,'tp'=4] {'ep'}, use_global_device_ids=true, to_apply=%region_21.22.clone | all-reduce | flops 6144 | bytes 49152
  2014.0 139.7 %reduce-scatter.18.cloned.1.call-done = f32[256,1408]{1,0:T(8,128)} async-done(((f32[2048,1408]{1,0:T(8,128)}), f32[256,1408]{1,0:T(8,128)}) %reduce-scatter.18.cloned.1.call-update) | async-done | bytes 1441808 | tf_op jit(solution)/shard_map/reduce_scatter | solution.py:270
  2153.7 196.1 %reduce-scatter.16.cloned.1.call-done = f32[256,1408]{1,0:T(8,128)} async-done(((f32[2048,1408]{1,0:T(8,128)}), f32[256,1408]{1,0:T(8,128)}) %reduce-scatter.16.cloned.1.call-update) | async-done | bytes 1441808 | tf_op jit(solution)/shard_map/reduce_scatter | solution.py:269
  2349.8 196.4 %reduce-scatter.20.cloned.1.call-done = f32[1408,256]{1,0:T(8,128)} async-done(((f32[1408,2048]{1,0:T(8,128)}), f32[1408,256]{1,0:T(8,128)}) %reduce-scatter.20.cloned.1.call-update) | async-done | bytes 1441808 | tf_op jit(solution)/shard_map/reduce_scatter | solution.py:271
  2546.2 91.9 %reduce-scatter.14.cloned.1.call-done = f32[512,256]{1,0:T(8,128)} async-done(((f32[512,2048]{1,0:T(8,128)}), f32[512,256]{1,0:T(8,128)}) %reduce-scatter.14.cloned.1.call-update) | async-done | bytes 524304 | tf_op jit(solution)/shard_map/reduce_scatter | solution.py:266
  2638.1 92.0 %reduce-scatter.12.cloned.1.call-done = f32[256,512]{1,0:T(8,128)} async-done(((f32[2048,512]{1,0:T(8,128)}), f32[256,512]{1,0:T(8,128)}) %reduce-scatter.12.cloned.1.call-update) | async-done | bytes 524304 | tf_op jit(solution)/shard_map/reduce_scatter | solution.py:265
  2730.1 92.0 %reduce-scatter.8.cloned.1.call-done = f32[256,512]{1,0:T(8,128)} async-done(((f32[2048,512]{1,0:T(8,128)}), f32[256,512]{1,0:T(8,128)}) %reduce-scatter.8.cloned.1.call-update) | async-done | bytes 524304 | tf_op jit(solution)/shard_map/reduce_scatter | solution.py:263
  2822.1 92.0 %reduce-scatter.10.cloned.1.call-done = f32[256,512]{1,0:T(8,128)} async-done(((f32[2048,512]{1,0:T(8,128)}), f32[256,512]{1,0:T(8,128)}) %reduce-scatter.10.cloned.1.call-update) | async-done | bytes 524304 | tf_op jit(solution)/shard_map/reduce_scatter | solution.py:264
  (246 shorter events, 148.9 us)
Async XLA Ops:
  7.2 870.4 %copy-start = (bf16[1,352,2048]{2,1,0:T(8,128)(2,1)S(1)}, bf16[1,352,2048]{2,1,0:T(8,128)(2,1)}, u32[]{:S(2)}) copy-start(bf16[1,352,2048]{2,1,0:T(8,128)(2,1)} %param.32) | copy-start | bytes 4325380
  7.2 55.0 %all-gather.13.cloned.1.call-start = ((), (), s32[]{:S(2)}) async-start(), calls=%async_computation.12 | async-start | bytes 2359296 | tf_op jit(solution)/shard_map/all_gather | solution.py:98
  7.9 104.0 %all-gather.15.cloned.1.call-start = ((), (), s32[]{:S(2)}) async-start(), calls=%async_computation.13 | async-start | bytes 2359296 | tf_op jit(solution)/shard_map/all_gather | solution.py:99
  8.7 153.1 %all-gather.11.cloned.1.call-start = ((), (), s32[]{:S(2)}) async-start(), calls=%async_computation.11 | async-start | bytes 2359296 | tf_op jit(solution)/shard_map/all_gather | solution.py:100
  9.4 203.1 %all-gather.17.cloned.1.call-start = ((), (), s32[]{:S(2)}) async-start(), calls=%async_computation.14 | async-start | bytes 2359296 | tf_op jit(solution)/shard_map/all_gather | solution.py:101
  10.0 273.6 %all-reduce.9.cloned.1.call-start = ((), (), s32[]{:S(2)}) async-start(), calls=%async_computation.15 | async-start | bytes 6291456 | tf_op jit(solution)/shard_map/psum | solution.py:134
  34.5 27.7 copy-start.38
  36.9 25.3 copy-start.46
  37.1 127.5 %copy-start.19 = (pred[384,384]{0,1:T(8,128)(4,1)}, pred[384,384]{0,1:T(8,128)(4,1)S(1)}, u32[]{:S(2)}) copy-start(pred[384,384]{0,1:T(8,128)(4,1)S(1)} %fusion.36) | copy-start | bytes 442372
  62.2 49.8 %copy-start.2 = (bf16[384,2048]{1,0:T(8,128)(2,1)S(1)}, bf16[384,2048]{1,0:T(8,128)(2,1)}, u32[]{:S(2)}) copy-start(bf16[384,2048]{1,0:T(8,128)(2,1)} %param.19) | copy-start | bytes 4718596
  67.4 49.9 %copy-start.21 = (bf16[384,512]{0,1:T(8,128)(2,1)}, bf16[384,512]{0,1:T(8,128)(2,1)S(1)}, u32[]{:S(2)}) copy-start(bf16[384,512]{0,1:T(8,128)(2,1)S(1)} %copy.86) | copy-start | bytes 1179652
  166.2 50.7 %copy-start.25 = (bf16[4,128,384]{2,1,0:T(8,128)(2,1)}, bf16[4,128,384]{2,1,0:T(8,128)(2,1)S(1)}, u32[]{:S(2)}) copy-start(bf16[4,128,384]{2,1,0:T(8,128)(2,1)S(1)} %convolution_convert_fusion.3) | copy-start | bytes 1179652
  237.8 50.2 %copy-start.48 = (f32[8,1,256]{2,1,0:T(1,128)}, f32[8,1,256]{2,1,0:T(1,128)S(1)}, u32[]{:S(2)}) copy-start(f32[8,1,256]{2,1,0:T(1,128)S(1)} %convert_element_type.172) | copy-start | bytes 24580
  289.3 1605.4 %copy-start.4 = (bf16[384,2048]{1,0:T(8,128)(2,1)}, bf16[384,2048]{1,0:T(8,128)(2,1)S(1)}, u32[]{:S(2)}) copy-start(bf16[384,2048]{1,0:T(8,128)(2,1)S(1)} %multiply_convert_fusion.6) | copy-start | bytes 4718596
  321.6 278.3 %all-to-all-start = ((bf16[8,384,2048]{2,1,0:T(8,128)(2,1)}), bf16[8,384,2048]{2,1,0:T(8,128)(2,1)}, u32[]{:S(2)}, u32[]{:S(2)}) async-start(bf16[8,384,2048]{2,1,0:T(8,128)(2,1)} %bitcast.148), calls=%async_computation | async-start | bytes 25165824 | tf_op jit(solution)/shard_map/all_to_all | solution.py:147
  327.2 7.9 copy-start.32
  599.9 277.6 %all-to-all-start.2 = ((bf16[8,384,2048]{2,1,0:T(8,128)(2,1)}), bf16[8,384,2048]{2,1,0:T(8,128)(2,1)}, u32[]{:S(2)}, u32[]{:S(2)}) async-start(bf16[8,384,2048]{2,1,0:T(8,128)(2,1)} %bitcast.149), calls=%async_computation.2 | async-start | bytes 25165824 | tf_op jit(solution)/shard_map/all_to_all | solution.py:194
  605.6 11.8 copy-start.36
  894.6 9.8 copy-start.62
  904.4 6.8 copy-start.37
  904.4 404.3 %all-to-all-start.1 = ((bf16[8,384,2048]{2,1,0:T(8,128)(2,1)}), bf16[8,384,2048]{2,1,0:T(8,128)(2,1)}, u32[]{:S(2)}, u32[]{:S(2)}) async-start(bf16[8,384,2048]{2,1,0:T(8,128)(2,1)} %bitcast.150), calls=%async_computation.1 | async-start | bytes 25165824 | tf_op jit(solution)/shard_map/all_to_all | solution.py:154
  909.9 645.4 %all-gather.21.cloned.1.call-start = ((), (), s32[]{:S(2)}) async-start(), calls=%async_computation.17 | async-start | bytes 6488064 | tf_op jit(solution)/shard_map/all_gather | solution.py:105
  910.4 651.6 %all-gather.19.cloned.1.call-start = ((), (), s32[]{:S(2)}) async-start(), calls=%async_computation.16 | async-start | bytes 6488064 | tf_op jit(solution)/shard_map/all_gather | solution.py:104
  1308.7 422.3 %all-to-all-start.3 = ((bf16[8,384,2048]{2,1,0:T(8,128)(2,1)}), bf16[8,384,2048]{2,1,0:T(8,128)(2,1)}, u32[]{:S(2)}, u32[]{:S(2)}) async-start(bf16[8,384,2048]{2,1,0:T(8,128)(2,1)} %bitcast.147), calls=%async_computation.3 | async-start | bytes 25165824 | tf_op jit(solution)/shard_map/all_to_all | solution.py:212
  1314.2 354.3 %all-gather.23.cloned.1.call-start = ((), (), s32[]{:S(2)}) async-start(), calls=%async_computation.18 | async-start | bytes 6488064 | tf_op jit(solution)/shard_map/all_gather | solution.py:106
  1314.9 474.4 %all-reduce.11.cloned.1.call-start = ((), (), s32[]{:S(2)}) async-start(), calls=%async_computation.19 | async-start | bytes 3145728 | tf_op jit(solution)/shard_map/psum | solution.py:159
  1668.5 8.8 copy-start.58
  1677.3 47.0 %copy-start.30 = (bf16[384,1408]{1,0:T(8,128)(2,1)}, bf16[384,1408]{1,0:T(8,128)(2,1)S(1)}, u32[]{:S(2)}) copy-start(bf16[384,1408]{1,0:T(8,128)(2,1)S(1)} %get-tuple-element.32) | copy-start | bytes 3244036
  1701.0 12.1 copy-start.33
  1713.1 11.2 copy-start.12
  1730.9 132.8 %all-reduce.13.cloned.1.call-start = ((), (), s32[]{:S(2)}) async-start(), calls=%async_computation.20 | async-start | bytes 6291456 | tf_op jit(solution)/shard_map/psum | solution.py:226
  1761.8 12.0 copy-start.42
  1782.7 80.9 %copy-start.49 = (f32[8,1,256]{2,1,0:T(1,128)S(1)}, f32[8,1,256]{2,1,0:T(1,128)}, u32[]{:S(2)}) copy-start(f32[8,1,256]{2,1,0:T(1,128)} %copy-done.48) | copy-start | bytes 24580
  1782.7 81.0 %copy-start.53 = (f32[384]{0:T(512)S(1)}, f32[384]{0:T(512)}, u32[]{:S(2)}) copy-start(f32[384]{0:T(512)} %copy-done.52) | copy-start | bytes 4612
  1782.8 181.7 %all-reduce.15.cloned.1.call-start = ((), (), s32[]{:S(2)}) async-start(), calls=%async_computation.21 | async-start | bytes 6291456 | tf_op jit(solution)/shard_map/psum | solution.py:258
  1789.3 80.2 %copy-start.56 = (f32[384]{0:T(512)S(1)}, f32[384]{0:T(512)}, u32[]{:S(2)}) copy-start(f32[384]{0:T(512)} %get-tuple-element.39) | copy-start | bytes 4612
  1887.2 266.5 %reduce-scatter.18.cloned.1.call-start = ((), (), s32[]{:S(2)}) async-start(), calls=%async_computation.27 | async-start | bytes 12976128 | tf_op jit(solution)/shard_map/reduce_scatter | solution.py:270
  1894.6 455.2 %reduce-scatter.16.cloned.1.call-start = ((), (), s32[]{:S(2)}) async-start(), calls=%async_computation.26 | async-start | bytes 12976128 | tf_op jit(solution)/shard_map/reduce_scatter | solution.py:269
  1902.2 644.0 %reduce-scatter.20.cloned.1.call-start = ((), (), s32[]{:S(2)}) async-start(), calls=%async_computation.28 | async-start | bytes 12976128 | tf_op jit(solution)/shard_map/reduce_scatter | solution.py:271
  1910.1 728.0 %reduce-scatter.14.cloned.1.call-start = ((), (), s32[]{:S(2)}) async-start(), calls=%async_computation.25 | async-start | bytes 4718592 | tf_op jit(solution)/shard_map/reduce_scatter | solution.py:266
  1916.2 813.9 %reduce-scatter.12.cloned.1.call-start = ((), (), s32[]{:S(2)}) async-start(), calls=%async_computation.24 | async-start | bytes 4718592 | tf_op jit(solution)/shard_map/reduce_scatter | solution.py:265
  1921.1 901.0 %reduce-scatter.8.cloned.1.call-start = ((), (), s32[]{:S(2)}) async-start(), calls=%async_computation.22 | async-start | bytes 4718592 | tf_op jit(solution)/shard_map/reduce_scatter | solution.py:263
  1925.6 988.6 %reduce-scatter.10.cloned.1.call-start = ((), (), s32[]{:S(2)}) async-start(), calls=%async_computation.23 | async-start | bytes 4718592 | tf_op jit(solution)/shard_map/reduce_scatter | solution.py:264
  1930.9 11.7 copy-start.18
  1942.6 9.7 copy-start.24
  1952.3 9.3 copy-start.5
  1961.6 47.0 %copy-start.55 = (f32[384]{0:T(512)S(1)}, f32[384]{0:T(512)}, u32[]{:S(2)}) copy-start(f32[384]{0:T(512)} %get-tuple-element.37) | copy-start | bytes 4612
  2008.6 905.6 %copy-start.1 = (bf16[1,352,2048]{2,1,0:T(8,128)(2,1)S(1)}, bf16[1,352,2048]{2,1,0:T(8,128)(2,1)}, u32[]{:S(2)}) copy-start(bf16[1,352,2048]{2,1,0:T(8,128)(2,1)} %param.32) | copy-start | bytes 4325380
  (37 other events, 96.0 us)
Sparse Core Ops, SparseCore 0:
  10.1 52.0 all-gather.12
  64.3 47.6 all-gather.14
  114.1 47.6 all-gather.10
  163.7 48.8 all-gather.16
  217.0 66.5 all-reduce.8
  912.5 296.3 all-gather.20
  1211.1 117.2 all-gather.18
  1330.4 338.0 all-gather.22
  1731.0 55.2 all-reduce.10
  1788.5 75.1 all-reduce.12
  1887.3 68.5 all-reduce.14
  1959.9 193.7 reduce-scatter.17
  2157.9 191.9 reduce-scatter.15
  2353.9 192.3 reduce-scatter.19
  2550.3 87.7 reduce-scatter.13
  2642.2 87.9 reduce-scatter.11
  2734.2 87.9 reduce-scatter.7
  2826.2 87.9 reduce-scatter.9
where the time goes:
time: 2930 us; the launch traced here: 2920 us
  waiting for transfers between devices  2130 us (73%)
  blocking collectives  326 us (11%)
  matrix products  212 us (7%)
  local copies, waits for them, and re-layouts  142 us (5%)
  other arithmetic  72.4 us (2%)
    all_to_all x1, waiting for transfers between devices, on_device(): lax.all_to_all(epart.reshape(groups, capacity, width), 'ep', split_axis=0...  368 us
    all_to_all x1, waiting for transfers between devices, on_device(): lax.all_to_all(grad_send, 'ep', split_axis=0, concat_axis=0, tiled=True)  250 us
    all_gather x1, blocking collectives, on_device(): lax.all_gather(shared_logit, 'ep', axis=0, tiled=True)  240 us
    all_to_all x1, waiting for transfers between devices, on_device(): lax.all_to_all(send, 'ep', split_axis=0, concat_axis=0, tiled=True)  232 us
    reduce_scatter x1, waiting for transfers between devices, on_device(): lax.psum_scatter(sdown_grad, 'ep', scatter_dimension=1, tiled=True)  196 us
    reduce_scatter x1, waiting for transfers between devices, on_device(): lax.psum_scatter(sgate_grad, 'ep', scatter_dimension=0, tiled=True)  196 us
    reduce_scatter x1, waiting for transfers between devices, on_device(): lax.psum_scatter(sup_grad, 'ep', scatter_dimension=0, tiled=True)  140 us
    all_gather x1, waiting for transfers between devices, on_device(): lax.all_gather(shared_down, 'ep', axis=1, tiled=True)  99.9 us
  transfers between devices with their start and end apart: 22, of which 17 were waited for; matrix products, arithmetic and copies ran while one was open for 11% of the time, Pallas kernels for 0%

commit v1 on v0

v1 whole, which is shorter than its diff:
```python
import jax
import jax.numpy as jnp
from jax import lax
from jax.sharding import PartitionSpec as P

HD = 128
EPS = 1e-06
BF = jnp.bfloat16
F32 = jnp.float32


def nn(left, right):
    return lax.dot_general(left, right, (((1,), (0,)), ((), ())), preferred_element_type=F32)


def nt(left, right):
    return lax.dot_general(left, right, (((1,), (1,)), ((), ())), preferred_element_type=F32)


def tn(left, right):
    return lax.dot_general(left, right, (((0,), (0,)), ((), ())), preferred_element_type=F32)


def at(array, index):
    return lax.dynamic_index_in_dim(array, index, 0, keepdims=False)


def put(array, value, index):
    return lax.dynamic_update_index_in_dim(array, value, index, 0)


def swap_inner(value):
    size = lax.axis_size("ep")
    return lax.ppermute(value, "ep", [(i, i ^ 1) for i in range(size)])


def ring_outer(value):
    size = lax.axis_size("ep")
    return lax.ppermute(value, "ep", [(i, (i + 2) % size) for i in range(size)])


def swap_tp(value, mask):
    size = lax.axis_size("tp")
    return lax.ppermute(value, "tp", [(i, i ^ mask) for i in range(size)])


def gather_ep(shard):
    size = lax.axis_size("ep")
    rounds = size // 2
    me = lax.axis_index("ep")
    outer, inner = me // 2, me % 2
    whole = jnp.zeros((size,) + shard.shape, shard.dtype)
    current = shard
    for k in range(rounds):
        where = (outer + rounds - k) % rounds * 2
        other = swap_inner(current)
        whole = put(whole, current, where + inner)
        following = ring_outer(current) if k < rounds - 1 else None
        whole = put(whole, other, where + 1 - inner)
        current = following
    return whole


def scatter_ep(parts, sent=BF):
    size = lax.axis_size("ep")
    rounds = size // 2
    me = lax.axis_index("ep")
    outer, inner = me // 2, me % 2
    arrived = None
    for k in list(range(1, rounds)) + [0]:
        where = (outer + rounds - k) % rounds * 2
        other = swap_inner(at(parts, where + 1 - inner).astype(sent))
        total = at(parts, where + inner).astype(F32) + other.astype(F32)
        if arrived is not None:
            total = total + arrived.astype(F32)
        if k:
            arrived = ring_outer(total.astype(sent))
    return total


def gather_tp(shard):
    me = lax.axis_index("tp")
    whole = jnp.zeros((lax.axis_size("tp"),) + shard.shape, shard.dtype)
    far = swap_tp(shard, 2)
    whole = put(whole, shard, me)
    whole = put(whole, swap_tp(shard, 1), me ^ 1)
    whole = put(whole, far, me ^ 2)
    return put(whole, swap_tp(far, 1), me ^ 3)


def scatter_tp(parts, sent=BF):
    me = lax.axis_index("tp")
    near_far = swap_tp(at(parts, me ^ 3).astype(sent), 1)
    far = at(parts, me ^ 2).astype(F32) + near_far.astype(F32)
    far = swap_tp(far.astype(sent), 2)
    near = swap_tp(at(parts, me ^ 1).astype(sent), 1)
    return at(parts, me).astype(F32) + near.astype(F32) + far.astype(F32)


def sum_tp(value):
    value = value + swap_tp(value, 1)
    return value + swap_tp(value, 2)


def rms_scale(values):
    return lax.rsqrt(jnp.mean(values * values, axis=-1, keepdims=True) + EPS)


def norm_back(grad, values, scale, gain):
    weighted = grad * gain
    inner = jnp.mean(values * weighted, axis=-1, keepdims=True)
    return (scale * weighted - values * scale**3 * inner, jnp.sum(grad * values * scale, axis=0))


def gated_back(grad_hidden, gate_val, up_val):
    squash = jax.nn.sigmoid(gate_val)
    grad_gate = grad_hidden * up_val * squash * (1.0 + gate_val * (1.0 - squash))
    grad_up = grad_hidden * gate_val * squash
    return (grad_gate.astype(BF), grad_up.astype(BF))


def expert_step(act, gout, gates, logit32, routed, shared):
    r_gate, r_up, r_down = routed
    s_gate, s_up, s_down = shared
    score = jax.nn.sigmoid(jnp.sum(act.astype(F32) * logit32, axis=1, keepdims=True))
    r_gate_val, r_up_val = nt(act, r_gate), nt(act, r_up)
    s_gate_val, s_up_val = nt(act, s_gate), nt(act, s_up)
    r_hidden = (jax.nn.silu(r_gate_val) * r_up_val * gates).astype(BF)
    s_plain = jax.nn.silu(s_gate_val) * s_up_val
    s_hidden = (s_plain * score).astype(BF)
    out = (nn(r_hidden, r_down) + nn(s_hidden, s_down)).astype(BF)
    r_back = nt(gout, r_down)
    s_back = nt(gout, s_down)
    r_dgate, r_dup = gated_back(r_back * gates, r_gate_val, r_up_val)
    s_dgate, s_dup = gated_back(s_back * score, s_gate_val, s_up_val)
    gscore = score * (1.0 - score) * jnp.sum(s_plain * s_back, axis=1, keepdims=True)
    gact = nn(r_dgate, r_gate) + nn(r_dup, r_up) + nn(s_dgate, s_gate) + nn(s_dup, s_up)
    gact = (gact + gscore * logit32).astype(BF)
    logit_part = jnp.sum(act.astype(F32) * gscore, axis=0)
    pairs = (
        (r_dgate, act),
        (r_dup, act),
        (r_hidden, gout),
        (s_dgate, act),
        (s_dup, act),
        (s_hidden, gout),
    )
    return out, gact, (logit_part,) + tuple(tn(left, right) for left, right in pairs)


def experts(act, gout, gates, logit32, routed, shared, most=1024):
    rows, width = act.shape
    steps = -(-rows // most)
    if steps == 1:
        out, gact, sums = expert_step(act, gout, gates, logit32, routed, shared)
        return out, gact, sums[0], sums[1:]

    def step(totals, block):
        out, gact, sums = expert_step(*block, logit32, routed, shared)
        return tuple(t + s for t, s in zip(totals, sums)), (out, gact)

    blocks = tuple(x.reshape(steps, rows // steps, -1) for x in (act, gout, gates))
    sizes = [(width,)] + [w.shape for w in routed + shared]
    totals = tuple(jnp.zeros(size, F32) for size in sizes)
    sums, (out, gact) = lax.scan(step, totals, blocks)
    return out.reshape(rows, width), gact.reshape(rows, width), sums[0], sums[1:]


def columns(array, head):
    return array[:, head * HD : (head + 1) * HD]


def on_device(
    tokens,
    first_gain,
    query_weight,
    key_weight,
    value_weight,
    output_weight,
    second_gain,
    shared_logit,
    shared_gate,
    shared_up,
    shared_down,
    routed_gate_weight,
    routed_up_weight,
    expert_down,
    route_ids,
    route_gates,
    piece_start,
    piece_length,
    block_grad,
):
    groups = lax.axis_size("ep")
    quarters = lax.axis_size("tp")
    me_ep = lax.axis_index("ep")
    me_tp = lax.axis_index("tp")
    count, width = tokens.shape
    part = count // quarters
    local_heads = query_weight.shape[1] // HD
    wide = local_heads * HD
    factor = HD ** (-0.5)

    def own(array):
        return lax.dynamic_slice_in_dim(array, me_tp * part, part, 0)

    vectors = jnp.stack([first_gain, second_gain, shared_logit])
    vectors = gather_ep(jnp.pad(vectors, ((0, 5), (0, 0))))
    vectors = vectors.transpose(1, 0, 2).reshape(8, width)
    gain_one32 = vectors[0:1].astype(F32)
    gain_two32 = vectors[1:2].astype(F32)
    logit32 = vectors[2:3].astype(F32)
    w_qkv = gather_ep(jnp.concatenate([query_weight, key_weight, value_weight], axis=1))
    w_qkv = w_qkv.reshape(width, 3 * wide)
    w_out = gather_ep(output_weight.T).reshape(width, wide)

    def units_first(array):
        return gather_tp(array).reshape(-1, width)

    r_gate = units_first(routed_gate_weight[0].T)
    r_up = units_first(routed_up_weight[0].T)
    r_down = units_first(expert_down[0])

    units = shared_down.shape[0]
    piece = units // groups
    shared = jnp.stack([shared_gate.T, shared_up.T, shared_down]).reshape(3, groups, piece, -1)
    shared = lax.all_to_all(shared, "ep", split_axis=1, concat_axis=1, tiled=True)
    shared = shared.transpose(0, 2, 1, 3).reshape(3, piece, width)
    shared = gather_tp(shared)
    shared = shared.transpose(1, 0, 2, 3).reshape(3, quarters * piece, width)
    s_gate, s_up, s_down = shared[0], shared[1], shared[2]

    inputs32 = tokens.astype(F32)
    scale_one = rms_scale(inputs32)
    act1 = (inputs32 * scale_one * gain_one32).astype(BF)
    qkv = nn(act1, w_qkv).astype(BF)
    query, key, value = qkv[:, :wide], qkv[:, wide : 2 * wide], qkv[:, 2 * wide :]
    positions = jnp.arange(count, dtype=jnp.int32)
    start = piece_start[0]
    inside = (positions >= start) & (positions < start + piece_length[0])
    visible = (positions[None, :] <= positions[:, None]) | inside[:, None] & inside[None, :]
    all_lse, mixes = [], []
    for h in range(local_heads):
        scores = jnp.where(visible, nt(columns(query, h), columns(key, h)) * factor, -1e30)
        highest = jnp.max(scores, axis=-1, keepdims=True)
        lse = highest + jnp.log(jnp.sum(jnp.exp(scores - highest), axis=-1, keepdims=True))
        probs = jnp.exp(scores - lse).astype(BF)
        all_lse.append(lse)
        mixes.append(nn(probs, columns(value, h)).astype(BF))
    attn_mix = jnp.concatenate(mixes, axis=1)
    branch = nt(attn_mix, w_out).reshape(quarters, part, width)
    attn_branch = scatter_tp(branch, F32)

    inputs_own = own(tokens).astype(F32)
    resid = inputs_own + attn_branch
    scale_two = rms_scale(resid)
    act2 = (resid * scale_two * gain_two32).astype(BF)

    dense = jnp.sum(
        own(route_gates)[:, :, None]
        * (own(route_ids)[:, :, None] == jnp.arange(groups, dtype=jnp.int32)).astype(F32),
        axis=1,
    )
    gates = gather_ep(dense).reshape(groups * part, groups)
    gates = jnp.sum(
        jnp.where(jnp.arange(groups)[None, :] == me_ep, gates, 0.0), axis=1, keepdims=True
    )
    gout_all = gather_ep(own(block_grad)).reshape(groups * part, width)
    act_all = gather_ep(act2).reshape(groups * part, width)

    ffn_part, gact_part, logit_part, sums = experts(
        act_all, gout_all, gates, logit32, (r_gate, r_up, r_down), (s_gate, s_up, s_down)
    )
    ffn_branch = scatter_ep(ffn_part.reshape(groups, part, width))
    block_sum = resid + ffn_branch
    block_out = gather_tp(block_sum.astype(BF)).reshape(count, width)
    squares = jnp.stack(
        [
            jnp.sum(attn_branch * attn_branch),
            jnp.sum(ffn_branch * ffn_branch),
            jnp.sum(block_sum * block_sum),
        ]
    )
    rms_values = jnp.sqrt(sum_tp(squares) / (count * width))[None, :]

    gact2 = scatter_ep(gact_part.reshape(groups, part, width))
    sums = [scatter_tp(total.astype(BF).reshape(quarters, -1, width)) for total in sums]
    gate_grad, up_grad, down_grad = sums[0].T, sums[1].T, sums[2]
    shared_grads = jnp.stack(sums[3:])
    shared_grads = shared_grads.astype(BF).reshape(3, piece, groups, -1).transpose(0, 2, 1, 3)
    shared_grads = lax.all_to_all(shared_grads, "ep", split_axis=1, concat_axis=1, tiled=True)
    shared_grads = shared_grads.reshape(3, units, -1)
    sgate_grad = shared_grads[0].T.astype(F32)
    sup_grad = shared_grads[1].T.astype(F32)
    sdown_grad = shared_grads[2].astype(F32)

    resid_part, gain_two_part = norm_back(gact2, resid, scale_two, gain_two32)
    gresid = own(block_grad).astype(F32) + resid_part
    gattn = gather_tp(gresid.astype(BF)).reshape(count, width)
    output_grad = scatter_ep(tn(gattn, attn_mix).astype(BF).reshape(groups, -1, wide)).T
    gmix = nn(gattn, w_out).astype(BF)
    gqs, gks, gvs = [], [], []
    for h in range(local_heads):
        query_h, key_h, gmix_h = columns(query, h), columns(key, h), columns(gmix, h)
        scores = jnp.where(visible, nt(query_h, key_h) * factor, -1e30)
        probs = jnp.exp(scores - all_lse[h])
        gprob = nt(gmix_h, columns(value, h))
        gvs.append(tn(probs.astype(BF), gmix_h).astype(BF))
        inner = jnp.sum(probs * gprob, axis=-1, keepdims=True)
        gscores = (probs * (gprob - inner)).astype(BF)
        gqs.append((nn(gscores, key_h) * factor).astype(BF))
        gks.append((tn(gscores, query_h) * factor).astype(BF))
    gqkv = jnp.concatenate(gqs + gks + gvs, axis=1)
    qkv_grad = scatter_ep(tn(act1, gqkv).astype(BF).reshape(groups, -1, 3 * wide))
    gact1 = scatter_tp(nt(gqkv, w_qkv).astype(BF).reshape(quarters, part, width))
    input_part, gain_one_part = norm_back(gact1, inputs_own, own(scale_one), gain_one32)
    tokens_grad = gather_tp((gresid + input_part).astype(BF)).reshape(count, width).astype(F32)

    def summed(vector_parts):
        stacked = jnp.stack(vector_parts).reshape(len(vector_parts), groups, -1)
        return sum_tp(scatter_ep(stacked.transpose(1, 0, 2), F32))

    early = summed([gain_two_part, logit_part])
    late = summed([gain_one_part])
    return (
        block_out,
        tokens_grad,
        late[0],
        qkv_grad[:, :wide],
        qkv_grad[:, wide : 2 * wide],
        qkv_grad[:, 2 * wide :],
        output_grad,
        early[0],
        early[1],
        sgate_grad,
        sup_grad,
        sdown_grad,
        gate_grad[None],
        up_grad[None],
        down_grad[None],
        rms_values,
    )


def solution(mesh):
    in_specs = (
        P("ep", None),
        P("ep"),
        P("ep", "tp"),
        P("ep", "tp"),
        P("ep", "tp"),
        P("tp", "ep"),
        P("ep"),
        P("ep"),
        P("ep", "tp"),
        P("ep", "tp"),
        P("tp", "ep"),
        P("ep", None, "tp"),
        P("ep", None, "tp"),
        P("ep", "tp", None),
        P("ep", None),
        P("ep", None),
        P("ep"),
        P("ep"),
        P("ep", None),
    )
    out_specs = (
        P("ep", None),
        P("ep", None),
        P("ep"),
        P("ep", "tp"),
        P("ep", "tp"),
        P("ep", "tp"),
        P("tp", "ep"),
        P("ep"),
        P("ep"),
        P("ep", "tp"),
        P("ep", "tp"),
        P("tp", "ep"),
        P("ep", None, "tp"),
        P("ep", None, "tp"),
        P("ep", "tp", None),
        P("ep", None),
    )
    return jax.shard_map(
        on_device, mesh=mesh, in_specs=in_specs, out_specs=out_specs, check_vma=False
    )
```

time: 2930 us -> 924 us (0.32)
  waiting for transfers between devices: 2130 us -> 400 us
  blocking collectives: 326 us -> 0 us
  starting transfers between devices: 23 us -> 127 us
  matrix products: 212 us -> 149 us
    reduce_scatter x7 -> x0, waiting for transfers between devices: 900 us -> none  [the longest x1 196 us: on_device(): lax.psum_scatter(sdown_grad, 'ep', scatter_dimension=1, tiled=True)]
    all_to_all x4 -> x2, waiting for transfers between devices: 850 us -> 0.01 us  [the longest x1 0.01 us: on_device(): lax.all_to_all(shared, 'ep', split_axis=1, concat_axis=1, tiled=True)]
    ppermute x0 -> x135, waiting for transfers between devices: none -> 400 us  [the longest x36 156 us: ring_outer(): return lax.ppermute(value, 'ep', [(i, (i + 2) % size) for i in range(size)])]
    all_gather x3 -> x0, blocking collectives: 280 us -> none  [the longest x1 240 us: on_device(): lax.all_gather(shared_logit, 'ep', axis=0, tiled=True)]
    all_gather x7 -> x0, waiting for transfers between devices: 256 us -> none  [the longest x1 99.9 us: on_device(): lax.all_gather(shared_down, 'ep', axis=1, tiled=True)]
    ppermute x0 -> x135, starting transfers between devices: none -> 118 us  [the longest x48 60.2 us: swap_inner(): return lax.ppermute(value, 'ep', [(i, i ^ 1) for i in range(size)])]
    psum x4 -> x0, waiting for transfers between devices: 117 us -> none  [the longest x1 74.4 us: on_device(): gact2_sum, score_sum = lax.psum((gact2_part, score_part), 'tp')]
    dynamic_update_slice x0 -> x72, local copies, waits for them, and re-layouts: none -> 68.7 us  [put(): return lax.dynamic_update_index_in_dim(array, value, index, 0)]
  transfers between devices with their start and end apart: 22 -> 137, of which waited for: 17 -> 60; matrix products, arithmetic and copies ran while one was open for 11% -> 40% of each run, Pallas kernels for 0% -> 0%
where the time goes in v1:
time: 924 us; the launch traced here: 914 us
  waiting for transfers between devices  400 us (43%)
  local copies, waits for them, and re-layouts  156 us (17%)
  matrix products  149 us (16%)
  starting transfers between devices  127 us (14%)
  other arithmetic  76.7 us (8%)
    ppermute x36, waiting for transfers between devices, ring_outer(): return lax.ppermute(value, 'ep', [(i, (i + 2) % size) for i in range(size)])  156 us
    ppermute x48, waiting for transfers between devices, swap_inner(): return lax.ppermute(value, 'ep', [(i, i ^ 1) for i in range(size)])  136 us
    ppermute x51, waiting for transfers between devices, swap_tp(): return lax.ppermute(value, 'tp', [(i, i ^ mask) for i in range(size)])  108 us
    dynamic_update_slice x72, local copies, waits for them, and re-layouts, put(): return lax.dynamic_update_index_in_dim(array, value, index, 0)  68.7 us
    ppermute x48, starting transfers between devices, swap_inner(): return lax.ppermute(value, 'ep', [(i, i ^ 1) for i in range(size)])  60.2 us
    dot_general x16, matrix products, nt(): lax.dot_general(left, right, (((1,), (1,)), ((), ())), preferred_element_...  56.2 us
    dot_general x16, matrix products, nn(): lax.dot_general(left, right, (((1,), (0,)), ((), ())), preferred_element_...  51.6 us
    dot_general x16, matrix products, tn(): lax.dot_general(left, right, (((0,), (0,)), ((), ())), preferred_element_...  41.3 us
  transfers between devices with their start and end apart: 137, of which 60 were waited for; matrix products, arithmetic and copies ran while one was open for 40% of the time, Pallas kernels for 0%

profile of v1, /device:TPU:0, one launch (start us, length us, event | category | flops | bytes accessed | tf_op | source)
XLA Modules:
  0.0 913.6 jit_solution(782583524305384355)
XLA Ops:
  49.4 17.0 %collective-permute-done.38 = f32[96,8]{0,1:T(8,128)S(1)} collective-permute-done((f32[96,8]{0,1:T(8,128)S(1)}, f32[96,8]{0,1:T(8,128)S(1)}, u32[]{:S(2)}, u32[]{:S(2)}) %collective-permute-start.38) | collective-permute-done | bytes 3104 | tf_op jit(solution)/shard_map/ppermute | solution.py:39
  69.9 10.3 %collective-permute-start.1 = (bf16[8,256]{1,0:T(8,128)(2,1)S(1)}, bf16[8,256]{1,0:T(8,128)(2,1)S(1)}, u32[]{:S(2)}, u32[]{:S(2)}) collective-permute-start(bf16[8,256]{1,0:T(8,128)(2,1)S(1)} %fusion.142), channel_id=1, source_target_pairs={{0,8},{4,12},{8,16},{12,20},{16,24},{20,28},{24,0},{28,4},{1,9},{5... | collective-permute-start | bytes 12296 | tf_op jit(solution)/shard_map/ppermute | solution.py:39
  94.8 4.8 collective-permute-done.3
  103.2 5.4 collective-permute-done.42
  112.3 5.4 collective-permute-done.5
  139.8 9.0 collective-permute-done.17
  148.9 6.3 collective-permute-done.18
  164.7 6.7 collective-permute-done.62
  190.0 10.5 %collective-permute-done.65 = bf16[96,2048]{1,0:T(8,128)(2,1)} collective-permute-done((bf16[96,2048]{1,0:T(8,128)(2,1)}, bf16[96,2048]{1,0:T(8,128)(2,1)}, u32[]{:S(2)}, u32[]{:S(2)}) %collective-permute-start.65) | collective-permute-done | bytes 393248 | tf_op jit(solution)/shard_map/ppermute | solution.py:39
  221.7 22.6 %collective-permute-done.32 = bf16[352,2048]{1,0:T(8,128)(2,1)} collective-permute-done((bf16[352,2048]{1,0:T(8,128)(2,1)S(1)}, bf16[352,2048]{1,0:T(8,128)(2,1)}, u32[]{:S(2)}, u32[]{:S(2)}) %collective-permute-start.32) | collective-permute-done | bytes 1441824 | tf_op jit(solution)/shard_map/ppermute | solution.py:44
  250.3 16.7 %collective-permute-done.11 = bf16[256,1536]{1,0:T(8,128)(2,1)S(1)} collective-permute-done((bf16[256,1536]{1,0:T(8,128)(2,1)S(1)}, bf16[256,1536]{1,0:T(8,128)(2,1)S(1)}, u32[]{:S(2)}, u32[]{:S(2)}) %collective-permute-start.11) | collective-permute-done | bytes 786464 | tf_op jit(solution)/shard_map/ppermute | solution.py:34
  272.6 16.2 %collective-permute-done.13 = bf16[256,1536]{1,0:T(8,128)(2,1)S(1)} collective-permute-done((bf16[256,1536]{1,0:T(8,128)(2,1)S(1)}, bf16[256,1536]{1,0:T(8,128)(2,1)S(1)}, u32[]{:S(2)}, u32[]{:S(2)}) %collective-permute-start.13) | collective-permute-done | bytes 786464 | tf_op jit(solution)/shard_map/ppermute | solution.py:34
  289.7 5.5 convolution_convert_fusion.9
  307.3 9.8 %fusion.178 = f32[768,1408]{1,0:T(8,128)} fusion(bf16[768,2048]{1,0:T(8,128)(2,1)} %bitcast.112, bf16[1408,2048]{1,0:T(8,128)(2,1)} %bitcast.581), kind=kOutput, calls=%fused_computation.449 | convolution fusion | flops 4429185024 | bytes 13238272 | tf_op jit(solution)/shard_map/dot_general | solution.py:17
  319.8 5.6 collective-permute-done.23
  350.1 12.0 %collective-permute-done.27 = bf16[96,2048]{1,0:T(8,128)(2,1)S(1)} collective-permute-done((bf16[96,2048]{1,0:T(8,128)(2,1)S(1)}, bf16[96,2048]{1,0:T(8,128)(2,1)S(1)}, u32[]{:S(2)}, u32[]{:S(2)}) %collective-permute-start.27) | collective-permute-done | bytes 393248 | tf_op jit(solution)/shard_map/ppermute | solution.py:39
  363.0 11.8 %collective-permute-done.29 = bf16[96,2048]{1,0:T(8,128)(2,1)S(1)} collective-permute-done((bf16[96,2048]{1,0:T(8,128)(2,1)S(1)}, bf16[96,2048]{1,0:T(8,128)(2,1)S(1)}, u32[]{:S(2)}, u32[]{:S(2)}) %collective-permute-start.29) | collective-permute-done | bytes 393248 | tf_op jit(solution)/shard_map/ppermute | solution.py:39
  376.1 9.9 %collective-permute-done.48 = bf16[3,176,2048]{2,1,0:T(8,128)(2,1)} collective-permute-done((bf16[3,176,2048]{2,1,0:T(8,128)(2,1)}, bf16[3,176,2048]{2,1,0:T(8,128)(2,1)}, u32[]{:S(2)}, u32[]{:S(2)}) %collective-permute-start.48) | collective-permute-done | bytes 2162720 | tf_op jit(solution)/shard_map/ppermute | solution.py:44
  389.9 7.3 fusion.175
  397.2 11.0 %multiply_convert_fusion.1 = (bf16[768,1408]{1,0:T(8,128)(2,1)S(1)}, bf16[768,1408]{1,0:T(8,128)(2,1)S(1)}, bf16[768,1408]{1,0:T(8,128)(2,1)S(1)}) fusion(f32[768,1408]{1,0:T(8,128)} %fusion.175, f32[768,1408]{1,0:T(8,128)} %fusion.178, f32[768]{0:T(1024)S(1)} %copy-done.88, bf16[768,2048]{1,0:T(8,128)(2,1)S(1)} %bitcast.550, bf16[1408,2048]{1,0:T(8,128)(2,1)} %bitcast.54), kind=kOutput, calls=%fused_computation.11 | convolution fusion | flops 4448649216 | bytes 24054784 | tf_op jit(solution)/shard_map/dot_general | solution.py:17
  408.2 7.0 fusion.179
  415.2 5.0 convolution_convert_fusion.1
  420.2 9.3 %convolution_convert_fusion = bf16[1408,2048]{1,0:T(8,128)(2,1)S(1)} fusion(bf16[768,1408]{1,0:T(8,128)(2,1)S(1)} %get-tuple-element.122, bf16[768,2048]{1,0:T(8,128)(2,1)} %bitcast.112), kind=kOutput, calls=%fused_computation.2 | convolution fusion | flops 4432068608 | bytes 11075584 | tf_op jit(solution)/shard_map/dot_general | solution.py:21
  435.3 5.1 convolution_convert_fusion.2
  469.3 5.3 multiply_reduce_fusion
  488.0 5.0 fusion.181
  496.9 6.0 convolution_convert_fusion.4
  503.0 11.7 %add_convert_fusion = bf16[768,2048]{1,0:T(8,128)(2,1)S(1)} fusion(f32[768,2048]{1,0:T(8,128)} %fusion.181, f32[768,2048]{1,0:T(8,128)} %fusion.180, f32[768,2048]{1,0:T(8,128)} %fusion.179, bf16[768,1408]{1,0:T(8,128)(2,1)} %copy-done.100, bf16[1408,2048]{1,0:T(8,128)(2,1)} %bitcast.54, f32[2048]{0:T(1024)S(1)} %bitcast.646, f32[768]{0:T(1024)S(1)} %fusion.139), kind=kOutput, calls=%fused_computation.8 | convolution fusion | flops 4438622208 | bytes 29961216 | tf_op jit(solution)/shard_map/dot_general | solution.py:13
  517.9 9.0 add_convert_fusion.1
  544.1 8.6 collective-permute-done.69
  557.8 5.2 collective-permute-done.52
  563.0 6.1 collective-permute-done.54
  583.0 25.1 %collective-permute-done.126 = bf16[352,2048]{1,0:T(8,128)(2,1)S(1)} collective-permute-done((bf16[352,2048]{1,0:T(8,128)(2,1)S(1)}, bf16[352,2048]{1,0:T(8,128)(2,1)S(1)}, u32[]{:S(2)}, u32[]{:S(2)}) %collective-permute-start.126) | collective-permute-done | bytes 1441824 | tf_op jit(solution)/shard_map/ppermute | solution.py:44
  612.6 8.0 collective-permute-done.72
  622.5 9.8 %collective-permute-done.55 = bf16[96,2048]{1,0:T(8,128)(2,1)S(1)} collective-permute-done((bf16[96,2048]{1,0:T(8,128)(2,1)S(1)}, bf16[96,2048]{1,0:T(8,128)(2,1)S(1)}, u32[]{:S(2)}, u32[]{:S(2)}) %collective-permute-start.55) | collective-permute-done | bytes 393248 | tf_op jit(solution)/shard_map/ppermute | solution.py:39
  638.0 13.2 %collective-permute-done.120 = bf16[176,2048]{1,0:T(8,128)(2,1)S(1)} collective-permute-done((bf16[176,2048]{1,0:T(8,128)(2,1)S(1)}, bf16[176,2048]{1,0:T(8,128)(2,1)S(1)}, u32[]{:S(2)}, u32[]{:S(2)}) %collective-permute-start.120) | collective-permute-done | bytes 720928 | tf_op jit(solution)/shard_map/ppermute | solution.py:44
  651.7 12.0 %collective-permute-done.123 = bf16[176,2048]{1,0:T(8,128)(2,1)S(1)} collective-permute-done((bf16[176,2048]{1,0:T(8,128)(2,1)S(1)}, bf16[176,2048]{1,0:T(8,128)(2,1)S(1)}, u32[]{:S(2)}, u32[]{:S(2)}) %collective-permute-start.123) | collective-permute-done | bytes 720928 | tf_op jit(solution)/shard_map/ppermute | solution.py:44
  676.1 11.0 %collective-permute-done.109 = f32[2,256]{1,0:T(2,128)S(1)} collective-permute-done((f32[2,256]{1,0:T(2,128)S(1)}, f32[2,256]{1,0:T(2,128)S(1)}, u32[]{:S(2)}, u32[]{:S(2)}) %collective-permute-start.109) | collective-permute-done | bytes 2080 | tf_op jit(solution)/shard_map/ppermute | solution.py:34
  693.4 14.6 %collective-permute-done.110 = f32[2,256]{1,0:T(2,128)S(1)} collective-permute-done((f32[2,256]{1,0:T(2,128)S(1)}, f32[2,256]{1,0:T(2,128)S(1)}, u32[]{:S(2)}, u32[]{:S(2)}) %collective-permute-start.110) | collective-permute-done | bytes 2080 | tf_op jit(solution)/shard_map/ppermute | solution.py:39
  708.0 8.9 collective-permute-start.111
  730.5 5.9 collective-permute-done.134
  769.2 5.6 convolution_convert_fusion.8
  807.7 13.1 %collective-permute-done.85 = f32[1,256]{1,0:T(1,128)S(1)} collective-permute-done((f32[1,256]{1,0:T(1,128)S(1)}, f32[1,256]{1,0:T(1,128)S(1)}, u32[]{:S(2)}, u32[]{:S(2)}) %collective-permute-start.85) | collective-permute-done | bytes 1056 | tf_op jit(solution)/shard_map/ppermute | solution.py:34
  838.0 6.8 collective-permute-done.91
  848.8 16.4 %collective-permute-done.94 = bf16[256,1536]{1,0:T(8,128)(2,1)S(1)} collective-permute-done((bf16[256,1536]{1,0:T(8,128)(2,1)S(1)}, bf16[256,1536]{1,0:T(8,128)(2,1)S(1)}, u32[]{:S(2)}, u32[]{:S(2)}) %collective-permute-start.94) | collective-permute-done | bytes 786464 | tf_op jit(solution)/shard_map/ppermute | solution.py:34
  872.3 9.8 %collective-permute-done.93 = bf16[256,1536]{1,0:T(8,128)(2,1)S(1)} collective-permute-done((bf16[256,1536]{1,0:T(8,128)(2,1)S(1)}, bf16[256,1536]{1,0:T(8,128)(2,1)S(1)}, u32[]{:S(2)}, u32[]{:S(2)}) %collective-permute-start.93) | collective-permute-done | bytes 786464 | tf_op jit(solution)/shard_map/ppermute | solution.py:34
  882.0 7.1 collective-permute-done.97
  898.7 11.4 %collective-permute-done.98 = bf16[256,1536]{1,0:T(8,128)(2,1)} collective-permute-done((bf16[256,1536]{1,0:T(8,128)(2,1)}, bf16[256,1536]{1,0:T(8,128)(2,1)}, u32[]{:S(2)}, u32[]{:S(2)}) %collective-permute-start.98) | collective-permute-done | bytes 786464 | tf_op jit(solution)/shard_map/ppermute | solution.py:39
  (712 shorter events, 443.6 us)
Async XLA Ops:
  0.7 126.5 %collective-permute-start.14 = (bf16[256,512]{0,1:T(8,128)(2,1)}, bf16[256,512]{0,1:T(8,128)(2,1)}, u32[]{:S(2)}, u32[]{:S(2)}) collective-permute-start(bf16[256,512]{0,1:T(8,128)(2,1)} %bitcast.625), channel_id=1, source_target_pairs={{0,4},{4,0},{8,12},{12,8},{16,20},{20,16},{24,28},{28,24},{1,5},{5... | collective-permute-start | bytes 786440 | tf_op jit(solution)/shard_map/ppermute | solution.py:34
  3.7 124.4 %collective-permute-start.15 = (bf16[256,512]{0,1:T(8,128)(2,1)}, bf16[256,512]{0,1:T(8,128)(2,1)}, u32[]{:S(2)}, u32[]{:S(2)}) collective-permute-start(bf16[256,512]{0,1:T(8,128)(2,1)} %bitcast.626), channel_id=1, source_target_pairs={{0,8},{4,12},{8,16},{12,20},{16,24},{20,28},{24,0},{28,4},{1,9},{5... | collective-permute-start | bytes 786440 | tf_op jit(solution)/shard_map/ppermute | solution.py:39
  10.3 149.1 %collective-permute-start.7 = (bf16[256,1536]{1,0:T(8,128)(2,1)}, bf16[256,1536]{1,0:T(8,128)(2,1)S(1)}, u32[]{:S(2)}, u32[]{:S(2)}) collective-permute-start(bf16[256,1536]{1,0:T(8,128)(2,1)} %constant_dynamic-update-slice_fusion.19), channel_id=1, source_target_pairs={{0,4},{4,0},{8,12},{12,8},{16,20},{20,16},{24,28},{28,24},{1,5},{5... | collective-permute-start | bytes 2359304 | tf_op jit(solution)/shard_map/ppermute | solution.py:34
  10.8 151.6 %collective-permute-start.8 = (bf16[256,1536]{1,0:T(8,128)(2,1)}, bf16[256,1536]{1,0:T(8,128)(2,1)}, u32[]{:S(2)}, u32[]{:S(2)}) collective-permute-start(bf16[256,1536]{1,0:T(8,128)(2,1)} %constant_dynamic-update-slice_fusion.19), channel_id=1, source_target_pairs={{0,8},{4,12},{8,16},{12,20},{16,24},{20,28},{24,0},{28,4},{1,9},{5... | collective-permute-start | bytes 2359304 | tf_op jit(solution)/shard_map/ppermute | solution.py:39
  16.9 316.1 %all-to-all-start = ((bf16[3,8,176,256]{3,2,0,1:T(8,128)(2,1)}), bf16[3,8,176,256]{3,2,0,1:T(8,128)(2,1)}, u32[]{:S(2)}, u32[]{:S(2)}) async-start(bf16[3,8,176,256]{3,2,0,1:T(8,128)(2,1)} %copy.146), calls=%async_computation | async-start | bytes 4325376 | tf_op jit(solution)/shard_map/all_to_all | solution.py:227
  22.3 25.6 %collective-permute-start.37 = (f32[96,8]{0,1:T(8,128)S(1)}, f32[96,8]{0,1:T(8,128)S(1)}, u32[]{:S(2)}, u32[]{:S(2)}) collective-permute-start(f32[96,8]{0,1:T(8,128)S(1)} %select_reduce_fusion.1), channel_id=1, source_target_pairs={{0,4},{4,0},{8,12},{12,8},{16,20},{20,16},{24,28},{28,24},{1,5},{5... | collective-permute-start | bytes 9224 | tf_op jit(solution)/shard_map/ppermute | solution.py:34
  128.2 74.1 %collective-permute-start.34 = (bf16[352,2048]{1,0:T(8,128)(2,1)}, bf16[352,2048]{1,0:T(8,128)(2,1)}, u32[]{:S(2)}, u32[]{:S(2)}) collective-permute-start(bf16[352,2048]{1,0:T(8,128)(2,1)} %bitcast.56), channel_id=1, source_target_pairs={{0,1},{1,0},{2,3},{3,2},{4,5},{5,4},{6,7},{7,6},{8,9},{9,8},{10,11... | collective-permute-start | bytes 4325384 | tf_op jit(solution)/shard_map/ppermute | solution.py:44
  155.1 55.2 %collective-permute-start.35 = (bf16[352,2048]{1,0:T(8,128)(2,1)}, bf16[352,2048]{1,0:T(8,128)(2,1)}, u32[]{:S(2)}, u32[]{:S(2)}) collective-permute-start(bf16[352,2048]{1,0:T(8,128)(2,1)} %bitcast.56), channel_id=1, source_target_pairs={{0,2},{1,3},{2,0},{3,1},{4,6},{5,7},{6,4},{7,5},{8,10},{9,11},{10,... | collective-permute-start | bytes 4325384 | tf_op jit(solution)/shard_map/ppermute | solution.py:44
  157.0 49.5 %collective-permute-start.44 = (bf16[352,2048]{1,0:T(8,128)(2,1)}, bf16[352,2048]{1,0:T(8,128)(2,1)}, u32[]{:S(2)}, u32[]{:S(2)}) collective-permute-start(bf16[352,2048]{1,0:T(8,128)(2,1)} %bitcast.71), channel_id=1, source_target_pairs={{0,1},{1,0},{2,3},{3,2},{4,5},{5,4},{6,7},{7,6},{8,9},{9,8},{10,11... | collective-permute-start | bytes 4325384 | tf_op jit(solution)/shard_map/ppermute | solution.py:44
  181.4 34.8 %collective-permute-start.45 = (bf16[352,2048]{1,0:T(8,128)(2,1)}, bf16[352,2048]{1,0:T(8,128)(2,1)}, u32[]{:S(2)}, u32[]{:S(2)}) collective-permute-start(bf16[352,2048]{1,0:T(8,128)(2,1)} %bitcast.71), channel_id=1, source_target_pairs={{0,2},{1,3},{2,0},{3,1},{4,6},{5,7},{6,4},{7,5},{8,10},{9,11},{10,... | collective-permute-start | bytes 4325384 | tf_op jit(solution)/shard_map/ppermute | solution.py:44
  202.3 42.0 %collective-permute-start.32 = (bf16[352,2048]{1,0:T(8,128)(2,1)S(1)}, bf16[352,2048]{1,0:T(8,128)(2,1)}, u32[]{:S(2)}, u32[]{:S(2)}) collective-permute-start(bf16[352,2048]{1,0:T(8,128)(2,1)S(1)} %bitcast.623), channel_id=1, source_target_pairs={{0,2},{1,3},{2,0},{3,1},{4,6},{5,7},{6,4},{7,5},{8,10},{9,11},{10,... | collective-permute-start | bytes 4325384 | tf_op jit(solution)/shard_map/ppermute | solution.py:44
  206.5 41.6 %collective-permute-start.9 = (bf16[256,1536]{1,0:T(8,128)(2,1)}, bf16[256,1536]{1,0:T(8,128)(2,1)S(1)}, u32[]{:S(2)}, u32[]{:S(2)}) collective-permute-start(bf16[256,1536]{1,0:T(8,128)(2,1)} %collective-permute-done.8), channel_id=1, source_target_pairs={{0,4},{4,0},{8,12},{12,8},{16,20},{20,16},{24,28},{28,24},{1,5},{5... | collective-permute-start | bytes 2359304 | tf_op jit(solution)/shard_map/ppermute | solution.py:34
  210.3 36.6 %collective-permute-start.10 = (bf16[256,1536]{1,0:T(8,128)(2,1)}, bf16[256,1536]{1,0:T(8,128)(2,1)S(1)}, u32[]{:S(2)}, u32[]{:S(2)}) collective-permute-start(bf16[256,1536]{1,0:T(8,128)(2,1)} %collective-permute-done.8), channel_id=1, source_target_pairs={{0,8},{4,12},{8,16},{12,20},{16,24},{20,28},{24,0},{28,4},{1,9},{5... | collective-permute-start | bytes 2359304 | tf_op jit(solution)/shard_map/ppermute | solution.py:39
  216.1 84.7 %collective-permute-start.66 = (bf16[96,2048]{1,0:T(8,128)(2,1)}, bf16[96,2048]{1,0:T(8,128)(2,1)}, u32[]{:S(2)}, u32[]{:S(2)}) collective-permute-start(bf16[96,2048]{1,0:T(8,128)(2,1)} %collective-permute-done.65), channel_id=1, source_target_pairs={{0,4},{4,0},{8,12},{12,8},{16,20},{20,16},{24,28},{28,24},{1,5},{5... | collective-permute-start | bytes 1179656 | tf_op jit(solution)/shard_map/ppermute | solution.py:34
  220.5 96.6 %collective-permute-start.36 = (bf16[352,2048]{1,0:T(8,128)(2,1)}, bf16[352,2048]{1,0:T(8,128)(2,1)}, u32[]{:S(2)}, u32[]{:S(2)}) collective-permute-start(bf16[352,2048]{1,0:T(8,128)(2,1)} %collective-permute-done.35), channel_id=1, source_target_pairs={{0,1},{1,0},{2,3},{3,2},{4,5},{5,4},{6,7},{7,6},{8,9},{9,8},{10,11... | collective-permute-start | bytes 4325384 | tf_op jit(solution)/shard_map/ppermute | solution.py:44
  244.3 58.3 %collective-permute-start.46 = (bf16[352,2048]{1,0:T(8,128)(2,1)}, bf16[352,2048]{1,0:T(8,128)(2,1)}, u32[]{:S(2)}, u32[]{:S(2)}) collective-permute-start(bf16[352,2048]{1,0:T(8,128)(2,1)} %collective-permute-done.45), channel_id=1, source_target_pairs={{0,1},{1,0},{2,3},{3,2},{4,5},{5,4},{6,7},{7,6},{8,9},{9,8},{10,11... | collective-permute-start | bytes 4325384 | tf_op jit(solution)/shard_map/ppermute | solution.py:44
  248.1 21.7 %collective-permute-start.12 = (bf16[256,1536]{1,0:T(8,128)(2,1)S(1)}, bf16[256,1536]{1,0:T(8,128)(2,1)S(1)}, u32[]{:S(2)}, u32[]{:S(2)}) collective-permute-start(bf16[256,1536]{1,0:T(8,128)(2,1)S(1)} %collective-permute-done.10), channel_id=1, source_target_pairs={{0,8},{4,12},{8,16},{12,20},{16,24},{20,28},{24,0},{28,4},{1,9},{5... | collective-permute-start | bytes 2359304 | tf_op jit(solution)/shard_map/ppermute | solution.py:39
  267.0 63.3 %collective-permute-start.33 = (bf16[352,2048]{1,0:T(8,128)(2,1)}, bf16[352,2048]{1,0:T(8,128)(2,1)}, u32[]{:S(2)}, u32[]{:S(2)}) collective-permute-start(bf16[352,2048]{1,0:T(8,128)(2,1)} %collective-permute-done.32), channel_id=1, source_target_pairs={{0,1},{1,0},{2,3},{3,2},{4,5},{5,4},{6,7},{7,6},{8,9},{9,8},{10,11... | collective-permute-start | bytes 4325384 | tf_op jit(solution)/shard_map/ppermute | solution.py:44
  336.2 49.8 %collective-permute-start.47 = (bf16[3,176,2048]{2,1,0:T(8,128)(2,1)}, bf16[3,176,2048]{2,1,0:T(8,128)(2,1)}, u32[]{:S(2)}, u32[]{:S(2)}) collective-permute-start(bf16[3,176,2048]{2,1,0:T(8,128)(2,1)} %bitcast.272), channel_id=1, source_target_pairs={{0,1},{1,0},{2,3},{3,2},{4,5},{5,4},{6,7},{7,6},{8,9},{9,8},{10,11... | collective-permute-start | bytes 6488072 | tf_op jit(solution)/shard_map/ppermute | solution.py:44
  336.2 49.8 %collective-permute-start.48 = (bf16[3,176,2048]{2,1,0:T(8,128)(2,1)}, bf16[3,176,2048]{2,1,0:T(8,128)(2,1)}, u32[]{:S(2)}, u32[]{:S(2)}) collective-permute-start(bf16[3,176,2048]{2,1,0:T(8,128)(2,1)} %bitcast.272), channel_id=1, source_target_pairs={{0,2},{1,3},{2,0},{3,1},{4,6},{5,7},{6,4},{7,5},{8,10},{9,11},{10,... | collective-permute-start | bytes 6488072 | tf_op jit(solution)/shard_map/ppermute | solution.py:44
  386.0 71.3 %collective-permute-start.49 = (bf16[3,176,2048]{2,1,0:T(8,128)(2,1)}, bf16[3,176,2048]{2,1,0:T(8,128)(2,1)}, u32[]{:S(2)}, u32[]{:S(2)}) collective-permute-start(bf16[3,176,2048]{2,1,0:T(8,128)(2,1)} %collective-permute-done.48), channel_id=1, source_target_pairs={{0,1},{1,0},{2,3},{3,2},{4,5},{5,4},{6,7},{7,6},{8,9},{9,8},{10,11... | collective-permute-start | bytes 6488072 | tf_op jit(solution)/shard_map/ppermute | solution.py:44
  445.0 98.4 %collective-permute-start.130 = (bf16[352,2048]{1,0:T(8,128)(2,1)}, bf16[352,2048]{1,0:T(8,128)(2,1)}, u32[]{:S(2)}, u32[]{:S(2)}) collective-permute-start(bf16[352,2048]{1,0:T(8,128)(2,1)} %get-tuple-element.133), channel_id=1, source_target_pairs={{0,1},{1,0},{2,3},{3,2},{4,5},{5,4},{6,7},{7,6},{8,9},{9,8},{10,11... | collective-permute-start | bytes 4325384 | tf_op jit(solution)/shard_map/ppermute | solution.py:44
  445.0 131.9 %collective-permute-start.127 = (bf16[352,2048]{1,0:T(8,128)(2,1)}, bf16[352,2048]{1,0:T(8,128)(2,1)}, u32[]{:S(2)}, u32[]{:S(2)}) collective-permute-start(bf16[352,2048]{1,0:T(8,128)(2,1)} %get-tuple-element.135), channel_id=1, source_target_pairs={{0,1},{1,0},{2,3},{3,2},{4,5},{5,4},{6,7},{7,6},{8,9},{9,8},{10,11... | collective-permute-start | bytes 4325384 | tf_op jit(solution)/shard_map/ppermute | solution.py:44
  449.0 122.0 %collective-permute-start.132 = (bf16[352,2048]{1,0:T(8,128)(2,1)}, bf16[352,2048]{1,0:T(8,128)(2,1)}, u32[]{:S(2)}, u32[]{:S(2)}) collective-permute-start(bf16[352,2048]{1,0:T(8,128)(2,1)} %fusion.5), channel_id=1, source_target_pairs={{0,2},{1,3},{2,0},{3,1},{4,6},{5,7},{6,4},{7,5},{8,10},{9,11},{10,... | collective-permute-start | bytes 4325384 | tf_op jit(solution)/shard_map/ppermute | solution.py:44
  543.4 34.5 %collective-permute-start.129 = (bf16[352,2048]{1,0:T(8,128)(2,1)S(1)}, bf16[352,2048]{1,0:T(8,128)(2,1)S(1)}, u32[]{:S(2)}, u32[]{:S(2)}) collective-permute-start(bf16[352,2048]{1,0:T(8,128)(2,1)S(1)} %copy-done.42), channel_id=1, source_target_pairs={{0,2},{1,3},{2,0},{3,1},{4,6},{5,7},{6,4},{7,5},{8,10},{9,11},{10,... | collective-permute-start | bytes 4325384 | tf_op jit(solution)/shard_map/ppermute | solution.py:44
  569.2 38.9 %collective-permute-start.126 = (bf16[352,2048]{1,0:T(8,128)(2,1)S(1)}, bf16[352,2048]{1,0:T(8,128)(2,1)S(1)}, u32[]{:S(2)}, u32[]{:S(2)}) collective-permute-start(bf16[352,2048]{1,0:T(8,128)(2,1)S(1)} %copy-done.41), channel_id=1, source_target_pairs={{0,2},{1,3},{2,0},{3,1},{4,6},{5,7},{6,4},{7,5},{8,10},{9,11},{10,... | collective-permute-start | bytes 4325384 | tf_op jit(solution)/shard_map/ppermute | solution.py:44
  571.1 40.9 %collective-permute-start.68 = (bf16[96,2048]{1,0:T(8,128)(2,1)S(1)}, bf16[96,2048]{1,0:T(8,128)(2,1)S(1)}, u32[]{:S(2)}, u32[]{:S(2)}) collective-permute-start(bf16[96,2048]{1,0:T(8,128)(2,1)S(1)} %copy-done.63), channel_id=1, source_target_pairs={{0,4},{4,0},{8,12},{12,8},{16,20},{20,16},{24,28},{28,24},{1,5},{5... | collective-permute-start | bytes 1179656 | tf_op jit(solution)/shard_map/ppermute | solution.py:34
  576.9 94.3 %collective-permute-start.67 = (bf16[96,2048]{1,0:T(8,128)(2,1)}, bf16[96,2048]{1,0:T(8,128)(2,1)}, u32[]{:S(2)}, u32[]{:S(2)}) collective-permute-start(bf16[96,2048]{1,0:T(8,128)(2,1)} %get-tuple-element.140), channel_id=1, source_target_pairs={{0,4},{4,0},{8,12},{12,8},{16,20},{20,16},{24,28},{28,24},{1,5},{5... | collective-permute-start | bytes 1179656 | tf_op jit(solution)/shard_map/ppermute | solution.py:34
  577.9 44.6 %collective-permute-start.51 = (bf16[96,2048]{1,0:T(8,128)(2,1)S(1)}, bf16[96,2048]{1,0:T(8,128)(2,1)S(1)}, u32[]{:S(2)}, u32[]{:S(2)}) collective-permute-start(bf16[96,2048]{1,0:T(8,128)(2,1)S(1)} %copy-done.62), channel_id=1, source_target_pairs={{0,4},{4,0},{8,12},{12,8},{16,20},{20,16},{24,28},{28,24},{1,5},{5... | collective-permute-start | bytes 1179656 | tf_op jit(solution)/shard_map/ppermute | solution.py:34
  583.0 51.9 %collective-permute-start.115 = (bf16[176,2048]{1,0:T(8,128)(2,1)S(1)}, bf16[176,2048]{1,0:T(8,128)(2,1)S(1)}, u32[]{:S(2)}, u32[]{:S(2)}) collective-permute-start(bf16[176,2048]{1,0:T(8,128)(2,1)S(1)} %copy-done.52), channel_id=1, source_target_pairs={{0,1},{1,0},{2,3},{3,2},{4,5},{5,4},{6,7},{7,6},{8,9},{9,8},{10,11... | collective-permute-start | bytes 2162696 | tf_op jit(solution)/shard_map/ppermute | solution.py:44
  612.0 22.8 %collective-permute-start.117 = (bf16[176,2048]{1,0:T(8,128)(2,1)S(1)}, bf16[176,2048]{1,0:T(8,128)(2,1)S(1)}, u32[]{:S(2)}, u32[]{:S(2)}) collective-permute-start(bf16[176,2048]{1,0:T(8,128)(2,1)S(1)} %fusion.26), channel_id=1, source_target_pairs={{0,2},{1,3},{2,0},{3,1},{4,6},{5,7},{6,4},{7,5},{8,10},{9,11},{10,... | collective-permute-start | bytes 2162696 | tf_op jit(solution)/shard_map/ppermute | solution.py:44
  634.8 28.9 %collective-permute-start.123 = (bf16[176,2048]{1,0:T(8,128)(2,1)S(1)}, bf16[176,2048]{1,0:T(8,128)(2,1)S(1)}, u32[]{:S(2)}, u32[]{:S(2)}) collective-permute-start(bf16[176,2048]{1,0:T(8,128)(2,1)S(1)} %fusion.20), channel_id=1, source_target_pairs={{0,2},{1,3},{2,0},{3,1},{4,6},{5,7},{6,4},{7,5},{8,10},{9,11},{10,... | collective-permute-start | bytes 2162696 | tf_op jit(solution)/shard_map/ppermute | solution.py:44
  636.7 34.5 %collective-permute-start.50 = (bf16[96,2048]{1,0:T(8,128)(2,1)}, bf16[96,2048]{1,0:T(8,128)(2,1)S(1)}, u32[]{:S(2)}, u32[]{:S(2)}) collective-permute-start(bf16[96,2048]{1,0:T(8,128)(2,1)} %get-tuple-element.144), channel_id=1, source_target_pairs={{0,4},{4,0},{8,12},{12,8},{16,20},{20,16},{24,28},{28,24},{1,5},{5... | collective-permute-start | bytes 1179656 | tf_op jit(solution)/shard_map/ppermute | solution.py:34
  666.6 224.9 %all-to-all-start.1 = ((bf16[3,8,176,256]{3,2,0,1:T(8,128)(2,1)}), bf16[3,8,176,256]{3,2,0,1:T(8,128)(2,1)}, u32[]{:S(2)}, u32[]{:S(2)}) async-start(bf16[3,8,176,256]{3,2,0,1:T(8,128)(2,1)} %copy.157), calls=%async_computation.1 | async-start | bytes 4325376 | tf_op jit(solution)/shard_map/all_to_all | solution.py:291
  687.0 20.9 %collective-permute-start.110 = (f32[2,256]{1,0:T(2,128)S(1)}, f32[2,256]{1,0:T(2,128)S(1)}, u32[]{:S(2)}, u32[]{:S(2)}) collective-permute-start(f32[2,256]{1,0:T(2,128)S(1)} %bitcast_add_fusion.2), channel_id=1, source_target_pairs={{0,8},{4,12},{8,16},{12,20},{16,24},{20,28},{24,0},{28,4},{1,9},{5... | collective-permute-start | bytes 6152 | tf_op jit(solution)/shard_map/ppermute | solution.py:39
  690.0 51.0 %collective-permute-start.74 = (bf16[96,2048]{1,0:T(8,128)(2,1)S(1)}, bf16[96,2048]{1,0:T(8,128)(2,1)S(1)}, u32[]{:S(2)}, u32[]{:S(2)}) collective-permute-start(bf16[96,2048]{1,0:T(8,128)(2,1)S(1)} %get-tuple-element.111), channel_id=1, source_target_pairs={{0,1},{1,0},{2,3},{3,2},{4,5},{5,4},{6,7},{7,6},{8,9},{9,8},{10,11... | collective-permute-start | bytes 1179656 | tf_op jit(solution)/shard_map/ppermute | solution.py:44
  690.1 50.4 %collective-permute-start.75 = (bf16[96,2048]{1,0:T(8,128)(2,1)S(1)}, bf16[96,2048]{1,0:T(8,128)(2,1)S(1)}, u32[]{:S(2)}, u32[]{:S(2)}) collective-permute-start(bf16[96,2048]{1,0:T(8,128)(2,1)S(1)} %get-tuple-element.111), channel_id=1, source_target_pairs={{0,2},{1,3},{2,0},{3,1},{4,6},{5,7},{6,4},{7,5},{8,10},{9,11},{10,... | collective-permute-start | bytes 1179656 | tf_op jit(solution)/shard_map/ppermute | solution.py:44
  690.8 29.4 %collective-permute-start.107 = (f32[2,256]{1,0:T(2,128)S(1)}, f32[2,256]{1,0:T(2,128)S(1)}, u32[]{:S(2)}, u32[]{:S(2)}) collective-permute-start(f32[2,256]{1,0:T(2,128)S(1)} %bitcast.649), channel_id=1, source_target_pairs={{0,4},{4,0},{8,12},{12,8},{16,20},{20,16},{24,28},{28,24},{1,5},{5... | collective-permute-start | bytes 6152 | tf_op jit(solution)/shard_map/ppermute | solution.py:34
  693.3 31.7 %collective-permute-start.106 = (f32[2,256]{1,0:T(2,128)S(1)}, f32[2,256]{1,0:T(2,128)S(1)}, u32[]{:S(2)}, u32[]{:S(2)}) collective-permute-start(f32[2,256]{1,0:T(2,128)S(1)} %bitcast.647), channel_id=1, source_target_pairs={{0,4},{4,0},{8,12},{12,8},{16,20},{20,16},{24,28},{28,24},{1,5},{5... | collective-permute-start | bytes 6152 | tf_op jit(solution)/shard_map/ppermute | solution.py:34
  720.3 20.8 %collective-permute-start.57 = (bf16[96,2048]{1,0:T(8,128)(2,1)S(1)}, bf16[96,2048]{1,0:T(8,128)(2,1)S(1)}, u32[]{:S(2)}, u32[]{:S(2)}) collective-permute-start(bf16[96,2048]{1,0:T(8,128)(2,1)S(1)} %get-tuple-element.116), channel_id=1, source_target_pairs={{0,1},{1,0},{2,3},{3,2},{4,5},{5,4},{6,7},{7,6},{8,9},{9,8},{10,11... | collective-permute-start | bytes 1179656 | tf_op jit(solution)/shard_map/ppermute | solution.py:44
  740.5 56.0 %collective-permute-start.59 = (bf16[96,2048]{1,0:T(8,128)(2,1)}, bf16[96,2048]{1,0:T(8,128)(2,1)}, u32[]{:S(2)}, u32[]{:S(2)}) collective-permute-start(bf16[96,2048]{1,0:T(8,128)(2,1)} %collective-permute-done.58), channel_id=1, source_target_pairs={{0,1},{1,0},{2,3},{3,2},{4,5},{5,4},{6,7},{7,6},{8,9},{9,8},{10,11... | collective-permute-start | bytes 1179656 | tf_op jit(solution)/shard_map/ppermute | solution.py:44
  759.9 31.0 %collective-permute-start.102 = (bf16[256,512]{0,1:T(8,128)(2,1)}, bf16[256,512]{0,1:T(8,128)(2,1)}, u32[]{:S(2)}, u32[]{:S(2)}) collective-permute-start(bf16[256,512]{0,1:T(8,128)(2,1)} %bitcast.629), channel_id=1, source_target_pairs={{0,4},{4,0},{8,12},{12,8},{16,20},{20,16},{24,28},{28,24},{1,5},{5... | collective-permute-start | bytes 786440 | tf_op jit(solution)/shard_map/ppermute | solution.py:34
  790.9 42.3 %collective-permute-start.100 = (bf16[256,512]{0,1:T(8,128)(2,1)}, bf16[256,512]{0,1:T(8,128)(2,1)}, u32[]{:S(2)}, u32[]{:S(2)}) collective-permute-start(bf16[256,512]{0,1:T(8,128)(2,1)} %bitcast.628), channel_id=1, source_target_pairs={{0,4},{4,0},{8,12},{12,8},{16,20},{20,16},{24,28},{28,24},{1,5},{5... | collective-permute-start | bytes 786440 | tf_op jit(solution)/shard_map/ppermute | solution.py:34
  802.0 33.2 %collective-permute-start.95 = (bf16[256,1536]{1,0:T(8,128)(2,1)}, bf16[256,1536]{1,0:T(8,128)(2,1)S(1)}, u32[]{:S(2)}, u32[]{:S(2)}) collective-permute-start(bf16[256,1536]{1,0:T(8,128)(2,1)} %get-tuple-element.130), channel_id=1, source_target_pairs={{0,4},{4,0},{8,12},{12,8},{16,20},{20,16},{24,28},{28,24},{1,5},{5... | collective-permute-start | bytes 2359304 | tf_op jit(solution)/shard_map/ppermute | solution.py:34
  805.4 28.6 %collective-permute-start.104 = (bf16[256,512]{0,1:T(8,128)(2,1)S(1)}, bf16[256,512]{0,1:T(8,128)(2,1)S(1)}, u32[]{:S(2)}, u32[]{:S(2)}) collective-permute-start(bf16[256,512]{0,1:T(8,128)(2,1)S(1)} %fusion.78), channel_id=1, source_target_pairs={{0,8},{4,12},{8,16},{12,20},{16,24},{20,28},{24,0},{28,4},{1,9},{5... | collective-permute-start | bytes 786440 | tf_op jit(solution)/shard_map/ppermute | solution.py:39
  845.7 36.4 %collective-permute-start.93 = (bf16[256,1536]{1,0:T(8,128)(2,1)S(1)}, bf16[256,1536]{1,0:T(8,128)(2,1)S(1)}, u32[]{:S(2)}, u32[]{:S(2)}) collective-permute-start(bf16[256,1536]{1,0:T(8,128)(2,1)S(1)} %copy-done.49), channel_id=1, source_target_pairs={{0,4},{4,0},{8,12},{12,8},{16,20},{20,16},{24,28},{28,24},{1,5},{5... | collective-permute-start | bytes 2359304 | tf_op jit(solution)/shard_map/ppermute | solution.py:34
  847.4 51.3 %collective-permute-start.92 = (bf16[256,1536]{1,0:T(8,128)(2,1)}, bf16[256,1536]{1,0:T(8,128)(2,1)}, u32[]{:S(2)}, u32[]{:S(2)}) collective-permute-start(bf16[256,1536]{1,0:T(8,128)(2,1)} %get-tuple-element.129), channel_id=1, source_target_pairs={{0,4},{4,0},{8,12},{12,8},{16,20},{20,16},{24,28},{28,24},{1,5},{5... | collective-permute-start | bytes 2359304 | tf_op jit(solution)/shard_map/ppermute | solution.py:34
  848.6 21.5 %collective-permute-start.82 = (bf16[96,2048]{1,0:T(8,128)(2,1)S(1)}, bf16[96,2048]{1,0:T(8,128)(2,1)S(1)}, u32[]{:S(2)}, u32[]{:S(2)}) collective-permute-start(bf16[96,2048]{1,0:T(8,128)(2,1)S(1)} %collective-permute-done.81), channel_id=1, source_target_pairs={{0,1},{1,0},{2,3},{3,2},{4,5},{5,4},{6,7},{7,6},{8,9},{9,8},{10,11... | collective-permute-start | bytes 1179656 | tf_op jit(solution)/shard_map/ppermute | solution.py:44
  (192 other events, 2419.5 us)

commit v2 on v1

--- a/solution.py
+++ b/solution.py
@@ -29,6 +29,10 @@
     return lax.dynamic_update_index_in_dim(array, value, index, 0)
 
 
+def after(value, *earlier):
+    return lax.optimization_barrier((value,) + earlier)[0]
+
+
 def swap_inner(value):
     size = lax.axis_size("ep")
     return lax.ppermute(value, "ep", [(i, i ^ 1) for i in range(size)])
@@ -44,57 +48,84 @@
     return lax.ppermute(value, "tp", [(i, i ^ mask) for i in range(size)])
 
 
-def gather_ep(shard):
+def relative_to_absolute():
     size = lax.axis_size("ep")
-    rounds = size // 2
     me = lax.axis_index("ep")
     outer, inner = me // 2, me % 2
-    whole = jnp.zeros((size,) + shard.shape, shard.dtype)
+    rounds = size // 2
+    return [(outer + rounds - r // 2) % rounds * 2 + (inner ^ r % 2) for r in range(size)]
+
+
+def gather_ep(shard):
+    rounds = lax.axis_size("ep") // 2
+    blocks = []
     current = shard
     for k in range(rounds):
-        where = (outer + rounds - k) % rounds * 2
-        other = swap_inner(current)
-        whole = put(whole, current, where + inner)
-        following = ring_outer(current) if k < rounds - 1 else None
-        whole = put(whole, other, where + 1 - inner)
-        current = following
+        blocks += [current, swap_inner(current)]
+        if k < rounds - 1:
+            current = ring_outer(current)
+    return blocks, current
+
+
+def stack_static(blocks):
+    whole = jnp.zeros((len(blocks),) + blocks[0].shape, blocks[0].dtype)
+    for i, block in enumerate(blocks):
+        whole = whole.at[i].set(block)
     return whole
 
 
-def scatter_ep(parts, sent=BF):
-    size = lax.axis_size("ep")
-    rounds = size // 2
-    me = lax.axis_index("ep")
-    outer, inner = me // 2, me % 2
-    arrived = None
+def stack_absolute(blocks):
+    whole = jnp.zeros((len(blocks),) + blocks[0].shape, blocks[0].dtype)
+    for block, index in zip(blocks, relative_to_absolute()):
+        whole = put(whole, block, index)
+    return whole
+
+
+def scatter_ep(block_of):
+    rounds = lax.axis_size("ep") // 2
+    arrived = other = None
     for k in list(range(1, rounds)) + [0]:
-        where = (outer + rounds - k) % rounds * 2
-        other = swap_inner(at(parts, where + 1 - inner).astype(sent))
-        total = at(parts, where + inner).astype(F32) + other.astype(F32)
+        away = block_of(2 * k + 1).astype(BF)
+        if other is not None:
+            away = after(away, other)
+        other = swap_inner(away)
+        total = block_of(2 * k).astype(F32) + other.astype(F32)
         if arrived is not None:
             total = total + arrived.astype(F32)
         if k:
-            arrived = ring_outer(total.astype(sent))
+            arrived = ring_outer(total.astype(BF))
     return total
 
 
+def scatter_absolute(parts):
+    order = relative_to_absolute()
+    return scatter_ep(lambda r: at(parts, order[r]))
+
+
 def gather_tp(shard):
+    far = swap_tp(shard, 2)
+    return [shard, swap_tp(shard, 1), far, swap_tp(far, 1)]
+
+
+def gather_tp_rows(shard):
     me = lax.axis_index("tp")
     whole = jnp.zeros((lax.axis_size("tp"),) + shard.shape, shard.dtype)
-    far = swap_tp(shard, 2)
-    whole = put(whole, shard, me)
-    whole = put(whole, swap_tp(shard, 1), me ^ 1)
-    whole = put(whole, far, me ^ 2)
-    return put(whole, swap_tp(far, 1), me ^ 3)
-
-
-def scatter_tp(parts, sent=BF):
+    for j, block in enumerate(gather_tp(shard)):
+        whole = put(whole, block, me ^ j)
+    return whole.reshape(-1, shard.shape[-1])
+
+
+def scatter_tp(block_of):
+    near_far = swap_tp(block_of(3).astype(BF), 1)
+    far = block_of(2).astype(F32) + near_far.astype(F32)
+    near = swap_tp(block_of(1).astype(BF), 1)
+    far = swap_tp(far.astype(BF), 2)
+    return block_of(0).astype(F32) + near.astype(F32) + far.astype(F32)
+
+
+def scatter_tp_rows(parts):
     me = lax.axis_index("tp")
-    near_far = swap_tp(at(parts, me ^ 3).astype(sent), 1)
-    far = at(parts, me ^ 2).astype(F32) + near_far.astype(F32)
-    far = swap_tp(far.astype(sent), 2)
-    near = swap_tp(at(parts, me ^ 1).astype(sent), 1)
-    return at(parts, me).astype(F32) + near.astype(F32) + far.astype(F32)
+    return scatter_tp(lambda j: at(parts, me ^ j))
 
 
 def sum_tp(value):
@@ -128,7 +159,6 @@
     r_hidden = (jax.nn.silu(r_gate_val) * r_up_val * gates).astype(BF)
     s_plain = jax.nn.silu(s_gate_val) * s_up_val
     s_hidden = (s_plain * score).astype(BF)
-    out = (nn(r_hidden, r_down) + nn(s_hidden, s_down)).astype(BF)
     r_back = nt(gout, r_down)
     s_back = nt(gout, s_down)
     r_dgate, r_dup = gated_back(r_back * gates, r_gate_val, r_up_val)
@@ -136,6 +166,9 @@
     gscore = score * (1.0 - score) * jnp.sum(s_plain * s_back, axis=1, keepdims=True)
     gact = nn(r_dgate, r_gate) + nn(r_dup, r_up) + nn(s_dgate, s_gate) + nn(s_dup, s_up)
     gact = (gact + gscore * logit32).astype(BF)
+    act, gout, r_hidden, s_hidden, gscore = lax.optimization_barrier(
+        (act, gout, r_hidden, s_hidden, gscore, gact)
+    )[:5]
     logit_part = jnp.sum(act.astype(F32) * gscore, axis=0)
     pairs = (
         (r_dgate, act),
@@ -145,6 +178,7 @@
         (s_dup, act),
         (s_hidden, gout),
     )
+    out = (nn(r_hidden, r_down) + nn(s_hidden, s_down)).astype(BF)
     return out, gact, (logit_part,) + tuple(tn(left, right) for left, right in pairs)
 
 
@@ -204,31 +238,47 @@
     def own(array):
         return lax.dynamic_slice_in_dim(array, me_tp * part, part, 0)
 
-    vectors = jnp.stack([first_gain, second_gain, shared_logit])
-    vectors = gather_ep(jnp.pad(vectors, ((0, 5), (0, 0))))
-    vectors = vectors.transpose(1, 0, 2).reshape(8, width)
-    gain_one32 = vectors[0:1].astype(F32)
-    gain_two32 = vectors[1:2].astype(F32)
-    logit32 = vectors[2:3].astype(F32)
-    w_qkv = gather_ep(jnp.concatenate([query_weight, key_weight, value_weight], axis=1))
-    w_qkv = w_qkv.reshape(width, 3 * wide)
-    w_out = gather_ep(output_weight.T).reshape(width, wide)
-
-    def units_first(array):
-        return gather_tp(array).reshape(-1, width)
-
-    r_gate = units_first(routed_gate_weight[0].T)
-    r_up = units_first(routed_up_weight[0].T)
-    r_down = units_first(expert_down[0])
+    dense = jnp.sum(
+        own(route_gates)[:, :, None]
+        * (own(route_ids)[:, :, None] == jnp.arange(groups, dtype=jnp.int32)).astype(F32),
+        axis=1,
+    )
+    rows = query_weight.shape[0]
+    high = dense.astype(BF)
+    low = (dense - high.astype(F32)).astype(BF)
+    packed = jnp.concatenate([high.reshape(-1), low.reshape(-1)]).reshape(-1, rows)
+    spare = jnp.concatenate([jnp.stack([first_gain, second_gain, shared_logit]), packed]).T
+    spare = jnp.pad(spare, ((0, 0), (0, -spare.shape[1] % 128)))
+    blocks, last = gather_ep(
+        jnp.concatenate([query_weight, key_weight, value_weight, spare], axis=1)
+    )
+    w_qkv = stack_absolute(blocks)
+    spare = w_qkv[:, :, 3 * wide :]
+    w_qkv = w_qkv.reshape(width, -1)
+    vectors = spare[:, :, :3].reshape(width, 3).T.astype(F32)
+    gain_one32, gain_two32, logit32 = vectors[0:1], vectors[1:2], vectors[2:3]
+    packed = spare[:, :, 3 : 3 + packed.shape[0]].transpose(0, 2, 1)
+    packed = packed.reshape(groups, 2, part, groups).astype(F32).sum(axis=1)
+    chosen = jnp.arange(groups, dtype=jnp.int32)
+    gates = jnp.sum(jnp.where(chosen == me_ep, packed, 0.0), axis=2)
+    order = jnp.stack(relative_to_absolute())
+    gates = jnp.sum(jnp.where((order[:, None] == chosen)[:, :, None], gates[None], 0.0), axis=1)
+    gates = gates.reshape(groups * part, 1)
+    blocks, last = gather_ep(after(output_weight.T, last))
+    w_out = stack_absolute(blocks).reshape(width, wide)
+
+    def from_tp(array):
+        return stack_static(gather_tp(array)).transpose(1, 0, 2, 3).reshape(3, -1, width)
+
+    routed = from_tp(
+        jnp.stack([routed_gate_weight[0].T, routed_up_weight[0].T, expert_down[0]])
+    )
 
     units = shared_down.shape[0]
     piece = units // groups
     shared = jnp.stack([shared_gate.T, shared_up.T, shared_down]).reshape(3, groups, piece, -1)
-    shared = lax.all_to_all(shared, "ep", split_axis=1, concat_axis=1, tiled=True)
-    shared = shared.transpose(0, 2, 1, 3).reshape(3, piece, width)
-    shared = gather_tp(shared)
-    shared = shared.transpose(1, 0, 2, 3).reshape(3, quarters * piece, width)
-    s_gate, s_up, s_down = shared[0], shared[1], shared[2]
+    shared = lax.all_to_all(after(shared, last), "ep", split_axis=1, concat_axis=1, tiled=True)
+    shared = from_tp(shared.transpose(0, 2, 1, 3).reshape(3, piece, width))
 
     inputs32 = tokens.astype(F32)
     scale_one = rms_scale(inputs32)
@@ -249,31 +299,26 @@
         mixes.append(nn(probs, columns(value, h)).astype(BF))
     attn_mix = jnp.concatenate(mixes, axis=1)
     branch = nt(attn_mix, w_out).reshape(quarters, part, width)
-    attn_branch = scatter_tp(branch, F32)
+    attn_branch = scatter_tp_rows(branch)
 
     inputs_own = own(tokens).astype(F32)
     resid = inputs_own + attn_branch
     scale_two = rms_scale(resid)
     act2 = (resid * scale_two * gain_two32).astype(BF)
 
-    dense = jnp.sum(
-        own(route_gates)[:, :, None]
-        * (own(route_ids)[:, :, None] == jnp.arange(groups, dtype=jnp.int32)).astype(F32),
-        axis=1,
-    )
-    gates = gather_ep(dense).reshape(groups * part, groups)
-    gates = jnp.sum(
-        jnp.where(jnp.arange(groups)[None, :] == me_ep, gates, 0.0), axis=1, keepdims=True
-    )
-    gout_all = gather_ep(own(block_grad)).reshape(groups * part, width)
-    act_all = gather_ep(act2).reshape(groups * part, width)
-
+    blocks, last = gather_ep(act2)
+    act_all = stack_static(blocks).reshape(groups * part, width)
+    blocks, _ = gather_ep(after(own(block_grad), last))
+    gout_all = stack_static(blocks).reshape(groups * part, width)
     ffn_part, gact_part, logit_part, sums = experts(
-        act_all, gout_all, gates, logit32, (r_gate, r_up, r_down), (s_gate, s_up, s_down)
-    )
-    ffn_branch = scatter_ep(ffn_part.reshape(groups, part, width))
+        act_all, gout_all, gates, logit32, tuple(routed), tuple(shared)
+    )
+    gact_part = gact_part.reshape(groups, part, width)
+    gact2 = scatter_ep(lambda r: gact_part[r])
+    ffn_part = after(ffn_part, gact2).reshape(groups, part, width)
+    ffn_branch = scatter_ep(lambda r: ffn_part[r])
     block_sum = resid + ffn_branch
-    block_out = gather_tp(block_sum.astype(BF)).reshape(count, width)
+    block_out = gather_tp_rows(block_sum.astype(BF))
     squares = jnp.stack(
         [
             jnp.sum(attn_branch * attn_branch),
@@ -283,10 +328,13 @@
     )
     rms_values = jnp.sqrt(sum_tp(squares) / (count * width))[None, :]
 
-    gact2 = scatter_ep(gact_part.reshape(groups, part, width))
-    sums = [scatter_tp(total.astype(BF).reshape(quarters, -1, width)) for total in sums]
-    gate_grad, up_grad, down_grad = sums[0].T, sums[1].T, sums[2]
-    shared_grads = jnp.stack(sums[3:])
+    def from_hidden(arrays):
+        parts = [array.astype(BF).reshape(quarters, -1, width) for array in arrays]
+        return scatter_tp(lambda j: jnp.stack([array[j] for array in parts]))
+
+    shared_grads = from_hidden(sums[3:])
+    gate_grad, up_grad, down_grad = from_hidden([after(x, shared_grads) for x in sums[:3]])
+    gate_grad, up_grad = gate_grad.T, up_grad.T
     shared_grads = shared_grads.astype(BF).reshape(3, piece, groups, -1).transpose(0, 2, 1, 3)
     shared_grads = lax.all_to_all(shared_grads, "ep", split_axis=1, concat_axis=1, tiled=True)
     shared_grads = shared_grads.reshape(3, units, -1)
@@ -296,8 +344,13 @@
 
     resid_part, gain_two_part = norm_back(gact2, resid, scale_two, gain_two32)
     gresid = own(block_grad).astype(F32) + resid_part
-    gattn = gather_tp(gresid.astype(BF)).reshape(count, width)
-    output_grad = scatter_ep(tn(gattn, attn_mix).astype(BF).reshape(groups, -1, wide)).T
+    gattn = gather_tp_rows(gresid.astype(BF))
+    vectors = jnp.stack([gain_two_part, logit_part], axis=1).reshape(groups, -1, 2)
+    vectors = jnp.pad(vectors, ((0, 0), (0, 0), (0, 126))).astype(BF)
+    out_grads = tn(gattn, attn_mix).astype(BF).reshape(groups, -1, wide)
+    out_grads = scatter_absolute(jnp.concatenate([out_grads, vectors], axis=2))
+    output_grad = out_grads[:, :wide].T
+    early = sum_tp(out_grads[:, wide : wide + 2])
     gmix = nn(gattn, w_out).astype(BF)
     gqs, gks, gvs = [], [], []
     for h in range(local_heads):
@@ -311,27 +364,25 @@
         gqs.append((nn(gscores, key_h) * factor).astype(BF))
         gks.append((tn(gscores, query_h) * factor).astype(BF))
     gqkv = jnp.concatenate(gqs + gks + gvs, axis=1)
-    qkv_grad = scatter_ep(tn(act1, gqkv).astype(BF).reshape(groups, -1, 3 * wide))
-    gact1 = scatter_tp(nt(gqkv, w_qkv).astype(BF).reshape(quarters, part, width))
+    gqkv_grad = tn(act1, gqkv).astype(BF).reshape(groups, -1, 3 * wide)
+    qkv_grad = scatter_absolute(after(gqkv_grad, out_grads))
+    gact1 = nt(gqkv, w_qkv[:, : 3 * wide]).astype(BF).reshape(quarters, part, width)
+    gact1 = scatter_tp_rows(gact1)
     input_part, gain_one_part = norm_back(gact1, inputs_own, own(scale_one), gain_one32)
-    tokens_grad = gather_tp((gresid + input_part).astype(BF)).reshape(count, width).astype(F32)
-
-    def summed(vector_parts):
-        stacked = jnp.stack(vector_parts).reshape(len(vector_parts), groups, -1)
-        return sum_tp(scatter_ep(stacked.transpose(1, 0, 2), F32))
-
-    early = summed([gain_two_part, logit_part])
-    late = summed([gain_one_part])
+    tokens_grad = gather_tp_rows((gresid + input_part).astype(BF)).astype(F32)
+
+    late = gain_one_part.reshape(groups, -1)
+    late = sum_tp(scatter_absolute(late))
     return (
         block_out,
         tokens_grad,
-        late[0],
+        late,
         qkv_grad[:, :wide],
         qkv_grad[:, wide : 2 * wide],
         qkv_grad[:, 2 * wide :],
         output_grad,
-        early[0],
-        early[1],
+        early[:, 0],
+        early[:, 1],
         sgate_grad,
         sup_grad,
         sdown_grad,

time: 924 us -> 776 us (0.84)
  waiting for transfers between devices: 400 us -> 312 us
  starting transfers between devices: 127 us -> 84.9 us
  matrix products: 149 us -> 126 us
    ppermute x48 -> x36, waiting for transfers between devices: 136 us -> 62.8 us  [swap_inner(): return lax.ppermute(value, 'ep', [(i, i ^ 1) for i in range(size)])]
    ppermute x51 -> x33, waiting for transfers between devices: 108 us -> 58.1 us  [swap_tp(): return lax.ppermute(value, 'tp', [(i, i ^ mask) for i in range(size)])]
    scatter x0 -> x24, local copies, waits for them, and re-layouts: none -> 40.7 us  [stack_static(): whole = whole.at[i].set(block)]
    dynamic_update_slice x72 -> x25, local copies, waits for them, and re-layouts: 68.7 us -> 29.8 us  [put(): return lax.dynamic_update_index_in_dim(array, value, index, 0)]
    ppermute x36 -> x27, waiting for transfers between devices: 156 us -> 191 us  [ring_outer(): return lax.ppermute(value, 'ep', [(i, (i + 2) % size) for i in range(size)])]
    ppermute x48 -> x36, starting transfers between devices: 60.2 us -> 37.4 us  [swap_inner(): return lax.ppermute(value, 'ep', [(i, i ^ 1) for i in range(size)])]
    slice x2 -> x11, local copies, waits for them, and re-layouts: 4.43 us -> 23.7 us  [the longest x5 19.2 us: from_hidden(): return scatter_tp(lambda j: jnp.stack([array[j] for array in parts]))]
    unnamed x224 -> x198, local copies, waits for them, and re-layouts: 24.5 us -> 10.6 us
  transfers between devices with their start and end apart: 137 -> 98, of which waited for: 60 -> 40; matrix products, arithmetic and copies ran while one was open for 40% -> 41% of each run, Pallas kernels for 0% -> 0%
where the time goes in v2:
time: 776 us; the launch traced here: 769 us
  waiting for transfers between devices  312 us (40%)
  local copies, waits for them, and re-layouts  163 us (21%)
  matrix products  126 us (16%)
  starting transfers between devices  84.9 us (11%)
  other arithmetic  79.1 us (10%)
    ppermute x27, waiting for transfers between devices, ring_outer(): return lax.ppermute(value, 'ep', [(i, (i + 2) % size) for i in range(size)])  191 us
    ppermute x36, waiting for transfers between devices, swap_inner(): return lax.ppermute(value, 'ep', [(i, i ^ 1) for i in range(size)])  62.8 us
    ppermute x33, waiting for transfers between devices, swap_tp(): return lax.ppermute(value, 'tp', [(i, i ^ mask) for i in range(size)])  58.1 us
    dot_general x16, matrix products, nt(): lax.dot_general(left, right, (((1,), (1,)), ((), ())), preferred_element_...  45.1 us
    dot_general x16, matrix products, nn(): lax.dot_general(left, right, (((1,), (0,)), ((), ())), preferred_element_...  44.7 us
    scatter x24, local copies, waits for them, and re-layouts, stack_static(): whole = whole.at[i].set(block)  40.7 us
    ppermute x36, starting transfers between devices, swap_inner(): return lax.ppermute(value, 'ep', [(i, i ^ 1) for i in range(size)])  37.4 us
    dot_general x16, matrix products, tn(): lax.dot_general(left, right, (((0,), (0,)), ((), ())), preferred_element_...  36.6 us
  transfers between devices with their start and end apart: 98, of which 40 were waited for; matrix products, arithmetic and copies ran while one was open for 41% of the time, Pallas kernels for 0%

profile of v2, /device:TPU:0, one launch (start us, length us, event | category | flops | bytes accessed | tf_op | source)
XLA Modules:
  0.0 769.0 jit_solution(6453263888214387458)
XLA Ops:
  10.7 5.1 pad_maximum_fusion
  23.8 7.7 scatter.106
  46.3 16.9 %collective-permute-done.3 = bf16[256,1664]{1,0:T(8,128)(2,1)S(1)} collective-permute-done((bf16[256,1664]{1,0:T(8,128)(2,1)}, bf16[256,1664]{1,0:T(8,128)(2,1)S(1)}, u32[]{:S(2)}, u32[]{:S(2)}) %collective-permute-start.3) | collective-permute-done | bytes 852000 | tf_op jit(solution)/shard_map/ppermute | solution.py:43
  66.7 19.5 %collective-permute-done.5 = bf16[256,1664]{1,0:T(8,128)(2,1)S(1)} collective-permute-done((bf16[256,1664]{1,0:T(8,128)(2,1)S(1)}, bf16[256,1664]{1,0:T(8,128)(2,1)S(1)}, u32[]{:S(2)}, u32[]{:S(2)}) %collective-permute-start.5) | collective-permute-done | bytes 852000 | tf_op jit(solution)/shard_map/ppermute | solution.py:43
  97.8 6.7 collective-permute-done.10
  105.0 14.0 %collective-permute-done.9 = bf16[256,512]{0,1:T(8,128)(2,1)S(1)} collective-permute-done((bf16[256,512]{0,1:T(8,128)(2,1)S(1)}, bf16[256,512]{0,1:T(8,128)(2,1)S(1)}, u32[]{:S(2)}, u32[]{:S(2)}) %collective-permute-start.9) | collective-permute-done | bytes 262176 | tf_op jit(solution)/shard_map/ppermute | solution.py:38
  145.1 6.0 convolution_convert_fusion.5
  155.4 5.5 collective-permute-done.13
  177.2 4.9 bitcast_dynamic-update-slice_fusion.2
  182.1 4.9 bitcast_dynamic-update-slice_fusion.1
  193.2 9.8 %collective-permute-done.18 = bf16[96,2048]{1,0:T(8,128)(2,1)S(1)} collective-permute-done((bf16[96,2048]{1,0:T(8,128)(2,1)S(1)}, bf16[96,2048]{1,0:T(8,128)(2,1)S(1)}, u32[]{:S(2)}, u32[]{:S(2)}) %collective-permute-start.18) | collective-permute-done | bytes 393248 | tf_op jit(solution)/shard_map/ppermute | solution.py:43
  204.8 11.1 %collective-permute-done.20 = bf16[96,2048]{1,0:T(8,128)(2,1)S(1)} collective-permute-done((bf16[96,2048]{1,0:T(8,128)(2,1)S(1)}, bf16[96,2048]{1,0:T(8,128)(2,1)S(1)}, u32[]{:S(2)}, u32[]{:S(2)}) %collective-permute-start.20) | collective-permute-done | bytes 393248 | tf_op jit(solution)/shard_map/ppermute | solution.py:43
  216.6 10.3 %collective-permute-done.22 = bf16[96,2048]{1,0:T(8,128)(2,1)S(1)} collective-permute-done((bf16[96,2048]{1,0:T(8,128)(2,1)S(1)}, bf16[96,2048]{1,0:T(8,128)(2,1)S(1)}, u32[]{:S(2)}, u32[]{:S(2)}) %collective-permute-start.22) | collective-permute-done | bytes 393248 | tf_op jit(solution)/shard_map/ppermute | solution.py:43
  231.1 12.0 %collective-permute-done.23 = bf16[96,2048]{1,0:T(8,128)(2,1)S(1)} collective-permute-done((bf16[96,2048]{1,0:T(8,128)(2,1)S(1)}, bf16[96,2048]{1,0:T(8,128)(2,1)S(1)}, u32[]{:S(2)}, u32[]{:S(2)}) %collective-permute-start.23) | collective-permute-done | bytes 393248 | tf_op jit(solution)/shard_map/ppermute | solution.py:38
  249.0 6.5 collective-permute-done.27
  258.7 8.0 %collective-permute-done.29 = bf16[96,2048]{1,0:T(8,128)(2,1)S(1)} collective-permute-done((bf16[96,2048]{1,0:T(8,128)(2,1)S(1)}, bf16[96,2048]{1,0:T(8,128)(2,1)S(1)}, u32[]{:S(2)}, u32[]{:S(2)}) %collective-permute-start.29) | collective-permute-done | bytes 393248 | tf_op jit(solution)/shard_map/ppermute | solution.py:43
  287.6 6.1 bitcast_dynamic-update-slice_fusion
  293.7 9.6 %fusion.129 = (bf16[1,4,352,2048]{3,2,0,1:T(8,128)(2,1)S(1)}, bf16[1,4,352,2048]{3,2,0,1:T(8,128)(2,1)S(1)}, bf16[1,4,352,2048]{3,2,0,1:T(8,128)(2,1)}) fusion(bf16[3,4,352,2048]{3,2,0,1:T(8,128)(2,1)} %bitcast.396), kind=kLoop, calls=%fused_computation.355 | loop fusion | bytes 34603008 | tf_op jit(solution)/shard_map/unstack | solution.py:314
  303.2 6.6 fusion.143
  309.9 6.7 fusion.146
  316.6 12.7 %multiply_convert_fusion.1 = (bf16[768,1408]{1,0:T(8,128)(2,1)}, bf16[768,1408]{1,0:T(8,128)(2,1)}, bf16[768,1408]{1,0:T(8,128)(2,1)}) fusion(f32[768,1408]{1,0:T(8,128)} %fusion.143, f32[768,1408]{1,0:T(8,128)} %fusion.146, f32[768]{0:T(1024)S(1)} %copy-done.82, bf16[768,2048]{1,0:T(8,128)(2,1)S(1)} %bitcast.399, bf16[1408,2048]{1,0:T(8,128)(2,1)} %bitcast.428), kind=kOutput, calls=%fused_computation.20 | convolution fusion | flops 4448649216 | bytes 24054784 | tf_op jit(solution)/shard_map/dot_general | solution.py:17
  329.5 9.5 %fusion.147 = f32[768,2048]{1,0:T(8,128)} fusion(bf16[768,1408]{1,0:T(8,128)(2,1)} %get-tuple-element.470, bf16[1408,2048]{1,0:T(8,128)(2,1)} %bitcast.431), kind=kOutput, calls=%fused_computation.373 | convolution fusion | flops 4429185024 | bytes 14221312 | tf_op jit(solution)/shard_map/dot_general | solution.py:13
  358.6 11.1 %add_convert_fusion.2 = bf16[768,2048]{1,0:T(8,128)(2,1)} fusion(f32[768,2048]{1,0:T(8,128)S(1)} %fusion.149, f32[768,2048]{1,0:T(8,128)S(1)} %fusion.148, f32[768,2048]{1,0:T(8,128)} %fusion.147, bf16[768,1408]{1,0:T(8,128)(2,1)} %get-tuple-element.468, bf16[1408,2048]{1,0:T(8,128)(2,1)} %bitcast.429, f32[2048]{0:T(1024)S(1)} %bitcast.463, f32[768]{0:T(1024)S(1)} %fusion.114), kind=kOutput, calls=%fused_computation.7 | convolution fusion | flops 4438622208 | bytes 29961216 | tf_op jit(solution)/shard_map/dot_general | solution.py:13
  375.6 5.2 add_convert_fusion.1
  380.9 6.6 fusion.153
  387.5 6.7 fusion.152
  399.9 9.7 %collective-permute-done.41 = bf16[96,2048]{1,0:T(8,128)(2,1)S(1)} collective-permute-done((bf16[96,2048]{1,0:T(8,128)(2,1)S(1)}, bf16[96,2048]{1,0:T(8,128)(2,1)S(1)}, u32[]{:S(2)}, u32[]{:S(2)}) %collective-permute-start.41) | collective-permute-done | bytes 393248 | tf_op jit(solution)/shard_map/ppermute | solution.py:43
  412.7 9.1 %collective-permute-done.42 = bf16[96,2048]{1,0:T(8,128)(2,1)S(1)} collective-permute-done((bf16[96,2048]{1,0:T(8,128)(2,1)S(1)}, bf16[96,2048]{1,0:T(8,128)(2,1)S(1)}, u32[]{:S(2)}, u32[]{:S(2)}) %collective-permute-start.42) | collective-permute-done | bytes 393248 | tf_op jit(solution)/shard_map/ppermute | solution.py:43
  425.2 7.9 %collective-permute-done.43 = bf16[96,2048]{1,0:T(8,128)(2,1)S(1)} collective-permute-done((bf16[96,2048]{1,0:T(8,128)(2,1)S(1)}, bf16[96,2048]{1,0:T(8,128)(2,1)S(1)}, u32[]{:S(2)}, u32[]{:S(2)}) %collective-permute-start.43) | collective-permute-done | bytes 393248 | tf_op jit(solution)/shard_map/ppermute | solution.py:43
  445.1 6.6 fusion.151
  461.1 5.3 collective-permute-done.49
  472.6 5.0 collective-permute-done.50
  493.2 8.1 %collective-permute-done.95 = f32[3]{0:T(128)S(1)} collective-permute-done((f32[3]{0:T(128)S(1)}, f32[3]{0:T(128)S(1)}, u32[]{:S(2)}, u32[]{:S(2)}) %collective-permute-start.95) | collective-permute-done | bytes 44 | tf_op jit(solution)/shard_map/ppermute | solution.py:48
  517.9 5.9 fusion.6
  533.1 5.8 convolution_convert_fusion
  541.4 7.7 collective-permute-done.72
  555.6 5.6 all-to-all-start.1
  561.2 5.6 slice_bitcast_fusion.11
  569.8 5.5 slice_bitcast_fusion.12
  591.1 8.6 %collective-permute-done.67 = bf16[256]{0:T(256)(128)(2,1)S(1)} collective-permute-done((bf16[256]{0:T(256)(128)(2,1)S(1)}, bf16[256]{0:T(256)(128)(2,1)S(1)}, u32[]{:S(2)}, u32[]{:S(2)}) %collective-permute-start.67) | collective-permute-done | bytes 544 | tf_op jit(solution)/shard_map/ppermute | solution.py:43
  599.7 9.8 %collective-permute-start.68 = (bf16[256]{0:T(256)(128)(2,1)S(1)}, bf16[256]{0:T(256)(128)(2,1)S(1)}, u32[]{:S(2)}, u32[]{:S(2)}) collective-permute-start(bf16[256]{0:T(256)(128)(2,1)S(1)} %add_convert_fusion.11), channel_id=1, source_target_pairs={{0,8},{4,12},{8,16},{12,20},{16,24},{20,28},{24,0},{28,4},{1,9},{5... | collective-permute-start | bytes 1544 | tf_op jit(solution)/shard_map/ppermute | solution.py:43
  630.4 5.2 collective-permute-done.61
  635.7 5.1 collective-permute-done.78
  647.8 13.5 %collective-permute-done.79 = bf16[256,1536]{1,0:T(8,128)(2,1)S(1)} collective-permute-done((bf16[256,1536]{1,0:T(8,128)(2,1)S(1)}, bf16[256,1536]{1,0:T(8,128)(2,1)S(1)}, u32[]{:S(2)}, u32[]{:S(2)}) %collective-permute-start.79) | collective-permute-done | bytes 786464 | tf_op jit(solution)/shard_map/ppermute | solution.py:38
  666.9 14.8 %collective-permute-done.83 = bf16[256,1536]{1,0:T(8,128)(2,1)S(1)} collective-permute-done((bf16[256,1536]{1,0:T(8,128)(2,1)S(1)}, bf16[256,1536]{1,0:T(8,128)(2,1)S(1)}, u32[]{:S(2)}, u32[]{:S(2)}) %collective-permute-start.83) | collective-permute-done | bytes 786464 | tf_op jit(solution)/shard_map/ppermute | solution.py:43
  685.5 16.1 %collective-permute-done.84 = bf16[256,1536]{1,0:T(8,128)(2,1)S(1)} collective-permute-done((bf16[256,1536]{1,0:T(8,128)(2,1)S(1)}, bf16[256,1536]{1,0:T(8,128)(2,1)S(1)}, u32[]{:S(2)}, u32[]{:S(2)}) %collective-permute-start.84) | collective-permute-done | bytes 786464 | tf_op jit(solution)/shard_map/ppermute | solution.py:43
  710.9 10.6 %collective-permute-done.85 = bf16[256,1536]{1,0:T(8,128)(2,1)} collective-permute-done((bf16[256,1536]{1,0:T(8,128)(2,1)}, bf16[256,1536]{1,0:T(8,128)(2,1)}, u32[]{:S(2)}, u32[]{:S(2)}) %collective-permute-start.85) | collective-permute-done | bytes 786464 | tf_op jit(solution)/shard_map/ppermute | solution.py:43
  724.6 35.9 %collective-permute-done.93 = bf16[3,352,2048]{2,1,0:T(8,128)(2,1)} collective-permute-done((bf16[3,352,2048]{2,1,0:T(8,128)(2,1)}, bf16[3,352,2048]{2,1,0:T(8,128)(2,1)}, u32[]{:S(2)}, u32[]{:S(2)}) %collective-permute-start.93) | collective-permute-done | bytes 4325408 | tf_op jit(solution)/shard_map/ppermute | solution.py:48
  (589 shorter events, 328.0 us)
Async XLA Ops:
  6.1 35.8 %collective-permute-start = (bf16[256,1664]{1,0:T(8,128)(2,1)}, bf16[256,1664]{1,0:T(8,128)(2,1)}, u32[]{:S(2)}, u32[]{:S(2)}) collective-permute-start(bf16[256,1664]{1,0:T(8,128)(2,1)} %fusion.41), channel_id=1, source_target_pairs={{0,4},{4,0},{8,12},{12,8},{16,20},{20,16},{24,28},{28,24},{1,5},{5... | collective-permute-start | bytes 2555912 | tf_op jit(solution)/shard_map/ppermute | solution.py:38
  9.1 30.7 %collective-permute-start.1 = (bf16[256,1664]{1,0:T(8,128)(2,1)}, bf16[256,1664]{1,0:T(8,128)(2,1)}, u32[]{:S(2)}, u32[]{:S(2)}) collective-permute-start(bf16[256,1664]{1,0:T(8,128)(2,1)} %fusion.41), channel_id=1, source_target_pairs={{0,8},{4,12},{8,16},{12,20},{16,24},{20,28},{24,0},{28,4},{1,9},{5... | collective-permute-start | bytes 2555912 | tf_op jit(solution)/shard_map/ppermute | solution.py:43
  15.8 161.4 %collective-permute-start.31 = (bf16[3,352,2048]{2,1,0:T(8,128)(2,1)}, bf16[3,352,2048]{2,1,0:T(8,128)(2,1)}, u32[]{:S(2)}, u32[]{:S(2)}) collective-permute-start(bf16[3,352,2048]{2,1,0:T(8,128)(2,1)} %get-tuple-element.497), channel_id=1, source_target_pairs={{0,1},{1,0},{2,3},{3,2},{4,5},{5,4},{6,7},{7,6},{8,9},{9,8},{10,11... | collective-permute-start | bytes 12976136 | tf_op jit(solution)/shard_map/ppermute | solution.py:48
  15.8 161.3 %collective-permute-start.32 = (bf16[3,352,2048]{2,1,0:T(8,128)(2,1)}, bf16[3,352,2048]{2,1,0:T(8,128)(2,1)}, u32[]{:S(2)}, u32[]{:S(2)}) collective-permute-start(bf16[3,352,2048]{2,1,0:T(8,128)(2,1)} %get-tuple-element.497), channel_id=1, source_target_pairs={{0,2},{1,3},{2,0},{3,1},{4,6},{5,7},{6,4},{7,5},{8,10},{9,11},{10,... | collective-permute-start | bytes 12976136 | tf_op jit(solution)/shard_map/ppermute | solution.py:48
  39.9 24.8 %collective-permute-start.2 = (bf16[256,1664]{1,0:T(8,128)(2,1)}, bf16[256,1664]{1,0:T(8,128)(2,1)S(1)}, u32[]{:S(2)}, u32[]{:S(2)}) collective-permute-start(bf16[256,1664]{1,0:T(8,128)(2,1)} %collective-permute-done.1), channel_id=1, source_target_pairs={{0,4},{4,0},{8,12},{12,8},{16,20},{20,16},{24,28},{28,24},{1,5},{5... | collective-permute-start | bytes 2555912 | tf_op jit(solution)/shard_map/ppermute | solution.py:38
  40.4 22.8 %collective-permute-start.3 = (bf16[256,1664]{1,0:T(8,128)(2,1)}, bf16[256,1664]{1,0:T(8,128)(2,1)S(1)}, u32[]{:S(2)}, u32[]{:S(2)}) collective-permute-start(bf16[256,1664]{1,0:T(8,128)(2,1)} %collective-permute-done.1), channel_id=1, source_target_pairs={{0,8},{4,12},{8,16},{12,20},{16,24},{20,28},{24,0},{28,4},{1,9},{5... | collective-permute-start | bytes 2555912 | tf_op jit(solution)/shard_map/ppermute | solution.py:43
  63.2 23.5 %collective-permute-start.4 = (bf16[256,1664]{1,0:T(8,128)(2,1)S(1)}, bf16[256,1664]{1,0:T(8,128)(2,1)S(1)}, u32[]{:S(2)}, u32[]{:S(2)}) collective-permute-start(bf16[256,1664]{1,0:T(8,128)(2,1)S(1)} %collective-permute-done.3), channel_id=1, source_target_pairs={{0,4},{4,0},{8,12},{12,8},{16,20},{20,16},{24,28},{28,24},{1,5},{5... | collective-permute-start | bytes 2555912 | tf_op jit(solution)/shard_map/ppermute | solution.py:38
  64.7 21.5 %collective-permute-start.5 = (bf16[256,1664]{1,0:T(8,128)(2,1)S(1)}, bf16[256,1664]{1,0:T(8,128)(2,1)S(1)}, u32[]{:S(2)}, u32[]{:S(2)}) collective-permute-start(bf16[256,1664]{1,0:T(8,128)(2,1)S(1)} %collective-permute-done.3), channel_id=1, source_target_pairs={{0,8},{4,12},{8,16},{12,20},{16,24},{20,28},{24,0},{28,4},{1,9},{5... | collective-permute-start | bytes 2555912 | tf_op jit(solution)/shard_map/ppermute | solution.py:43
  86.7 54.6 %collective-permute-start.6 = (bf16[256,1664]{1,0:T(8,128)(2,1)S(1)}, bf16[256,1664]{1,0:T(8,128)(2,1)}, u32[]{:S(2)}, u32[]{:S(2)}) collective-permute-start(bf16[256,1664]{1,0:T(8,128)(2,1)S(1)} %collective-permute-done.5), channel_id=1, source_target_pairs={{0,4},{4,0},{8,12},{12,8},{16,20},{20,16},{24,28},{28,24},{1,5},{5... | collective-permute-start | bytes 2555912 | tf_op jit(solution)/shard_map/ppermute | solution.py:38
  94.8 24.2 %collective-permute-start.9 = (bf16[256,512]{0,1:T(8,128)(2,1)S(1)}, bf16[256,512]{0,1:T(8,128)(2,1)S(1)}, u32[]{:S(2)}, u32[]{:S(2)}) collective-permute-start(bf16[256,512]{0,1:T(8,128)(2,1)S(1)} %collective-permute-done.8), channel_id=1, source_target_pairs={{0,4},{4,0},{8,12},{12,8},{16,20},{20,16},{24,28},{28,24},{1,5},{5... | collective-permute-start | bytes 786440 | tf_op jit(solution)/shard_map/ppermute | solution.py:38
  104.5 17.3 %collective-permute-start.11 = (bf16[256,512]{0,1:T(8,128)(2,1)S(1)}, bf16[256,512]{0,1:T(8,128)(2,1)S(1)}, u32[]{:S(2)}, u32[]{:S(2)}) collective-permute-start(bf16[256,512]{0,1:T(8,128)(2,1)S(1)} %collective-permute-done.10), channel_id=1, source_target_pairs={{0,4},{4,0},{8,12},{12,8},{16,20},{20,16},{24,28},{28,24},{1,5},{5... | collective-permute-start | bytes 786440 | tf_op jit(solution)/shard_map/ppermute | solution.py:38
  134.3 134.3 %all-to-all-start = ((bf16[3,8,176,256]{3,2,0,1:T(8,128)(2,1)}), bf16[3,8,176,256]{3,2,0,1:T(8,128)(2,1)}, u32[]{:S(2)}, u32[]{:S(2)}) async-start(bf16[3,8,176,256]{3,2,0,1:T(8,128)(2,1)} %copy.135), calls=%async_computation | async-start | bytes 4325376 | tf_op jit(solution)/shard_map/all_to_all | solution.py:280
  139.2 21.6 %collective-permute-start.13 = (bf16[256,512]{0,1:T(8,128)(2,1)}, bf16[256,512]{0,1:T(8,128)(2,1)}, u32[]{:S(2)}, u32[]{:S(2)}) collective-permute-start(bf16[256,512]{0,1:T(8,128)(2,1)} %collective-permute-done.12), channel_id=1, source_target_pairs={{0,4},{4,0},{8,12},{12,8},{16,20},{20,16},{24,28},{28,24},{1,5},{5... | collective-permute-start | bytes 786440 | tf_op jit(solution)/shard_map/ppermute | solution.py:38
  177.2 110.4 %collective-permute-start.33 = (bf16[3,352,2048]{2,1,0:T(8,128)(2,1)}, bf16[3,352,2048]{2,1,0:T(8,128)(2,1)}, u32[]{:S(2)}, u32[]{:S(2)}) collective-permute-start(bf16[3,352,2048]{2,1,0:T(8,128)(2,1)} %collective-permute-done.32), channel_id=1, source_target_pairs={{0,1},{1,0},{2,3},{3,2},{4,5},{5,4},{6,7},{7,6},{8,9},{9,8},{10,11... | collective-permute-start | bytes 12976136 | tf_op jit(solution)/shard_map/ppermute | solution.py:48
  190.3 14.5 %collective-permute-start.17 = (bf16[96,2048]{1,0:T(8,128)(2,1)S(1)}, bf16[96,2048]{1,0:T(8,128)(2,1)S(1)}, u32[]{:S(2)}, u32[]{:S(2)}) collective-permute-start(bf16[96,2048]{1,0:T(8,128)(2,1)S(1)} %multiply_convert_fusion.6), channel_id=1, source_target_pairs={{0,4},{4,0},{8,12},{12,8},{16,20},{20,16},{24,28},{28,24},{1,5},{5... | collective-permute-start | bytes 1179656 | tf_op jit(solution)/shard_map/ppermute | solution.py:38
  203.0 13.5 %collective-permute-start.19 = (bf16[96,2048]{1,0:T(8,128)(2,1)S(1)}, bf16[96,2048]{1,0:T(8,128)(2,1)S(1)}, u32[]{:S(2)}, u32[]{:S(2)}) collective-permute-start(bf16[96,2048]{1,0:T(8,128)(2,1)S(1)} %collective-permute-done.18), channel_id=1, source_target_pairs={{0,4},{4,0},{8,12},{12,8},{16,20},{20,16},{24,28},{28,24},{1,5},{5... | collective-permute-start | bytes 1179656 | tf_op jit(solution)/shard_map/ppermute | solution.py:38
  226.9 18.5 %collective-permute-start.24 = (bf16[96,2048]{1,0:T(8,128)(2,1)S(1)}, bf16[96,2048]{1,0:T(8,128)(2,1)}, u32[]{:S(2)}, u32[]{:S(2)}) collective-permute-start(bf16[96,2048]{1,0:T(8,128)(2,1)S(1)} %copy-done.47), channel_id=1, source_target_pairs={{0,4},{4,0},{8,12},{12,8},{16,20},{20,16},{24,28},{28,24},{1,5},{5... | collective-permute-start | bytes 1179656 | tf_op jit(solution)/shard_map/ppermute | solution.py:38
  228.0 16.5 %collective-permute-start.25 = (bf16[96,2048]{1,0:T(8,128)(2,1)S(1)}, bf16[96,2048]{1,0:T(8,128)(2,1)}, u32[]{:S(2)}, u32[]{:S(2)}) collective-permute-start(bf16[96,2048]{1,0:T(8,128)(2,1)S(1)} %copy-done.47), channel_id=1, source_target_pairs={{0,8},{4,12},{8,16},{12,20},{16,24},{20,28},{24,0},{28,4},{1,9},{5... | collective-permute-start | bytes 1179656 | tf_op jit(solution)/shard_map/ppermute | solution.py:43
  228.0 15.0 %collective-permute-start.23 = (bf16[96,2048]{1,0:T(8,128)(2,1)S(1)}, bf16[96,2048]{1,0:T(8,128)(2,1)S(1)}, u32[]{:S(2)}, u32[]{:S(2)}) collective-permute-start(bf16[96,2048]{1,0:T(8,128)(2,1)S(1)} %collective-permute-done.22), channel_id=1, source_target_pairs={{0,4},{4,0},{8,12},{12,8},{16,20},{20,16},{24,28},{28,24},{1,5},{5... | collective-permute-start | bytes 1179656 | tf_op jit(solution)/shard_map/ppermute | solution.py:38
  266.7 19.8 %collective-permute-start.30 = (bf16[96,2048]{1,0:T(8,128)(2,1)S(1)}, bf16[96,2048]{1,0:T(8,128)(2,1)}, u32[]{:S(2)}, u32[]{:S(2)}) collective-permute-start(bf16[96,2048]{1,0:T(8,128)(2,1)S(1)} %collective-permute-done.29), channel_id=1, source_target_pairs={{0,4},{4,0},{8,12},{12,8},{16,20},{20,16},{24,28},{28,24},{1,5},{5... | collective-permute-start | bytes 1179656 | tf_op jit(solution)/shard_map/ppermute | solution.py:38
  271.8 67.1 %collective-permute-start.34 = (bf16[3,176,2048]{2,1,0:T(8,128)(2,1)}, bf16[3,176,2048]{2,1,0:T(8,128)(2,1)}, u32[]{:S(2)}, u32[]{:S(2)}) collective-permute-start(bf16[3,176,2048]{2,1,0:T(8,128)(2,1)} %bitcast.207), channel_id=1, source_target_pairs={{0,1},{1,0},{2,3},{3,2},{4,5},{5,4},{6,7},{7,6},{8,9},{9,8},{10,11... | collective-permute-start | bytes 6488072 | tf_op jit(solution)/shard_map/ppermute | solution.py:48
  271.8 57.4 %collective-permute-start.35 = (bf16[3,176,2048]{2,1,0:T(8,128)(2,1)}, bf16[3,176,2048]{2,1,0:T(8,128)(2,1)}, u32[]{:S(2)}, u32[]{:S(2)}) collective-permute-start(bf16[3,176,2048]{2,1,0:T(8,128)(2,1)} %bitcast.207), channel_id=1, source_target_pairs={{0,2},{1,3},{2,0},{3,1},{4,6},{5,7},{6,4},{7,5},{8,10},{9,11},{10,... | collective-permute-start | bytes 6488072 | tf_op jit(solution)/shard_map/ppermute | solution.py:48
  374.1 22.5 %collective-permute-start.37 = (bf16[96,2048]{1,0:T(8,128)(2,1)S(1)}, bf16[96,2048]{1,0:T(8,128)(2,1)S(1)}, u32[]{:S(2)}, u32[]{:S(2)}) collective-permute-start(bf16[96,2048]{1,0:T(8,128)(2,1)S(1)} %get-tuple-element.505), channel_id=1, source_target_pairs={{0,4},{4,0},{8,12},{12,8},{16,20},{20,16},{24,28},{28,24},{1,5},{5... | collective-permute-start | bytes 1179656 | tf_op jit(solution)/shard_map/ppermute | solution.py:38
  438.8 30.0 %collective-permute-start.89 = (bf16[3,176,2048]{2,1,0:T(8,128)(2,1)}, bf16[3,176,2048]{2,1,0:T(8,128)(2,1)}, u32[]{:S(2)}, u32[]{:S(2)}) collective-permute-start(bf16[3,176,2048]{2,1,0:T(8,128)(2,1)} %pad_maximum_fusion.5), channel_id=1, source_target_pairs={{0,1},{1,0},{2,3},{3,2},{4,5},{5,4},{6,7},{7,6},{8,9},{9,8},{10,11... | collective-permute-start | bytes 6488072 | tf_op jit(solution)/shard_map/ppermute | solution.py:48
  461.1 88.8 %collective-permute-start.88 = (bf16[3,176,2048]{2,1,0:T(8,128)(2,1)}, bf16[3,176,2048]{2,1,0:T(8,128)(2,1)}, u32[]{:S(2)}, u32[]{:S(2)}) collective-permute-start(bf16[3,176,2048]{2,1,0:T(8,128)(2,1)} %pad_maximum_fusion.4), channel_id=1, source_target_pairs={{0,1},{1,0},{2,3},{3,2},{4,5},{5,4},{6,7},{7,6},{8,9},{9,8},{10,11... | collective-permute-start | bytes 6488072 | tf_op jit(solution)/shard_map/ppermute | solution.py:48
  481.0 21.1 %collective-permute-start.51 = (bf16[96,2048]{1,0:T(8,128)(2,1)}, bf16[96,2048]{1,0:T(8,128)(2,1)}, u32[]{:S(2)}, u32[]{:S(2)}) collective-permute-start(bf16[96,2048]{1,0:T(8,128)(2,1)} %get-tuple-element.460), channel_id=1, source_target_pairs={{0,1},{1,0},{2,3},{3,2},{4,5},{5,4},{6,7},{7,6},{8,9},{9,8},{10,11... | collective-permute-start | bytes 1179656 | tf_op jit(solution)/shard_map/ppermute | solution.py:48
  481.0 21.1 %collective-permute-start.52 = (bf16[96,2048]{1,0:T(8,128)(2,1)}, bf16[96,2048]{1,0:T(8,128)(2,1)}, u32[]{:S(2)}, u32[]{:S(2)}) collective-permute-start(bf16[96,2048]{1,0:T(8,128)(2,1)} %get-tuple-element.460), channel_id=1, source_target_pairs={{0,2},{1,3},{2,0},{3,1},{4,6},{5,7},{6,4},{7,5},{8,10},{9,11},{10,... | collective-permute-start | bytes 1179656 | tf_op jit(solution)/shard_map/ppermute | solution.py:48
  485.8 16.9 %collective-permute-start.55 = (bf16[96,2048]{1,0:T(8,128)(2,1)S(1)}, bf16[96,2048]{1,0:T(8,128)(2,1)}, u32[]{:S(2)}, u32[]{:S(2)}) collective-permute-start(bf16[96,2048]{1,0:T(8,128)(2,1)S(1)} %get-tuple-element.457), channel_id=1, source_target_pairs={{0,2},{1,3},{2,0},{3,1},{4,6},{5,7},{6,4},{7,5},{8,10},{9,11},{10,... | collective-permute-start | bytes 1179656 | tf_op jit(solution)/shard_map/ppermute | solution.py:48
  501.3 49.6 %collective-permute-start.90 = (bf16[3,176,2048]{2,1,0:T(8,128)(2,1)}, bf16[3,176,2048]{2,1,0:T(8,128)(2,1)}, u32[]{:S(2)}, u32[]{:S(2)}) collective-permute-start(bf16[3,176,2048]{2,1,0:T(8,128)(2,1)} %add_convert_fusion.3), channel_id=1, source_target_pairs={{0,2},{1,3},{2,0},{3,1},{4,6},{5,7},{6,4},{7,5},{8,10},{9,11},{10,... | collective-permute-start | bytes 6488072 | tf_op jit(solution)/shard_map/ppermute | solution.py:48
  502.1 36.8 %collective-permute-start.53 = (bf16[96,2048]{1,0:T(8,128)(2,1)}, bf16[96,2048]{1,0:T(8,128)(2,1)}, u32[]{:S(2)}, u32[]{:S(2)}) collective-permute-start(bf16[96,2048]{1,0:T(8,128)(2,1)} %collective-permute-done.52), channel_id=1, source_target_pairs={{0,1},{1,0},{2,3},{3,2},{4,5},{5,4},{6,7},{7,6},{8,9},{9,8},{10,11... | collective-permute-start | bytes 1179656 | tf_op jit(solution)/shard_map/ppermute | solution.py:48
  524.8 42.0 %collective-permute-start.58 = (bf16[96,2048]{1,0:T(8,128)(2,1)}, bf16[96,2048]{1,0:T(8,128)(2,1)}, u32[]{:S(2)}, u32[]{:S(2)}) collective-permute-start(bf16[96,2048]{1,0:T(8,128)(2,1)} %get-tuple-element.533), channel_id=1, source_target_pairs={{0,1},{1,0},{2,3},{3,2},{4,5},{5,4},{6,7},{7,6},{8,9},{9,8},{10,11... | collective-permute-start | bytes 1179656 | tf_op jit(solution)/shard_map/ppermute | solution.py:48
  525.3 50.0 %collective-permute-start.57 = (bf16[96,2048]{1,0:T(8,128)(2,1)}, bf16[96,2048]{1,0:T(8,128)(2,1)}, u32[]{:S(2)}, u32[]{:S(2)}) collective-permute-start(bf16[96,2048]{1,0:T(8,128)(2,1)} %get-tuple-element.532), channel_id=1, source_target_pairs={{0,1},{1,0},{2,3},{3,2},{4,5},{5,4},{6,7},{7,6},{8,9},{9,8},{10,11... | collective-permute-start | bytes 1179656 | tf_op jit(solution)/shard_map/ppermute | solution.py:48
  549.9 66.5 %collective-permute-start.76 = (bf16[256,640]{0,1:T(8,128)(2,1)}, bf16[256,640]{0,1:T(8,128)(2,1)}, u32[]{:S(2)}, u32[]{:S(2)}) collective-permute-start(bf16[256,640]{0,1:T(8,128)(2,1)} %fusion.53), channel_id=1, source_target_pairs={{0,8},{4,12},{8,16},{12,20},{16,24},{20,28},{24,0},{28,4},{1,9},{5... | collective-permute-start | bytes 983048 | tf_op jit(solution)/shard_map/ppermute | solution.py:43
  549.9 66.5 %collective-permute-start.73 = (bf16[256,640]{0,1:T(8,128)(2,1)}, bf16[256,640]{0,1:T(8,128)(2,1)}, u32[]{:S(2)}, u32[]{:S(2)}) collective-permute-start(bf16[256,640]{0,1:T(8,128)(2,1)} %get-tuple-element.349), channel_id=1, source_target_pairs={{0,4},{4,0},{8,12},{12,8},{16,20},{20,16},{24,28},{28,24},{1,5},{5... | collective-permute-start | bytes 983048 | tf_op jit(solution)/shard_map/ppermute | solution.py:38
  555.6 148.0 %all-to-all-start.1 = ((bf16[3,8,176,256]{3,2,0,1:T(8,128)(2,1)}), bf16[3,8,176,256]{3,2,0,1:T(8,128)(2,1)}, u32[]{:S(2)}, u32[]{:S(2)}) async-start(bf16[3,8,176,256]{3,2,0,1:T(8,128)(2,1)} %bitcast.413), calls=%async_computation.1 | async-start | bytes 4325376 | tf_op jit(solution)/shard_map/all_to_all | solution.py:339
  583.3 16.3 %collective-permute-start.67 = (bf16[256]{0:T(256)(128)(2,1)S(1)}, bf16[256]{0:T(256)(128)(2,1)S(1)}, u32[]{:S(2)}, u32[]{:S(2)}) collective-permute-start(bf16[256]{0:T(256)(128)(2,1)S(1)} %add_convert_fusion.12), channel_id=1, source_target_pairs={{0,8},{4,12},{8,16},{12,20},{16,24},{20,28},{24,0},{28,4},{1,9},{5... | collective-permute-start | bytes 1544 | tf_op jit(solution)/shard_map/ppermute | solution.py:43
  585.1 14.6 %collective-permute-start.64 = (bf16[256]{0:T(256)(128)(2,1)S(1)}, bf16[256]{0:T(256)(128)(2,1)S(1)}, u32[]{:S(2)}, u32[]{:S(2)}) collective-permute-start(bf16[256]{0:T(256)(128)(2,1)S(1)} %get-tuple-element.344), channel_id=1, source_target_pairs={{0,4},{4,0},{8,12},{12,8},{16,20},{20,16},{24,28},{28,24},{1,5},{5... | collective-permute-start | bytes 1544 | tf_op jit(solution)/shard_map/ppermute | solution.py:38
  611.0 52.2 %collective-permute-start.92 = (bf16[3,352,2048]{2,1,0:T(8,128)(2,1)S(1)}, bf16[3,352,2048]{2,1,0:T(8,128)(2,1)S(1)}, u32[]{:S(2)}, u32[]{:S(2)}) collective-permute-start(bf16[3,352,2048]{2,1,0:T(8,128)(2,1)S(1)} %pad_maximum_fusion.2), channel_id=1, source_target_pairs={{0,1},{1,0},{2,3},{3,2},{4,5},{5,4},{6,7},{7,6},{8,9},{9,8},{10,11... | collective-permute-start | bytes 12976136 | tf_op jit(solution)/shard_map/ppermute | solution.py:48
  628.6 96.1 %collective-permute-start.91 = (bf16[3,352,2048]{2,1,0:T(8,128)(2,1)}, bf16[3,352,2048]{2,1,0:T(8,128)(2,1)}, u32[]{:S(2)}, u32[]{:S(2)}) collective-permute-start(bf16[3,352,2048]{2,1,0:T(8,128)(2,1)} %pad_maximum_fusion.1), channel_id=1, source_target_pairs={{0,1},{1,0},{2,3},{3,2},{4,5},{5,4},{6,7},{7,6},{8,9},{9,8},{10,11... | collective-permute-start | bytes 12976136 | tf_op jit(solution)/shard_map/ppermute | solution.py:48
  635.6 47.6 %collective-permute-start.62 = (bf16[96,2048]{1,0:T(8,128)(2,1)S(1)}, bf16[96,2048]{1,0:T(8,128)(2,1)S(1)}, u32[]{:S(2)}, u32[]{:S(2)}) collective-permute-start(bf16[96,2048]{1,0:T(8,128)(2,1)S(1)} %collective-permute-done.61), channel_id=1, source_target_pairs={{0,1},{1,0},{2,3},{3,2},{4,5},{5,4},{6,7},{7,6},{8,9},{9,8},{10,11... | collective-permute-start | bytes 1179656 | tf_op jit(solution)/shard_map/ppermute | solution.py:48
  642.1 19.2 %collective-permute-start.79 = (bf16[256,1536]{1,0:T(8,128)(2,1)S(1)}, bf16[256,1536]{1,0:T(8,128)(2,1)S(1)}, u32[]{:S(2)}, u32[]{:S(2)}) collective-permute-start(bf16[256,1536]{1,0:T(8,128)(2,1)S(1)} %get-tuple-element.480), channel_id=1, source_target_pairs={{0,4},{4,0},{8,12},{12,8},{16,20},{20,16},{24,28},{28,24},{1,5},{5... | collective-permute-start | bytes 2359304 | tf_op jit(solution)/shard_map/ppermute | solution.py:38
  661.5 20.2 %collective-permute-start.83 = (bf16[256,1536]{1,0:T(8,128)(2,1)S(1)}, bf16[256,1536]{1,0:T(8,128)(2,1)S(1)}, u32[]{:S(2)}, u32[]{:S(2)}) collective-permute-start(bf16[256,1536]{1,0:T(8,128)(2,1)S(1)} %fusion.11), channel_id=1, source_target_pairs={{0,8},{4,12},{8,16},{12,20},{16,24},{20,28},{24,0},{28,4},{1,9},{5... | collective-permute-start | bytes 2359304 | tf_op jit(solution)/shard_map/ppermute | solution.py:43
  661.6 20.1 %collective-permute-start.80 = (bf16[256,1536]{1,0:T(8,128)(2,1)S(1)}, bf16[256,1536]{1,0:T(8,128)(2,1)S(1)}, u32[]{:S(2)}, u32[]{:S(2)}) collective-permute-start(bf16[256,1536]{1,0:T(8,128)(2,1)S(1)} %get-tuple-element.353), channel_id=1, source_target_pairs={{0,4},{4,0},{8,12},{12,8},{16,20},{20,16},{24,28},{28,24},{1,5},{5... | collective-permute-start | bytes 2359304 | tf_op jit(solution)/shard_map/ppermute | solution.py:38
  666.3 94.2 %collective-permute-start.93 = (bf16[3,352,2048]{2,1,0:T(8,128)(2,1)}, bf16[3,352,2048]{2,1,0:T(8,128)(2,1)}, u32[]{:S(2)}, u32[]{:S(2)}) collective-permute-start(bf16[3,352,2048]{2,1,0:T(8,128)(2,1)} %add_convert_fusion), channel_id=1, source_target_pairs={{0,2},{1,3},{2,0},{3,1},{4,6},{5,7},{6,4},{7,5},{8,10},{9,11},{10,... | collective-permute-start | bytes 12976136 | tf_op jit(solution)/shard_map/ppermute | solution.py:48
  682.0 19.5 %collective-permute-start.84 = (bf16[256,1536]{1,0:T(8,128)(2,1)S(1)}, bf16[256,1536]{1,0:T(8,128)(2,1)S(1)}, u32[]{:S(2)}, u32[]{:S(2)}) collective-permute-start(bf16[256,1536]{1,0:T(8,128)(2,1)S(1)} %fusion.13), channel_id=1, source_target_pairs={{0,8},{4,12},{8,16},{12,20},{16,24},{20,28},{24,0},{28,4},{1,9},{5... | collective-permute-start | bytes 2359304 | tf_op jit(solution)/shard_map/ppermute | solution.py:43
  682.3 19.3 %collective-permute-start.81 = (bf16[256,1536]{1,0:T(8,128)(2,1)S(1)}, bf16[256,1536]{1,0:T(8,128)(2,1)S(1)}, u32[]{:S(2)}, u32[]{:S(2)}) collective-permute-start(bf16[256,1536]{1,0:T(8,128)(2,1)S(1)} %get-tuple-element.354), channel_id=1, source_target_pairs={{0,4},{4,0},{8,12},{12,8},{16,20},{20,16},{24,28},{28,24},{1,5},{5... | collective-permute-start | bytes 2359304 | tf_op jit(solution)/shard_map/ppermute | solution.py:38
  702.7 18.7 %collective-permute-start.85 = (bf16[256,1536]{1,0:T(8,128)(2,1)}, bf16[256,1536]{1,0:T(8,128)(2,1)}, u32[]{:S(2)}, u32[]{:S(2)}) collective-permute-start(bf16[256,1536]{1,0:T(8,128)(2,1)} %fusion.15), channel_id=1, source_target_pairs={{0,8},{4,12},{8,16},{12,20},{16,24},{20,28},{24,0},{28,4},{1,9},{5... | collective-permute-start | bytes 2359304 | tf_op jit(solution)/shard_map/ppermute | solution.py:43
  702.7 18.7 %collective-permute-start.82 = (bf16[256,1536]{1,0:T(8,128)(2,1)}, bf16[256,1536]{1,0:T(8,128)(2,1)}, u32[]{:S(2)}, u32[]{:S(2)}) collective-permute-start(bf16[256,1536]{1,0:T(8,128)(2,1)} %get-tuple-element.355), channel_id=1, source_target_pairs={{0,4},{4,0},{8,12},{12,8},{16,20},{20,16},{24,28},{28,24},{1,5},{5... | collective-permute-start | bytes 2359304 | tf_op jit(solution)/shard_map/ppermute | solution.py:38
  (146 other events, 1428.3 us)

commit v3 on v2

v3 whole, which is shorter than its diff:
```python
import jax
import jax.numpy as jnp
from jax import lax
from jax.sharding import PartitionSpec as P

HD = 128
EPS = 1e-06
BF = jnp.bfloat16
F32 = jnp.float32


def nn(left, right):
    return lax.dot_general(left, right, (((1,), (0,)), ((), ())), preferred_element_type=F32)


def nt(left, right):
    return lax.dot_general(left, right, (((1,), (1,)), ((), ())), preferred_element_type=F32)


def tn(left, right):
    return lax.dot_general(left, right, (((0,), (0,)), ((), ())), preferred_element_type=F32)


def at(array, index):
    return lax.dynamic_index_in_dim(array, index, 0, keepdims=False)


def put(array, value, index):
    return lax.dynamic_update_index_in_dim(array, value, index, 0)


def after(value, *earlier):
    return lax.optimization_barrier((value,) + earlier)[0]


def swap_inner(value):
    size = lax.axis_size("ep")
    return lax.ppermute(value, "ep", [(i, i ^ 1) for i in range(size)])


def ring_outer(value):
    size = lax.axis_size("ep")
    return lax.ppermute(value, "ep", [(i, (i + 2) % size) for i in range(size)])


def swap_tp(value, mask):
    size = lax.axis_size("tp")
    return lax.ppermute(value, "tp", [(i, i ^ mask) for i in range(size)])


def relative_to_absolute():
    size = lax.axis_size("ep")
    me = lax.axis_index("ep")
    outer, inner = me // 2, me % 2
    rounds = size // 2
    return [(outer + rounds - r // 2) % rounds * 2 + (inner ^ r % 2) for r in range(size)]


def gather_ep(shard, works=()):
    rounds = lax.axis_size("ep") // 2
    blocks, done = [], []
    current = shard
    for k in range(rounds):
        other = swap_inner(current)
        following = ring_outer(current) if k < rounds - 1 else None
        if k < len(works):
            result = works[k](current)
            done.append(result)
            other = after(other, *jax.tree.leaves(result))
        blocks += [current, other]
        if following is not None:
            current = after(following, other)
    return (blocks, done + [work(other) for work in works[rounds:]]) if works else blocks


def stack_static(blocks):
    whole = jnp.zeros((len(blocks),) + blocks[0].shape, blocks[0].dtype)
    for i, block in enumerate(blocks):
        whole = whole.at[i].set(block)
    return whole


def stack_absolute(blocks):
    whole = jnp.zeros((len(blocks),) + blocks[0].shape, blocks[0].dtype)
    for block, index in zip(blocks, relative_to_absolute()):
        whole = put(whole, block, index)
    return whole


def scatter_ep(block_of, works=()):
    rounds = lax.axis_size("ep") // 2
    arrived = other = token = None
    done = []
    for step, k in enumerate(list(range(1, rounds)) + [0]):
        away = block_of(2 * k + 1).astype(BF)
        if other is not None:
            away = after(away, other)
        other = swap_inner(away)
        if step < len(works):
            result = works[step](token)
            done.append(result)
            other = after(other, *jax.tree.leaves(result))
        total = block_of(2 * k).astype(F32) + other.astype(F32)
        if arrived is not None:
            total = total + arrived.astype(F32)
        if k:
            token = total.astype(BF)
            arrived = ring_outer(token)
    done += [work(total) for work in works[rounds:]]
    return (total, done) if works else total


def scatter_absolute(parts, works=()):
    order = relative_to_absolute()
    return scatter_ep(lambda r: at(parts, order[r]), works)


TP_ORDER = (0, 2, 1, 3)


def gather_tp(shard):
    far = swap_tp(shard, 2)
    return [shard, far, swap_tp(shard, 1), swap_tp(far, 1)]


def gather_tp_rows(shard):
    me = lax.axis_index("tp")
    whole = jnp.zeros((lax.axis_size("tp"),) + shard.shape, shard.dtype)
    for j, block in zip(TP_ORDER, gather_tp(shard)):
        whole = put(whole, block, me ^ j)
    return whole.reshape(-1, shard.shape[-1])


def scatter_tp(parts):
    near = parts[0].astype(F32) + swap_tp(parts[1], 1).astype(F32)
    return near[0] + swap_tp(near[1].astype(BF), 2).astype(F32)


def scatter_tp_rows(parts):
    me = lax.axis_index("tp")
    far = at(parts, me ^ 2).astype(F32) + swap_tp(at(parts, me ^ 3).astype(BF), 1).astype(F32)
    far = swap_tp(far.astype(BF), 2)
    near = swap_tp(at(parts, me ^ 1).astype(BF), 1)
    return at(parts, me).astype(F32) + near.astype(F32) + far.astype(F32)


def sum_tp(value):
    value = value + swap_tp(value, 1)
    return value + swap_tp(value, 2)


def rms_scale(values):
    return lax.rsqrt(jnp.mean(values * values, axis=-1, keepdims=True) + EPS)


def norm_back(grad, values, scale, gain):
    weighted = grad * gain
    inner = jnp.mean(values * weighted, axis=-1, keepdims=True)
    return (scale * weighted - values * scale**3 * inner, jnp.sum(grad * values * scale, axis=0))


def gated_back(grad_hidden, gate_val, up_val):
    squash = jax.nn.sigmoid(gate_val)
    grad_gate = grad_hidden * up_val * squash * (1.0 + gate_val * (1.0 - squash))
    grad_up = grad_hidden * gate_val * squash
    return (grad_gate.astype(BF), grad_up.astype(BF))


def group_forward(act, coef, group):
    gate_val, up_val = nt(act, group[0]), nt(act, group[1])
    return gate_val, up_val, (jax.nn.silu(gate_val) * up_val * coef).astype(BF)


def group_back(gout, coef, kept, group):
    return gated_back(nt(gout, group[2]) * coef, kept[0], kept[1])


def score_of(act, logit32):
    return jax.nn.sigmoid(jnp.sum(act.astype(F32) * logit32, axis=1, keepdims=True))


def score_back(gout, score, kept, group):
    plain = jax.nn.silu(kept[0]) * kept[1]
    return score * (1.0 - score) * jnp.sum(plain * nt(gout, group[2]), axis=1, keepdims=True)


def hidden_to_rows(hidden, groups):
    return sum(nn(h, group[2]) for h, group in zip(hidden, groups)).astype(BF)


def grads_to_rows(grads, gscore, logit32, groups):
    total = sum(nn(g[0], group[0]) + nn(g[1], group[1]) for g, group in zip(grads, groups))
    return (total + gscore * logit32).astype(BF)


def expert_step(act, gout, gates, logit32, groups):
    score = score_of(act, logit32)
    coefs = [gates] * (len(groups) - 1) + [score]
    kept = [group_forward(act, c, group) for c, group in zip(coefs, groups)]
    out = hidden_to_rows([k[2] for k in kept], groups)
    grads = [group_back(gout, c, k, group) for c, k, group in zip(coefs, kept, groups)]
    gscore = score_back(gout, score, kept[-1], groups[-1])
    gact = grads_to_rows(grads, gscore, logit32, groups)
    sums = [jnp.sum(act.astype(F32) * gscore, axis=0)]
    for g, k in zip(grads, kept):
        sums += [tn(g[0], act), tn(g[1], act), tn(k[2], gout)]
    return out, gact, tuple(sums)


def experts_in_blocks(act, gout, gates, logit32, groups, steps):
    rows, width = act.shape

    def step(totals, block):
        out, gact, sums = expert_step(*block, logit32, groups)
        return tuple(t + s for t, s in zip(totals, sums)), (out, gact)

    blocks = tuple(x.reshape(steps, rows // steps, -1) for x in (act, gout, gates))
    sizes = [(width,)] + [w.shape for group in groups for w in group]
    totals = tuple(jnp.zeros(size, F32) for size in sizes)
    sums, (out, gact) = lax.scan(step, totals, blocks)
    return out.reshape(rows, width), gact.reshape(rows, width), sums[0], sums[1:]


def columns(array, head):
    return array[:, head * HD : (head + 1) * HD]


def on_device(
    tokens,
    first_gain,
    query_weight,
    key_weight,
    value_weight,
    output_weight,
    second_gain,
    shared_logit,
    shared_gate,
    shared_up,
    shared_down,
    routed_gate_weight,
    routed_up_weight,
    expert_down,
    route_ids,
    route_gates,
    piece_start,
    piece_length,
    block_grad,
):
    groups = lax.axis_size("ep")
    quarters = lax.axis_size("tp")
    me_ep = lax.axis_index("ep")
    me_tp = lax.axis_index("tp")
    count, width = tokens.shape
    part = count // quarters
    local_heads = query_weight.shape[1] // HD
    wide = local_heads * HD
    factor = HD ** (-0.5)

    def own(array):
        return lax.dynamic_slice_in_dim(array, me_tp * part, part, 0)

    dense = jnp.sum(
        own(route_gates)[:, :, None]
        * (own(route_ids)[:, :, None] == jnp.arange(groups, dtype=jnp.int32)).astype(F32),
        axis=1,
    )
    rows = query_weight.shape[0]
    high = dense.astype(BF)
    low = (dense - high.astype(F32)).astype(BF)
    packed = jnp.concatenate([high.reshape(-1), low.reshape(-1)]).reshape(-1, rows)
    spare = jnp.concatenate([jnp.stack([first_gain, second_gain, shared_logit]), packed]).T
    spare = jnp.pad(spare, ((0, 0), (0, -spare.shape[1] % 128)))
    blocks = gather_ep(
        jnp.concatenate(
            [query_weight, key_weight, value_weight, output_weight.T, spare], axis=1
        )
    )
    weights = stack_absolute(blocks)
    spare = weights[:, :, 4 * wide :]
    weights = weights.reshape(width, -1)
    w_qkv, w_out = weights[:, : 3 * wide], weights[:, 3 * wide : 4 * wide]
    vectors = spare[:, :, :3].reshape(width, 3).T.astype(F32)
    gain_one32, gain_two32, logit32 = vectors[0:1], vectors[1:2], vectors[2:3]
    packed = spare[:, :, 3 : 3 + packed.shape[0]].transpose(0, 2, 1)
    packed = packed.reshape(groups, 2, part, groups).astype(F32).sum(axis=1)
    chosen = jnp.arange(groups, dtype=jnp.int32)
    gates = jnp.sum(jnp.where(chosen == me_ep, packed, 0.0), axis=2)
    order = jnp.stack(relative_to_absolute())
    gates = jnp.sum(jnp.where((order[:, None] == chosen)[:, :, None], gates[None], 0.0), axis=1)
    gates = gates.reshape(groups * part, 1)

    def from_tp(array):
        parts = gather_tp(array)

        def joined(chosen, i):
            return stack_static([part[i] for part in chosen]).reshape(-1, width)

        return parts, joined

    routed_gate, routed_up, routed_down = lax.optimization_barrier(
        (routed_gate_weight[0], routed_up_weight[0], expert_down[0], blocks[0])
    )[:3]
    parts, joined = from_tp(jnp.stack([routed_gate.T, routed_up.T, routed_down]))
    near_group = tuple(joined(parts[:2], i) for i in range(3))
    far_group = tuple(joined(parts[2:], i) for i in range(3))

    units = shared_down.shape[0]
    piece = units // groups
    shared = jnp.stack([shared_gate.T, shared_up.T, shared_down]).reshape(3, groups, piece, -1)
    shared = lax.all_to_all(after(shared, blocks[-1]), "ep", split_axis=1, concat_axis=1, tiled=True)
    parts, joined = from_tp(shared.transpose(0, 2, 1, 3).reshape(3, piece, width))
    shared_group = tuple(joined(parts, i) for i in range(3))
    units_of = (near_group, far_group, shared_group)

    inputs32 = tokens.astype(F32)
    scale_one = rms_scale(inputs32)
    act1 = (inputs32 * scale_one * gain_one32).astype(BF)
    qkv = nn(act1, w_qkv).astype(BF)
    query, key, value = qkv[:, :wide], qkv[:, wide : 2 * wide], qkv[:, 2 * wide :]
    positions = jnp.arange(count, dtype=jnp.int32)
    start = piece_start[0]
    inside = (positions >= start) & (positions < start + piece_length[0])
    visible = (positions[None, :] <= positions[:, None]) | inside[:, None] & inside[None, :]
    all_lse, mixes = [], []
    for h in range(local_heads):
        scores = jnp.where(visible, nt(columns(query, h), columns(key, h)) * factor, -1e30)
        highest = jnp.max(scores, axis=-1, keepdims=True)
        lse = highest + jnp.log(jnp.sum(jnp.exp(scores - highest), axis=-1, keepdims=True))
        probs = jnp.exp(scores - lse).astype(BF)
        all_lse.append(lse)
        mixes.append(nn(probs, columns(value, h)).astype(BF))
    attn_mix = jnp.concatenate(mixes, axis=1)
    branch = nt(attn_mix, w_out).reshape(quarters, part, width)
    attn_branch = scatter_tp_rows(branch)

    inputs_own = own(tokens).astype(F32)
    resid = inputs_own + attn_branch
    scale_two = rms_scale(resid)
    act2 = (resid * scale_two * gain_two32).astype(BF)

    act_all = stack_static(gather_ep(act2)).reshape(groups * part, width)
    gout_own = after(own(block_grad), act_all)

    def tokens_back(block):
        return block.reshape(groups, part, width)

    def prepare_shared(total):
        total = total.astype(BF).reshape(3, piece, groups, -1).transpose(0, 2, 1, 3)
        return lax.optimization_barrier(total)

    steps = -(-groups * part // 768)
    if steps == 1:
        score = score_of(act_all, logit32)
        coefs = (gates, gates, score)
        kept, grads = [], []

        def forward(i):
            def run(token):
                kept.append(group_forward(after(act_all, token), coefs[i], units_of[i]))
                return kept[-1]

            return run

        def output(token):
            return hidden_to_rows([k[2] for k in kept], units_of)

        blocks, done = gather_ep(gout_own, [forward(0), forward(1), forward(2), output])
        gout_all = stack_static(blocks).reshape(groups * part, width)
        ffn_part = tokens_back(done[-1])

        def backward(i):
            def run(token):
                gout = gout_all if token is None else after(gout_all, token)
                grads.append(group_back(gout, coefs[i], kept[i], units_of[i]))
                if i < 2:
                    return grads[-1]
                return grads[-1], score_back(gout, score, kept[i], units_of[i])

            return run

        def rows_back(token):
            return grads_to_rows(grads, done_back[0], logit32, units_of)

        done_back = []

        def last_backward(token):
            result = backward(2)(token)
            done_back.append(result[1])
            return result

        ffn_branch, done = scatter_ep(
            lambda r: ffn_part[r], [backward(0), backward(1), last_backward, rows_back]
        )
        gscore = done_back[0]
        gact_part = after(tokens_back(done[-1]), ffn_branch)
        hidden = [k[2] for k in kept]

        def weight_grads(i, act, gout):
            return [
                tn(grads[i][0], act).astype(BF),
                tn(grads[i][1], act).astype(BF),
                tn(hidden[i], gout).astype(BF),
            ]

        state = {}

        def shared_grads_work(token):
            act, gout = lax.optimization_barrier((act_all, gout_all, gact_part))[:2]
            state["shared"] = weight_grads(2, act, gout)
            away = jnp.stack([w[2 * piece :] for w in state["shared"]])
            state["shared_got"] = swap_tp(away, 1)
            state["logit"] = jnp.sum(act.astype(F32) * gscore, axis=0)
            return away, state["logit"]

        def far_work(token):
            act, gout = lax.optimization_barrier((act_all, gout_all, token))[:2]
            away = weight_grads(1, act, gout)
            state["got"] = [swap_tp(w, 1) for w in away]
            return away

        def near_work(token):
            along_x = jnp.stack([w[piece : 2 * piece] for w in state["shared"]]).astype(F32)
            along_x = (along_x + state["shared_got"][:, piece:].astype(F32)).astype(BF)
            state["shared_x"] = swap_tp(along_x, 2)
            act = lax.optimization_barrier((act_all, token, along_x))[0]
            state["near"] = [tn(grads[0][0], act).astype(BF), tn(grads[0][1], act).astype(BF)]
            return state["near"]

        def quarter_x(i):
            rows = routed_down.shape[0]
            return (
                state["near"][i][rows:].astype(F32) + state["got"][i][rows:].astype(F32)
            ).astype(BF)

        def down_work(token):
            along_x = [quarter_x(0), quarter_x(1)]
            state["x"] = [swap_tp(a, 2) for a in along_x]
            gout = lax.optimization_barrier((gout_all, token, *along_x))[0]
            state["near"].append(tn(hidden[0], gout).astype(BF))
            return state["near"][2]

        gact2, _ = scatter_ep(
            lambda r: gact_part[r], [shared_grads_work, far_work, near_work, down_work]
        )
        along_x = quarter_x(2)
        state["x"].append(swap_tp(along_x, 2))
        logit_part = state["logit"]

        def own_grad(i):
            rows = routed_down.shape[0]
            total = state["near"][i][:rows].astype(F32) + state["got"][i][:rows].astype(F32)
            return total + state["x"][i].astype(F32)

        def shared_total():
            total = jnp.stack([w[:piece] for w in state["shared"]]).astype(F32)
            total = total + state["shared_got"][:, :piece].astype(F32)
            return prepare_shared(total + state["shared_x"].astype(F32))

        def expert_grads():
            return own_grad(0), own_grad(1), own_grad(2)

    else:
        gout_all = stack_static(gather_ep(gout_own)).reshape(groups * part, width)
        ffn_part, gact_part, logit_part, sums = experts_in_blocks(
            act_all, gout_all, gates, logit32, units_of, steps
        )
        ffn_part, gact_part = tokens_back(ffn_part), tokens_back(gact_part)
        gact2 = scatter_ep(lambda r: gact_part[r])
        ffn_branch = scatter_ep(lambda r: ffn_part[r])
        along_x = sums[0]

        def expert_grads():
            pairs = [jnp.stack([a.astype(BF), b.astype(BF)]) for a, b in zip(sums[:3], sums[3:6])]
            return [scatter_tp(pair.reshape(2, 2, -1, width)) for pair in pairs]

        def shared_total():
            parts = [w.reshape(2, 2, -1, width).astype(BF) for w in sums[6:]]
            return prepare_shared(jnp.stack([scatter_tp(w) for w in parts]))

    block_sum = resid + ffn_branch
    block_out = gather_tp_rows(block_sum.astype(BF))
    squares = jnp.stack(
        [
            jnp.sum(attn_branch * attn_branch),
            jnp.sum(ffn_branch * ffn_branch),
            jnp.sum(block_sum * block_sum),
        ]
    )
    rms_values = jnp.sqrt(sum_tp(squares) / (count * width))[None, :]

    resid_part, gain_two_part = norm_back(gact2, resid, scale_two, gain_two32)
    gresid = own(block_grad).astype(F32) + resid_part
    gattn = after(gather_tp_rows(gresid.astype(BF)), along_x)
    vectors = jnp.stack([gain_two_part, logit_part], axis=1).reshape(groups, -1, 2)
    vectors = jnp.pad(vectors, ((0, 0), (0, 0), (0, 126))).astype(BF)
    out_grads = tn(gattn, attn_mix).astype(BF).reshape(groups, -1, wide)
    gmix = nn(gattn, w_out).astype(BF)

    def head_back(h):
        def run(token):
            gmix_h = columns(gmix, h)
            if token is not None:
                gmix_h = after(gmix_h, token)
            if h == local_heads - 2:
                gmix_h = after(gmix_h, shared_grads)
            query_h, key_h = columns(query, h), columns(key, h)
            scores = jnp.where(visible, nt(query_h, key_h) * factor, -1e30)
            probs = jnp.exp(scores - all_lse[h])
            gprob = nt(gmix_h, columns(value, h))
            gvalue = tn(probs.astype(BF), gmix_h).astype(BF)
            inner = jnp.sum(probs * gprob, axis=-1, keepdims=True)
            gscores = (probs * (gprob - inner)).astype(BF)
            gquery = (nn(gscores, key_h) * factor).astype(BF)
            gkey = (tn(gscores, query_h) * factor).astype(BF)
            return gquery, gkey, gvalue

        return run

    shared_grads = shared_total()
    out_grads, heads = scatter_absolute(
        jnp.concatenate([out_grads, vectors], axis=2), [head_back(h) for h in range(local_heads)]
    )
    output_grad = out_grads[:, :wide].T
    early = sum_tp(out_grads[:, wide : wide + 2])
    gqkv = jnp.concatenate([head[i] for i in range(3) for head in heads], axis=1)
    gqkv_grad = tn(act1, gqkv).astype(BF).reshape(groups, -1, 3 * wide)
    qkv_grad = scatter_absolute(gqkv_grad)
    gact1 = nt(after(gqkv, gqkv_grad), w_qkv).astype(BF).reshape(quarters, part, width)
    gact1 = scatter_tp_rows(gact1)
    input_part, _ = norm_back(gact1, inputs_own, own(scale_one), gain_one32)
    tokens_grad = gather_tp_rows((gresid + input_part).astype(BF)).astype(F32)

    shared_grads = lax.all_to_all(shared_grads, "ep", split_axis=1, concat_axis=1, tiled=True)
    shared_grads = shared_grads.reshape(3, units, -1)
    sgate_grad = shared_grads[0].T.astype(F32)
    sup_grad = shared_grads[1].T.astype(F32)
    sdown_grad = shared_grads[2].astype(F32)
    gate_grad, up_grad, down_grad = expert_grads()

    own_qkv = jnp.concatenate([query_weight, key_weight, value_weight], axis=1).astype(F32)
    late = sum_tp(jnp.sum(own_qkv * qkv_grad, axis=1) / first_gain.astype(F32))
    return (
        block_out,
        tokens_grad,
        late,
        qkv_grad[:, :wide],
        qkv_grad[:, wide : 2 * wide],
        qkv_grad[:, 2 * wide :],
        output_grad,
        early[:, 0],
        early[:, 1],
        sgate_grad,
        sup_grad,
        sdown_grad,
        gate_grad.T[None],
        up_grad.T[None],
        down_grad[None],
        rms_values,
    )


def solution(mesh):
    in_specs = (
        P("ep", None),
        P("ep"),
        P("ep", "tp"),
        P("ep", "tp"),
        P("ep", "tp"),
        P("tp", "ep"),
        P("ep"),
        P("ep"),
        P("ep", "tp"),
        P("ep", "tp"),
        P("tp", "ep"),
        P("ep", None, "tp"),
        P("ep", None, "tp"),
        P("ep", "tp", None),
        P("ep", None),
        P("ep", None),
        P("ep"),
        P("ep"),
        P("ep", None),
    )
    out_specs = (
        P("ep", None),
        P("ep", None),
        P("ep"),
        P("ep", "tp"),
        P("ep", "tp"),
        P("ep", "tp"),
        P("tp", "ep"),
        P("ep"),
        P("ep"),
        P("ep", "tp"),
        P("ep", "tp"),
        P("tp", "ep"),
        P("ep", None, "tp"),
        P("ep", None, "tp"),
        P("ep", "tp", None),
        P("ep", None),
    )
    return jax.shard_map(
        on_device, mesh=mesh, in_specs=in_specs, out_specs=out_specs, check_vma=False
    )
```

time: 776 us -> 1250 us (1.61)
  local copies, waits for them, and re-layouts: 163 us -> 535 us
  waiting for transfers between devices: 312 us -> 368 us
  starting transfers between devices: 84.9 us -> 104 us
  matrix products: 126 us -> 140 us
    dynamic_update_slice x25 -> x18, local copies, waits for them, and re-layouts: 29.8 us -> 395 us  [put(): return lax.dynamic_update_index_in_dim(array, value, index, 0)]
    ppermute x27 -> x21, waiting for transfers between devices: 191 us -> 76.4 us  [ring_outer(): return lax.ppermute(value, 'ep', [(i, (i + 2) % size) for i in range(size)])]
    ppermute x33 -> x35, waiting for transfers between devices: 58.1 us -> 160 us  [swap_tp(): return lax.ppermute(value, 'tp', [(i, i ^ mask) for i in range(size)])]
    ppermute x36 -> x28, waiting for transfers between devices: 62.8 us -> 131 us  [swap_inner(): return lax.ppermute(value, 'ep', [(i, i ^ 1) for i in range(size)])]
    broadcast_in_dim x1 -> x8, local copies, waits for them, and re-layouts: 1.09 us -> 49.1 us  [put(): return lax.dynamic_update_index_in_dim(array, value, index, 0)]
    scatter x24 -> x22, local copies, waits for them, and re-layouts: 40.7 us -> 14.2 us  [stack_static(): whole = whole.at[i].set(block)]
    ppermute x27 -> x21, starting transfers between devices: 21 us -> 43.6 us  [ring_outer(): return lax.ppermute(value, 'ep', [(i, (i + 2) % size) for i in range(size)])]
    unnamed x198 -> x287, local copies, waits for them, and re-layouts: 10.6 us -> 28.9 us
  transfers between devices with their start and end apart: 98 -> 86, of which waited for: 40 -> 33; matrix products, arithmetic and copies ran while one was open for 41% -> 58% of each run, Pallas kernels for 0% -> 0%
where the time goes in v3:
time: 1250 us; the launch traced here: 1240 us
  local copies, waits for them, and re-layouts  535 us (43%)
  waiting for transfers between devices  368 us (29%)
  matrix products  140 us (11%)
  starting transfers between devices  104 us (8%)
  other arithmetic  85.5 us (7%)
    dynamic_update_slice x18, local copies, waits for them, and re-layouts, put(): return lax.dynamic_update_index_in_dim(array, value, index, 0)  395 us
    ppermute x35, waiting for transfers between devices, swap_tp(): return lax.ppermute(value, 'tp', [(i, i ^ mask) for i in range(size)])  160 us
    ppermute x28, waiting for transfers between devices, swap_inner(): return lax.ppermute(value, 'ep', [(i, i ^ 1) for i in range(size)])  131 us
    ppermute x21, waiting for transfers between devices, ring_outer(): return lax.ppermute(value, 'ep', [(i, (i + 2) % size) for i in range(size)])  76.4 us
    dot_general x19, matrix products, nn(): lax.dot_general(left, right, (((1,), (0,)), ((), ())), preferred_element_...  59.7 us
    broadcast_in_dim x8, local copies, waits for them, and re-layouts, put(): return lax.dynamic_update_index_in_dim(array, value, index, 0)  49.1 us
    dot_general x19, matrix products, nt(): lax.dot_general(left, right, (((1,), (1,)), ((), ())), preferred_element_...  44.1 us
    ppermute x21, starting transfers between devices, ring_outer(): return lax.ppermute(value, 'ep', [(i, (i + 2) % size) for i in range(size)])  43.6 us
  transfers between devices with their start and end apart: 86, of which 33 were waited for; matrix products, arithmetic and copies ran while one was open for 58% of the time, Pallas kernels for 0%

profile of v3, /device:TPU:0, one launch (start us, length us, event | category | flops | bytes accessed | tf_op | source)
XLA Modules:
  0.0 1237.0 jit_solution(3757584324616473762)
XLA Ops:
  21.8 23.9 %collective-permute-done = bf16[256,2176]{1,0:T(8,128)(2,1)S(1)} collective-permute-done((bf16[256,2176]{1,0:T(8,128)(2,1)S(1)}, bf16[256,2176]{1,0:T(8,128)(2,1)S(1)}, u32[]{:S(2)}, u32[]{:S(2)}) %collective-permute-start) | collective-permute-done | bytes 1114144 | tf_op jit(solution)/shard_map/ppermute | solution.py:38
  51.6 23.1 %collective-permute-done.2 = bf16[256,2176]{1,0:T(8,128)(2,1)S(1)} collective-permute-done((bf16[256,2176]{1,0:T(8,128)(2,1)S(1)}, bf16[256,2176]{1,0:T(8,128)(2,1)S(1)}, u32[]{:S(2)}, u32[]{:S(2)}) %collective-permute-start.2) | collective-permute-done | bytes 1114144 | tf_op jit(solution)/shard_map/ppermute | solution.py:38
  82.6 6.5 copy.377
  94.2 47.1 %dynamic_update_slice.62 = bf16[8,256,2176]{1,0,2:T(8,128)(2,1)} dynamic-update-slice(bf16[8,256,2176]{1,0,2:T(8,128)(2,1)} %broadcast_in_dim.145, bf16[1,256,2176]{1,0,2:T(2,128)(2,1)S(1)} %copy.377, s32[]{:T(128)S(6)} %select_n.203, s32[]{:T(128)} %constant.1122.clone.1, s32[]{:T(128)} %constant.1122.clone.1) | dynamic-update-slice | bytes 2228228 | tf_op jit(solution)/shard_map/jit(dynamic_update_index_in_dim)/dynamic_update_slice | solution.py:29
  146.6 6.0 copy.378
  152.7 6.1 copy.379
  158.8 47.1 %dynamic_update_slice.63 = bf16[8,256,2176]{1,0,2:T(8,128)(2,1)} dynamic-update-slice(bf16[8,256,2176]{1,0,2:T(8,128)(2,1)} %dynamic_update_slice.62, bf16[1,256,2176]{1,0,2:T(2,128)(2,1)S(1)} %copy.378, s32[]{:T(128)S(6)} %select_n.204, s32[]{:T(128)} %constant.1122.clone.1, s32[]{:T(128)} %constant.1122.clone.1) | dynamic-update-slice | bytes 2228228 | tf_op jit(solution)/shard_map/jit(dynamic_update_index_in_dim)/dynamic_update_slice | solution.py:29
  205.9 47.3 %dynamic_update_slice.64 = bf16[8,256,2176]{1,0,2:T(8,128)(2,1)} dynamic-update-slice(bf16[8,256,2176]{1,0,2:T(8,128)(2,1)} %dynamic_update_slice.63, bf16[1,256,2176]{1,0,2:T(2,128)(2,1)} %copy.379, s32[]{:T(128)S(6)} %select_n.206, s32[]{:T(128)} %constant.1122.clone.1, s32[]{:T(128)} %constant.1122.clone.1) | dynamic-update-slice | bytes 2228228 | tf_op jit(solution)/shard_map/jit(dynamic_update_index_in_dim)/dynamic_update_slice | solution.py:29
  253.2 6.0 copy.380
  259.2 6.1 copy.381
  265.3 47.1 %dynamic_update_slice.65 = bf16[8,256,2176]{1,0,2:T(8,128)(2,1)} dynamic-update-slice(bf16[8,256,2176]{1,0,2:T(8,128)(2,1)} %dynamic_update_slice.64, bf16[1,256,2176]{1,0,2:T(2,128)(2,1)S(1)} %copy.380, s32[]{:T(128)S(6)} %select_n.207, s32[]{:T(128)} %constant.1122.clone.1, s32[]{:T(128)} %constant.1122.clone.1) | dynamic-update-slice | bytes 2228228 | tf_op jit(solution)/shard_map/jit(dynamic_update_index_in_dim)/dynamic_update_slice | solution.py:29
  312.4 47.3 %dynamic_update_slice.66 = bf16[8,256,2176]{1,0,2:T(8,128)(2,1)} dynamic-update-slice(bf16[8,256,2176]{1,0,2:T(8,128)(2,1)} %dynamic_update_slice.65, bf16[1,256,2176]{1,0,2:T(2,128)(2,1)} %copy.381, s32[]{:T(128)S(6)} %select_n.209, s32[]{:T(128)} %constant.1122.clone.1, s32[]{:T(128)} %constant.1122.clone.1) | dynamic-update-slice | bytes 2228228 | tf_op jit(solution)/shard_map/jit(dynamic_update_index_in_dim)/dynamic_update_slice | solution.py:29
  360.3 6.0 copy.382
  366.3 6.1 copy.383
  372.4 47.1 %dynamic_update_slice.67 = bf16[8,256,2176]{1,0,2:T(8,128)(2,1)} dynamic-update-slice(bf16[8,256,2176]{1,0,2:T(8,128)(2,1)} %dynamic_update_slice.66, bf16[1,256,2176]{1,0,2:T(2,128)(2,1)S(1)} %copy.382, s32[]{:T(128)S(6)} %select_n.210, s32[]{:T(128)} %constant.1122.clone.1, s32[]{:T(128)} %constant.1122.clone.1) | dynamic-update-slice | bytes 2228228 | tf_op jit(solution)/shard_map/jit(dynamic_update_index_in_dim)/dynamic_update_slice | solution.py:29
  419.5 47.3 %dynamic_update_slice.68 = bf16[8,256,2176]{1,0,2:T(8,128)(2,1)} dynamic-update-slice(bf16[8,256,2176]{1,0,2:T(8,128)(2,1)} %dynamic_update_slice.67, bf16[1,256,2176]{1,0,2:T(2,128)(2,1)} %copy.383, s32[]{:T(128)S(6)} %select_n.212, s32[]{:T(128)} %constant.1122.clone.1, s32[]{:T(128)} %constant.1122.clone.1) | dynamic-update-slice | bytes 2228228 | tf_op jit(solution)/shard_map/jit(dynamic_update_index_in_dim)/dynamic_update_slice | solution.py:29
  478.7 6.0 copy.384
  484.7 47.1 %dynamic_update_slice.69 = bf16[8,256,2176]{1,0,2:T(8,128)(2,1)} dynamic-update-slice(bf16[8,256,2176]{1,0,2:T(8,128)(2,1)} %dynamic_update_slice.68, bf16[1,256,2176]{1,0,2:T(2,128)(2,1)S(1)} %copy.384, s32[]{:T(128)S(6)} %select_n.213, s32[]{:T(128)} %constant.1122.clone.1, s32[]{:T(128)} %constant.1122.clone.1) | dynamic-update-slice | bytes 2228228 | tf_op jit(solution)/shard_map/jit(dynamic_update_index_in_dim)/dynamic_update_slice | solution.py:29
  531.8 12.8 %copy.385 = bf16[8,256,2176]{2,1,0:T(8,128)(2,1)} copy(bf16[8,256,2176]{1,0,2:T(8,128)(2,1)} %dynamic_update_slice.69) | data formatting | bytes 17825792 | tf_op jit(solution)/shard_map/jit(dynamic_update_index_in_dim)/dynamic_update_slice | solution.py:29
  545.5 5.5 fusion.8
  568.4 6.0 all-to-all-start
  580.9 7.5 collective-permute-done.9
  595.2 16.6 %collective-permute-done.10 = bf16[96,2048]{1,0:T(8,128)(2,1)S(1)} collective-permute-done((bf16[96,2048]{1,0:T(8,128)(2,1)S(1)}, bf16[96,2048]{1,0:T(8,128)(2,1)S(1)}, u32[]{:S(2)}, u32[]{:S(2)}) %collective-permute-start.10) | collective-permute-done | bytes 393248 | tf_op jit(solution)/shard_map/ppermute | solution.py:38
  611.8 10.9 collective-permute-done.11
  624.2 9.1 collective-permute-start.13
  634.7 7.0 collective-permute-done.13
  645.6 6.0 collective-permute-done.14
  656.0 8.6 collective-permute-done.16
  708.4 28.1 %collective-permute-done.24 = bf16[3,176,2048]{2,1,0:T(8,128)(2,1)S(1)} collective-permute-done((bf16[3,176,2048]{2,1,0:T(8,128)(2,1)}, bf16[3,176,2048]{2,1,0:T(8,128)(2,1)S(1)}, u32[]{:S(2)}, u32[]{:S(2)}) %collective-permute-start.24) | collective-permute-done | bytes 2162720 | tf_op jit(solution)/shard_map/ppermute | solution.py:48
  753.5 6.6 add_convert_fusion.1
  764.8 6.3 multiply_convert_fusion.4
  775.4 4.6 fusion.135
  784.5 5.1 multiply_convert_fusion.2
  791.0 4.5 fusion.137
  795.5 4.6 fusion.136
  804.2 5.4 multiply_reduce_fusion.2
  822.1 12.9 %add_convert_fusion = bf16[768,2048]{1,0:T(8,128)(2,1)S(1)} fusion(f32[768,2048]{1,0:T(8,128)} %fusion.138, f32[768,2048]{1,0:T(8,128)} %fusion.136, f32[768,2048]{1,0:T(8,128)} %fusion.137, f32[768,2048]{1,0:T(8,128)} %fusion.134, f32[768,2048]{1,0:T(8,128)} %fusion.135, bf16[768,704]{0,1:T(8,128)(2,1)S(1)} %get-tuple-element.847, ...), kind=kOutput, calls=%fused_computation.2 | convolution fusion | flops 2227175424 | bytes 38579200 | tf_op jit(solution)/shard_map/dot_general | solution.py:13
  860.6 7.6 collective-permute-done.40
  886.2 9.4 collective-permute-done.39
  925.3 6.5 collective-permute-done.45
  940.7 90.3 %collective-permute-done.83 = f32[3]{0:T(128)S(1)} collective-permute-done((f32[3]{0:T(128)S(1)}, f32[3]{0:T(128)S(1)}, u32[]{:S(2)}, u32[]{:S(2)}) %collective-permute-start.83) | collective-permute-done | bytes 44 | tf_op jit(solution)/shard_map/ppermute | solution.py:48
  1047.8 15.4 %collective-permute-done.81 = bf16[352,2048]{1,0:T(8,128)(2,1)} collective-permute-done((bf16[352,2048]{1,0:T(8,128)(2,1)}, bf16[352,2048]{1,0:T(8,128)(2,1)}, u32[]{:S(2)}, u32[]{:S(2)}) %collective-permute-start.81) | collective-permute-done | bytes 1441824 | tf_op jit(solution)/shard_map/ppermute | solution.py:48
  1125.0 5.4 collective-permute-done.62
  1132.2 25.9 %collective-permute-done.67 = bf16[256,1536]{1,0:T(8,128)(2,1)S(1)} collective-permute-done((bf16[256,1536]{1,0:T(8,128)(2,1)}, bf16[256,1536]{1,0:T(8,128)(2,1)S(1)}, u32[]{:S(2)}, u32[]{:S(2)}) %collective-permute-start.67) | collective-permute-done | bytes 786464 | tf_op jit(solution)/shard_map/ppermute | solution.py:38
  1158.1 13.6 %collective-permute-done.70 = bf16[256,1536]{1,0:T(8,128)(2,1)S(1)} collective-permute-done((bf16[256,1536]{1,0:T(8,128)(2,1)S(1)}, bf16[256,1536]{1,0:T(8,128)(2,1)S(1)}, u32[]{:S(2)}, u32[]{:S(2)}) %collective-permute-start.70) | collective-permute-done | bytes 786464 | tf_op jit(solution)/shard_map/ppermute | solution.py:43
  1173.1 10.3 collective-permute-start.71
  1186.2 14.2 %collective-permute-done.71 = bf16[256,1536]{1,0:T(8,128)(2,1)S(1)} collective-permute-done((bf16[256,1536]{1,0:T(8,128)(2,1)S(1)}, bf16[256,1536]{1,0:T(8,128)(2,1)S(1)}, u32[]{:S(2)}, u32[]{:S(2)}) %collective-permute-start.71) | collective-permute-done | bytes 786464 | tf_op jit(solution)/shard_map/ppermute | solution.py:43
  1205.0 18.1 %collective-permute-done.72 = bf16[256,1536]{1,0:T(8,128)(2,1)S(1)} collective-permute-done((bf16[256,1536]{1,0:T(8,128)(2,1)S(1)}, bf16[256,1536]{1,0:T(8,128)(2,1)S(1)}, u32[]{:S(2)}, u32[]{:S(2)}) %collective-permute-start.72) | collective-permute-done | bytes 786464 | tf_op jit(solution)/shard_map/ppermute | solution.py:43
  (653 shorter events, 374.4 us)
Async XLA Ops:
  15.7 451.1 %collective-permute-start.17 = (bf16[3,352,2048]{2,1,0:T(8,128)(2,1)}, bf16[3,352,2048]{2,1,0:T(8,128)(2,1)}, u32[]{:S(2)}, u32[]{:S(2)}) collective-permute-start(bf16[3,352,2048]{2,1,0:T(8,128)(2,1)} %pad_maximum_fusion), channel_id=1, source_target_pairs={{0,2},{1,3},{2,0},{3,1},{4,6},{5,7},{6,4},{7,5},{8,10},{9,11},{10,... | collective-permute-start | bytes 12976136 | tf_op jit(solution)/shard_map/ppermute | solution.py:48
  18.7 452.5 %collective-permute-start.20 = (bf16[3,352,2048]{2,1,0:T(8,128)(2,1)}, bf16[3,352,2048]{2,1,0:T(8,128)(2,1)}, u32[]{:S(2)}, u32[]{:S(2)}) collective-permute-start(bf16[3,352,2048]{2,1,0:T(8,128)(2,1)} %pad_maximum_fusion), channel_id=1, source_target_pairs={{0,1},{1,0},{2,3},{3,2},{4,5},{5,4},{6,7},{7,6},{8,9},{9,8},{10,11... | collective-permute-start | bytes 12976136 | tf_op jit(solution)/shard_map/ppermute | solution.py:48
  18.7 27.0 %collective-permute-start = (bf16[256,2176]{1,0:T(8,128)(2,1)S(1)}, bf16[256,2176]{1,0:T(8,128)(2,1)S(1)}, u32[]{:S(2)}, u32[]{:S(2)}) collective-permute-start(bf16[256,2176]{1,0:T(8,128)(2,1)S(1)} %copy-done.65), channel_id=1, source_target_pairs={{0,4},{4,0},{8,12},{12,8},{16,20},{20,16},{24,28},{28,24},{1,5},{5... | collective-permute-start | bytes 3342344 | tf_op jit(solution)/shard_map/ppermute | solution.py:38
  20.2 28.6 %collective-permute-start.1 = (bf16[256,2176]{1,0:T(8,128)(2,1)S(1)}, bf16[256,2176]{1,0:T(8,128)(2,1)S(1)}, u32[]{:S(2)}, u32[]{:S(2)}) collective-permute-start(bf16[256,2176]{1,0:T(8,128)(2,1)S(1)} %copy-done.65), channel_id=1, source_target_pairs={{0,8},{4,12},{8,16},{12,20},{16,24},{20,28},{24,0},{28,4},{1,9},{5... | collective-permute-start | bytes 3342344 | tf_op jit(solution)/shard_map/ppermute | solution.py:43
  48.8 25.9 %collective-permute-start.2 = (bf16[256,2176]{1,0:T(8,128)(2,1)S(1)}, bf16[256,2176]{1,0:T(8,128)(2,1)S(1)}, u32[]{:S(2)}, u32[]{:S(2)}) collective-permute-start(bf16[256,2176]{1,0:T(8,128)(2,1)S(1)} %collective-permute-done.1), channel_id=1, source_target_pairs={{0,4},{4,0},{8,12},{12,8},{16,20},{20,16},{24,28},{28,24},{1,5},{5... | collective-permute-start | bytes 3342344 | tf_op jit(solution)/shard_map/ppermute | solution.py:38
  49.3 27.5 %collective-permute-start.3 = (bf16[256,2176]{1,0:T(8,128)(2,1)S(1)}, bf16[256,2176]{1,0:T(8,128)(2,1)}, u32[]{:S(2)}, u32[]{:S(2)}) collective-permute-start(bf16[256,2176]{1,0:T(8,128)(2,1)S(1)} %collective-permute-done.1), channel_id=1, source_target_pairs={{0,8},{4,12},{8,16},{12,20},{16,24},{20,28},{24,0},{28,4},{1,9},{5... | collective-permute-start | bytes 3342344 | tf_op jit(solution)/shard_map/ppermute | solution.py:43
  76.8 282.9 %collective-permute-start.4 = (bf16[256,2176]{1,0:T(8,128)(2,1)}, bf16[256,2176]{1,0:T(8,128)(2,1)}, u32[]{:S(2)}, u32[]{:S(2)}) collective-permute-start(bf16[256,2176]{1,0:T(8,128)(2,1)} %collective-permute-done.3), channel_id=1, source_target_pairs={{0,4},{4,0},{8,12},{12,8},{16,20},{20,16},{24,28},{28,24},{1,5},{5... | collective-permute-start | bytes 3342344 | tf_op jit(solution)/shard_map/ppermute | solution.py:38
  78.3 281.4 %collective-permute-start.5 = (bf16[256,2176]{1,0:T(8,128)(2,1)}, bf16[256,2176]{1,0:T(8,128)(2,1)}, u32[]{:S(2)}, u32[]{:S(2)}) collective-permute-start(bf16[256,2176]{1,0:T(8,128)(2,1)} %collective-permute-done.3), channel_id=1, source_target_pairs={{0,8},{4,12},{8,16},{12,20},{16,24},{20,28},{24,0},{28,4},{1,9},{5... | collective-permute-start | bytes 3342344 | tf_op jit(solution)/shard_map/ppermute | solution.py:43
  359.7 119.0 %collective-permute-start.6 = (bf16[256,2176]{1,0:T(8,128)(2,1)}, bf16[256,2176]{1,0:T(8,128)(2,1)}, u32[]{:S(2)}, u32[]{:S(2)}) collective-permute-start(bf16[256,2176]{1,0:T(8,128)(2,1)} %collective-permute-done.5), channel_id=1, source_target_pairs={{0,4},{4,0},{8,12},{12,8},{16,20},{20,16},{24,28},{28,24},{1,5},{5... | collective-permute-start | bytes 3342344 | tf_op jit(solution)/shard_map/ppermute | solution.py:38
  466.8 228.6 %collective-permute-start.21 = (bf16[3,352,2048]{2,1,0:T(8,128)(2,1)}, bf16[3,352,2048]{2,1,0:T(8,128)(2,1)}, u32[]{:S(2)}, u32[]{:S(2)}) collective-permute-start(bf16[3,352,2048]{2,1,0:T(8,128)(2,1)} %collective-permute-done.17), channel_id=1, source_target_pairs={{0,1},{1,0},{2,3},{3,2},{4,5},{5,4},{6,7},{7,6},{8,9},{9,8},{10,11... | collective-permute-start | bytes 12976136 | tf_op jit(solution)/shard_map/ppermute | solution.py:48
  568.4 120.2 %all-to-all-start = ((bf16[3,8,176,256]{3,2,0,1:T(8,128)(2,1)}), bf16[3,8,176,256]{3,2,0,1:T(8,128)(2,1)}, u32[]{:S(2)}, u32[]{:S(2)}) async-start(bf16[3,8,176,256]{3,2,0,1:T(8,128)(2,1)} %copy.390), calls=%async_computation | async-start | bytes 4325376 | tf_op jit(solution)/shard_map/all_to_all | solution.py:310
  591.2 20.6 %collective-permute-start.10 = (bf16[96,2048]{1,0:T(8,128)(2,1)S(1)}, bf16[96,2048]{1,0:T(8,128)(2,1)S(1)}, u32[]{:S(2)}, u32[]{:S(2)}) collective-permute-start(bf16[96,2048]{1,0:T(8,128)(2,1)S(1)} %multiply_convert_fusion.9), channel_id=1, source_target_pairs={{0,4},{4,0},{8,12},{12,8},{16,20},{20,16},{24,28},{28,24},{1,5},{5... | collective-permute-start | bytes 1179656 | tf_op jit(solution)/shard_map/ppermute | solution.py:38
  593.2 29.5 %collective-permute-start.11 = (bf16[96,2048]{1,0:T(8,128)(2,1)S(1)}, bf16[96,2048]{1,0:T(8,128)(2,1)S(1)}, u32[]{:S(2)}, u32[]{:S(2)}) collective-permute-start(bf16[96,2048]{1,0:T(8,128)(2,1)S(1)} %multiply_convert_fusion.9), channel_id=1, source_target_pairs={{0,8},{4,12},{8,16},{12,20},{16,24},{20,28},{24,0},{28,4},{1,9},{5... | collective-permute-start | bytes 1179656 | tf_op jit(solution)/shard_map/ppermute | solution.py:43
  681.8 25.3 %collective-permute-start.23 = (bf16[96,2048]{1,0:T(8,128)(2,1)}, bf16[96,2048]{1,0:T(8,128)(2,1)}, u32[]{:S(2)}, u32[]{:S(2)}) collective-permute-start(bf16[96,2048]{1,0:T(8,128)(2,1)} %collective-permute-done.18), channel_id=1, source_target_pairs={{0,4},{4,0},{8,12},{12,8},{16,20},{20,16},{24,28},{28,24},{1,5},{5... | collective-permute-start | bytes 1179656 | tf_op jit(solution)/shard_map/ppermute | solution.py:38
  683.0 24.1 %collective-permute-start.22 = (bf16[96,2048]{1,0:T(8,128)(2,1)}, bf16[96,2048]{1,0:T(8,128)(2,1)S(1)}, u32[]{:S(2)}, u32[]{:S(2)}) collective-permute-start(bf16[96,2048]{1,0:T(8,128)(2,1)} %collective-permute-done.18), channel_id=1, source_target_pairs={{0,8},{4,12},{8,16},{12,20},{16,24},{20,28},{24,0},{28,4},{1,9},{5... | collective-permute-start | bytes 1179656 | tf_op jit(solution)/shard_map/ppermute | solution.py:43
  691.9 44.6 %collective-permute-start.24 = (bf16[3,176,2048]{2,1,0:T(8,128)(2,1)}, bf16[3,176,2048]{2,1,0:T(8,128)(2,1)S(1)}, u32[]{:S(2)}, u32[]{:S(2)}) collective-permute-start(bf16[3,176,2048]{2,1,0:T(8,128)(2,1)} %bitcast.181), channel_id=1, source_target_pairs={{0,2},{1,3},{2,0},{3,1},{4,6},{5,7},{6,4},{7,5},{8,10},{9,11},{10,... | collective-permute-start | bytes 6488072 | tf_op jit(solution)/shard_map/ppermute | solution.py:48
  692.4 49.5 %collective-permute-start.25 = (bf16[3,176,2048]{2,1,0:T(8,128)(2,1)}, bf16[3,176,2048]{2,1,0:T(8,128)(2,1)}, u32[]{:S(2)}, u32[]{:S(2)}) collective-permute-start(bf16[3,176,2048]{2,1,0:T(8,128)(2,1)} %bitcast.181), channel_id=1, source_target_pairs={{0,1},{1,0},{2,3},{3,2},{4,5},{5,4},{6,7},{7,6},{8,9},{9,8},{10,11... | collective-permute-start | bytes 6488072 | tf_op jit(solution)/shard_map/ppermute | solution.py:48
  707.1 44.9 %collective-permute-start.28 = (bf16[96,2048]{1,0:T(8,128)(2,1)S(1)}, bf16[96,2048]{1,0:T(8,128)(2,1)S(1)}, u32[]{:S(2)}, u32[]{:S(2)}) collective-permute-start(bf16[96,2048]{1,0:T(8,128)(2,1)S(1)} %collective-permute-done.22), channel_id=1, source_target_pairs={{0,4},{4,0},{8,12},{12,8},{16,20},{20,16},{24,28},{28,24},{1,5},{5... | collective-permute-start | bytes 1179656 | tf_op jit(solution)/shard_map/ppermute | solution.py:38
  707.8 44.2 %collective-permute-start.29 = (bf16[96,2048]{1,0:T(8,128)(2,1)S(1)}, bf16[96,2048]{1,0:T(8,128)(2,1)S(1)}, u32[]{:S(2)}, u32[]{:S(2)}) collective-permute-start(bf16[96,2048]{1,0:T(8,128)(2,1)S(1)} %collective-permute-done.22), channel_id=1, source_target_pairs={{0,8},{4,12},{8,16},{12,20},{16,24},{20,28},{24,0},{28,4},{1,9},{5... | collective-permute-start | bytes 1179656 | tf_op jit(solution)/shard_map/ppermute | solution.py:43
  774.2 25.9 %collective-permute-start.33 = (bf16[96,2048]{1,0:T(8,128)(2,1)S(1)}, bf16[96,2048]{1,0:T(8,128)(2,1)S(1)}, u32[]{:S(2)}, u32[]{:S(2)}) collective-permute-start(bf16[96,2048]{1,0:T(8,128)(2,1)S(1)} %add_convert_fusion.9), channel_id=1, source_target_pairs={{0,8},{4,12},{8,16},{12,20},{16,24},{20,28},{24,0},{28,4},{1,9},{5... | collective-permute-start | bytes 1179656 | tf_op jit(solution)/shard_map/ppermute | solution.py:43
  801.3 18.6 %collective-permute-start.35 = (bf16[96,2048]{1,0:T(8,128)(2,1)S(1)}, bf16[96,2048]{1,0:T(8,128)(2,1)S(1)}, u32[]{:S(2)}, u32[]{:S(2)}) collective-permute-start(bf16[96,2048]{1,0:T(8,128)(2,1)S(1)} %add_convert_fusion.8), channel_id=1, source_target_pairs={{0,8},{4,12},{8,16},{12,20},{16,24},{20,28},{24,0},{28,4},{1,9},{5... | collective-permute-start | bytes 1179656 | tf_op jit(solution)/shard_map/ppermute | solution.py:43
  848.5 32.9 %collective-permute-start.37 = (bf16[96,2048]{1,0:T(8,128)(2,1)}, bf16[96,2048]{1,0:T(8,128)(2,1)}, u32[]{:S(2)}, u32[]{:S(2)}) collective-permute-start(bf16[96,2048]{1,0:T(8,128)(2,1)} %get-tuple-element.840), channel_id=1, source_target_pairs={{0,2},{1,3},{2,0},{3,1},{4,6},{5,7},{6,4},{7,5},{8,10},{9,11},{10,... | collective-permute-start | bytes 1179656 | tf_op jit(solution)/shard_map/ppermute | solution.py:48
  849.0 34.3 %collective-permute-start.38 = (bf16[96,2048]{1,0:T(8,128)(2,1)}, bf16[96,2048]{1,0:T(8,128)(2,1)}, u32[]{:S(2)}, u32[]{:S(2)}) collective-permute-start(bf16[96,2048]{1,0:T(8,128)(2,1)} %get-tuple-element.840), channel_id=1, source_target_pairs={{0,1},{1,0},{2,3},{3,2},{4,5},{5,4},{6,7},{7,6},{8,9},{9,8},{10,11... | collective-permute-start | bytes 1179656 | tf_op jit(solution)/shard_map/ppermute | solution.py:48
  856.4 40.6 %collective-permute-start.44 = (bf16[3,352,2048]{2,1,0:T(8,128)(2,1)}, bf16[3,352,2048]{2,1,0:T(8,128)(2,1)}, u32[]{:S(2)}, u32[]{:S(2)}) collective-permute-start(bf16[3,352,2048]{2,1,0:T(8,128)(2,1)} %pad_maximum_fusion.1), channel_id=1, source_target_pairs={{0,1},{1,0},{2,3},{3,2},{4,5},{5,4},{6,7},{7,6},{8,9},{9,8},{10,11... | collective-permute-start | bytes 12976136 | tf_op jit(solution)/shard_map/ppermute | solution.py:48
  881.4 29.0 %collective-permute-start.48 = (bf16[704,2048]{1,0:T(8,128)(2,1)S(1)}, bf16[704,2048]{1,0:T(8,128)(2,1)S(1)}, u32[]{:S(2)}, u32[]{:S(2)}) collective-permute-start(bf16[704,2048]{1,0:T(8,128)(2,1)S(1)} %convolution_convert_fusion.5), channel_id=1, source_target_pairs={{0,1},{1,0},{2,3},{3,2},{4,5},{5,4},{6,7},{7,6},{8,9},{9,8},{10,11... | collective-permute-start | bytes 8650760 | tf_op jit(solution)/shard_map/ppermute | solution.py:48
  883.3 30.5 %collective-permute-start.47 = (bf16[704,2048]{1,0:T(8,128)(2,1)S(1)}, bf16[704,2048]{1,0:T(8,128)(2,1)S(1)}, u32[]{:S(2)}, u32[]{:S(2)}) collective-permute-start(bf16[704,2048]{1,0:T(8,128)(2,1)S(1)} %convolution_convert_fusion.6), channel_id=1, source_target_pairs={{0,1},{1,0},{2,3},{3,2},{4,5},{5,4},{6,7},{7,6},{8,9},{9,8},{10,11... | collective-permute-start | bytes 8650760 | tf_op jit(solution)/shard_map/ppermute | solution.py:48
  885.5 36.8 %collective-permute-start.53 = (bf16[704,2048]{1,0:T(8,128)(2,1)S(1)}, bf16[704,2048]{1,0:T(8,128)(2,1)S(1)}, u32[]{:S(2)}, u32[]{:S(2)}) collective-permute-start(bf16[704,2048]{1,0:T(8,128)(2,1)S(1)} %convolution_convert_fusion.4), channel_id=1, source_target_pairs={{0,1},{1,0},{2,3},{3,2},{4,5},{5,4},{6,7},{7,6},{8,9},{9,8},{10,11... | collective-permute-start | bytes 8650760 | tf_op jit(solution)/shard_map/ppermute | solution.py:48
  909.9 21.9 %collective-permute-start.49 = (bf16[96,2048]{1,0:T(8,128)(2,1)S(1)}, bf16[96,2048]{1,0:T(8,128)(2,1)S(1)}, u32[]{:S(2)}, u32[]{:S(2)}) collective-permute-start(bf16[96,2048]{1,0:T(8,128)(2,1)S(1)} %fusion.49), channel_id=1, source_target_pairs={{0,8},{4,12},{8,16},{12,20},{16,24},{20,28},{24,0},{28,4},{1,9},{5... | collective-permute-start | bytes 1179656 | tf_op jit(solution)/shard_map/ppermute | solution.py:43
  912.4 154.2 %collective-permute-start.80 = (bf16[352,2048]{1,0:T(8,128)(2,1)}, bf16[352,2048]{1,0:T(8,128)(2,1)}, u32[]{:S(2)}, u32[]{:S(2)}) collective-permute-start(bf16[352,2048]{1,0:T(8,128)(2,1)} %add_convert_fusion.5), channel_id=1, source_target_pairs={{0,2},{1,3},{2,0},{3,1},{4,6},{5,7},{6,4},{7,5},{8,10},{9,11},{10,... | collective-permute-start | bytes 4325384 | tf_op jit(solution)/shard_map/ppermute | solution.py:48
  915.9 191.5 %collective-permute-start.79 = (bf16[352,2048]{1,0:T(8,128)(2,1)}, bf16[352,2048]{1,0:T(8,128)(2,1)}, u32[]{:S(2)}, u32[]{:S(2)}) collective-permute-start(bf16[352,2048]{1,0:T(8,128)(2,1)} %add_convert_fusion.6), channel_id=1, source_target_pairs={{0,2},{1,3},{2,0},{3,1},{4,6},{5,7},{6,4},{7,5},{8,10},{9,11},{10,... | collective-permute-start | bytes 4325384 | tf_op jit(solution)/shard_map/ppermute | solution.py:48
  916.5 164.5 %collective-permute-start.57 = (bf16[3,176,2048]{2,1,0:T(8,128)(2,1)}, bf16[3,176,2048]{2,1,0:T(8,128)(2,1)}, u32[]{:S(2)}, u32[]{:S(2)}) collective-permute-start(bf16[3,176,2048]{2,1,0:T(8,128)(2,1)} %add_convert_fusion.3), channel_id=1, source_target_pairs={{0,2},{1,3},{2,0},{3,1},{4,6},{5,7},{6,4},{7,5},{8,10},{9,11},{10,... | collective-permute-start | bytes 6488072 | tf_op jit(solution)/shard_map/ppermute | solution.py:48
  936.6 96.5 %collective-permute-start.50 = (bf16[96,2048]{1,0:T(8,128)(2,1)S(1)}, bf16[96,2048]{1,0:T(8,128)(2,1)S(1)}, u32[]{:S(2)}, u32[]{:S(2)}) collective-permute-start(bf16[96,2048]{1,0:T(8,128)(2,1)S(1)} %get-tuple-element.837), channel_id=1, source_target_pairs={{0,2},{1,3},{2,0},{3,1},{4,6},{5,7},{6,4},{7,5},{8,10},{9,11},{10,... | collective-permute-start | bytes 1179656 | tf_op jit(solution)/shard_map/ppermute | solution.py:48
  939.3 91.8 %collective-permute-start.83 = (f32[3]{0:T(128)S(1)}, f32[3]{0:T(128)S(1)}, u32[]{:S(2)}, u32[]{:S(2)}) collective-permute-start(f32[3]{0:T(128)S(1)} %fusion.211), channel_id=1, source_target_pairs={{0,2},{1,3},{2,0},{3,1},{4,6},{5,7},{6,4},{7,5},{8,10},{9,11},{10,... | collective-permute-start | bytes 44 | tf_op jit(solution)/shard_map/ppermute | solution.py:48
  1031.1 32.1 %collective-permute-start.81 = (bf16[352,2048]{1,0:T(8,128)(2,1)}, bf16[352,2048]{1,0:T(8,128)(2,1)}, u32[]{:S(2)}, u32[]{:S(2)}) collective-permute-start(bf16[352,2048]{1,0:T(8,128)(2,1)} %add_convert_fusion.4), channel_id=1, source_target_pairs={{0,2},{1,3},{2,0},{3,1},{4,6},{5,7},{6,4},{7,5},{8,10},{9,11},{10,... | collective-permute-start | bytes 4325384 | tf_op jit(solution)/shard_map/ppermute | solution.py:48
  1045.0 25.2 %collective-permute-start.54 = (bf16[256,640]{0,1:T(8,128)(2,1)S(1)}, bf16[256,640]{0,1:T(8,128)(2,1)S(1)}, u32[]{:S(2)}, u32[]{:S(2)}) collective-permute-start(bf16[256,640]{0,1:T(8,128)(2,1)S(1)} %get-tuple-element.885), channel_id=1, source_target_pairs={{0,4},{4,0},{8,12},{12,8},{16,20},{20,16},{24,28},{28,24},{1,5},{5... | collective-permute-start | bytes 983048 | tf_op jit(solution)/shard_map/ppermute | solution.py:38
  1087.7 18.2 %collective-permute-start.75 = (bf16[256,640]{0,1:T(8,128)(2,1)S(1)}, bf16[256,640]{0,1:T(8,128)(2,1)S(1)}, u32[]{:S(2)}, u32[]{:S(2)}) collective-permute-start(bf16[256,640]{0,1:T(8,128)(2,1)S(1)} %get-tuple-element.614), channel_id=1, source_target_pairs={{0,4},{4,0},{8,12},{12,8},{16,20},{20,16},{24,28},{28,24},{1,5},{5... | collective-permute-start | bytes 983048 | tf_op jit(solution)/shard_map/ppermute | solution.py:38
  1102.3 17.7 %collective-permute-start.66 = (bf16[256,1536]{1,0:T(8,128)(2,1)}, bf16[256,1536]{1,0:T(8,128)(2,1)}, u32[]{:S(2)}, u32[]{:S(2)}) collective-permute-start(bf16[256,1536]{1,0:T(8,128)(2,1)} %get-tuple-element.849), channel_id=1, source_target_pairs={{0,4},{4,0},{8,12},{12,8},{16,20},{20,16},{24,28},{28,24},{1,5},{5... | collective-permute-start | bytes 2359304 | tf_op jit(solution)/shard_map/ppermute | solution.py:38
  1111.4 119.8 %all-to-all-start.1 = ((bf16[3,8,176,256]{3,2,0,1:T(8,128)(2,1)}), bf16[3,8,176,256]{3,2,0,1:T(8,128)(2,1)S(1)}, u32[]{:S(2)}, u32[]{:S(2)}) async-start(bf16[3,8,176,256]{3,2,0,1:T(8,128)(2,1)} %bitcast.372), calls=%async_computation.1 | async-start | bytes 4325376 | tf_op jit(solution)/shard_map/all_to_all | solution.py:533
  1116.6 67.6 %collective-permute-start.78 = (f32[256,2]{0,1:T(2,128)S(1)}, f32[256,2]{0,1:T(2,128)S(1)}, u32[]{:S(2)}, u32[]{:S(2)}) collective-permute-start(f32[256,2]{0,1:T(2,128)S(1)} %slice_add_fusion), channel_id=1, source_target_pairs={{0,2},{1,3},{2,0},{3,1},{4,6},{5,7},{6,4},{7,5},{8,10},{9,11},{10,... | collective-permute-start | bytes 6152 | tf_op jit(solution)/shard_map/ppermute | solution.py:48
  1119.9 38.1 %collective-permute-start.67 = (bf16[256,1536]{1,0:T(8,128)(2,1)}, bf16[256,1536]{1,0:T(8,128)(2,1)S(1)}, u32[]{:S(2)}, u32[]{:S(2)}) collective-permute-start(bf16[256,1536]{1,0:T(8,128)(2,1)} %get-tuple-element.611), channel_id=1, source_target_pairs={{0,4},{4,0},{8,12},{12,8},{16,20},{20,16},{24,28},{28,24},{1,5},{5... | collective-permute-start | bytes 2359304 | tf_op jit(solution)/shard_map/ppermute | solution.py:38
  1123.5 48.3 %collective-permute-start.70 = (bf16[256,1536]{1,0:T(8,128)(2,1)S(1)}, bf16[256,1536]{1,0:T(8,128)(2,1)S(1)}, u32[]{:S(2)}, u32[]{:S(2)}) collective-permute-start(bf16[256,1536]{1,0:T(8,128)(2,1)S(1)} %fusion.19), channel_id=1, source_target_pairs={{0,8},{4,12},{8,16},{12,20},{16,24},{20,28},{24,0},{28,4},{1,9},{5... | collective-permute-start | bytes 2359304 | tf_op jit(solution)/shard_map/ppermute | solution.py:43
  1131.5 53.3 %collective-permute-start.63 = (bf16[96,2048]{1,0:T(8,128)(2,1)S(1)}, bf16[96,2048]{1,0:T(8,128)(2,1)S(1)}, u32[]{:S(2)}, u32[]{:S(2)}) collective-permute-start(bf16[96,2048]{1,0:T(8,128)(2,1)S(1)} %get-tuple-element.833), channel_id=1, source_target_pairs={{0,2},{1,3},{2,0},{3,1},{4,6},{5,7},{6,4},{7,5},{8,10},{9,11},{10,... | collective-permute-start | bytes 1179656 | tf_op jit(solution)/shard_map/ppermute | solution.py:48
  1158.1 27.3 %collective-permute-start.68 = (bf16[256,1536]{1,0:T(8,128)(2,1)S(1)}, bf16[256,1536]{1,0:T(8,128)(2,1)S(1)}, u32[]{:S(2)}, u32[]{:S(2)}) collective-permute-start(bf16[256,1536]{1,0:T(8,128)(2,1)S(1)} %copy-done.87), channel_id=1, source_target_pairs={{0,4},{4,0},{8,12},{12,8},{16,20},{20,16},{24,28},{28,24},{1,5},{5... | collective-permute-start | bytes 2359304 | tf_op jit(solution)/shard_map/ppermute | solution.py:38
  1173.1 27.2 %collective-permute-start.71 = (bf16[256,1536]{1,0:T(8,128)(2,1)S(1)}, bf16[256,1536]{1,0:T(8,128)(2,1)S(1)}, u32[]{:S(2)}, u32[]{:S(2)}) collective-permute-start(bf16[256,1536]{1,0:T(8,128)(2,1)S(1)} %fusion.21), channel_id=1, source_target_pairs={{0,8},{4,12},{8,16},{12,20},{16,24},{20,28},{24,0},{28,4},{1,9},{5... | collective-permute-start | bytes 2359304 | tf_op jit(solution)/shard_map/ppermute | solution.py:43
  1184.8 19.5 %collective-permute-start.64 = (bf16[96,2048]{1,0:T(8,128)(2,1)S(1)}, bf16[96,2048]{1,0:T(8,128)(2,1)S(1)}, u32[]{:S(2)}, u32[]{:S(2)}) collective-permute-start(bf16[96,2048]{1,0:T(8,128)(2,1)S(1)} %get-tuple-element.833), channel_id=1, source_target_pairs={{0,1},{1,0},{2,3},{3,2},{4,5},{5,4},{6,7},{7,6},{8,9},{9,8},{10,11... | collective-permute-start | bytes 1179656 | tf_op jit(solution)/shard_map/ppermute | solution.py:48
  1184.8 19.6 %collective-permute-start.65 = (bf16[96,2048]{1,0:T(8,128)(2,1)S(1)}, bf16[96,2048]{1,0:T(8,128)(2,1)S(1)}, u32[]{:S(2)}, u32[]{:S(2)}) collective-permute-start(bf16[96,2048]{1,0:T(8,128)(2,1)S(1)} %collective-permute-done.63), channel_id=1, source_target_pairs={{0,1},{1,0},{2,3},{3,2},{4,5},{5,4},{6,7},{7,6},{8,9},{9,8},{10,11... | collective-permute-start | bytes 1179656 | tf_op jit(solution)/shard_map/ppermute | solution.py:48
  1185.4 19.6 %collective-permute-start.69 = (bf16[256,1536]{1,0:T(8,128)(2,1)S(1)}, bf16[256,1536]{1,0:T(8,128)(2,1)S(1)}, u32[]{:S(2)}, u32[]{:S(2)}) collective-permute-start(bf16[256,1536]{1,0:T(8,128)(2,1)S(1)} %copy-done.86), channel_id=1, source_target_pairs={{0,4},{4,0},{8,12},{12,8},{16,20},{20,16},{24,28},{28,24},{1,5},{5... | collective-permute-start | bytes 2359304 | tf_op jit(solution)/shard_map/ppermute | solution.py:38
  1201.8 21.3 %collective-permute-start.72 = (bf16[256,1536]{1,0:T(8,128)(2,1)S(1)}, bf16[256,1536]{1,0:T(8,128)(2,1)S(1)}, u32[]{:S(2)}, u32[]{:S(2)}) collective-permute-start(bf16[256,1536]{1,0:T(8,128)(2,1)S(1)} %fusion.23), channel_id=1, source_target_pairs={{0,8},{4,12},{8,16},{12,20},{16,24},{20,28},{24,0},{28,4},{1,9},{5... | collective-permute-start | bytes 2359304 | tf_op jit(solution)/shard_map/ppermute | solution.py:43
  (172 other events, 1887.1 us)

commit v4 on v3

v4 whole, which is shorter than its diff:
```python
import jax
import jax.numpy as jnp
from jax import lax
from jax.sharding import PartitionSpec as P

HD = 128
EPS = 1e-06
BF = jnp.bfloat16
F32 = jnp.float32


def nn(left, right):
    return lax.dot_general(left, right, (((1,), (0,)), ((), ())), preferred_element_type=F32)


def nt(left, right):
    return lax.dot_general(left, right, (((1,), (1,)), ((), ())), preferred_element_type=F32)


def tn(left, right):
    return lax.dot_general(left, right, (((0,), (0,)), ((), ())), preferred_element_type=F32)


def at(array, index):
    return lax.dynamic_index_in_dim(array, index, 0, keepdims=False)


def put(array, value, index):
    return lax.dynamic_update_index_in_dim(array, value, index, 0)


def after(value, *earlier):
    return lax.optimization_barrier((value,) + earlier)[0]


def together(value, result):
    leaves, tree = jax.tree.flatten(result)
    value, *leaves = lax.optimization_barrier((value, *leaves))
    return value, jax.tree.unflatten(tree, leaves)


def swap_inner(value):
    size = lax.axis_size("ep")
    return lax.ppermute(value, "ep", [(i, i ^ 1) for i in range(size)])


def ring_outer(value):
    size = lax.axis_size("ep")
    return lax.ppermute(value, "ep", [(i, (i + 2) % size) for i in range(size)])


def swap_tp(value, mask):
    size = lax.axis_size("tp")
    return lax.ppermute(value, "tp", [(i, i ^ mask) for i in range(size)])


def relative_to_absolute():
    size = lax.axis_size("ep")
    me = lax.axis_index("ep")
    outer, inner = me // 2, me % 2
    rounds = size // 2
    return [(outer + rounds - r // 2) % rounds * 2 + (inner ^ r % 2) for r in range(size)]


def gather_ep(shard, works=()):
    rounds = lax.axis_size("ep") // 2
    blocks, done = [], []
    current = shard
    for k in range(rounds):
        other = swap_inner(current)
        following = ring_outer(current) if k < rounds - 1 else None
        if k < len(works):
            other, result = together(other, works[k](current))
            done.append(result)
        blocks += [current, other]
        if following is not None:
            current = after(following, other)
    return (blocks, done + [work(other) for work in works[rounds:]]) if works else blocks


def stack_static(blocks):
    whole = jnp.zeros((len(blocks),) + blocks[0].shape, blocks[0].dtype)
    for i, block in enumerate(blocks):
        whole = whole.at[i].set(block)
    return whole


def stack_absolute(blocks):
    whole = jnp.zeros((len(blocks),) + blocks[0].shape, blocks[0].dtype)
    for block, index in zip(blocks, relative_to_absolute()):
        whole = put(whole, block, index)
    return whole


def scatter_ep(block_of, works=()):
    rounds = lax.axis_size("ep") // 2
    arrived = other = token = None
    done = []
    for step, k in enumerate(list(range(1, rounds)) + [0]):
        away = block_of(2 * k + 1).astype(BF)
        if other is not None:
            away = after(away, other)
        other = swap_inner(away)
        if step < len(works):
            other, result = together(other, works[step](token))
            done.append(result)
        total = block_of(2 * k).astype(F32) + other.astype(F32)
        if arrived is not None:
            total = total + arrived.astype(F32)
        if k:
            token = total.astype(BF)
            arrived = ring_outer(token)
    done += [work(total) for work in works[rounds:]]
    return (total, done) if works else total


def scatter_absolute(parts, works=()):
    order = relative_to_absolute()
    return scatter_ep(lambda r: at(parts, order[r]), works)


TP_ORDER = (0, 2, 1, 3)


def gather_tp(shard):
    far = swap_tp(shard, 2)
    return [shard, far, swap_tp(shard, 1), swap_tp(far, 1)]


def gather_tp_rows(shard):
    me = lax.axis_index("tp")
    whole = jnp.zeros((lax.axis_size("tp"),) + shard.shape, shard.dtype)
    for j, block in zip(TP_ORDER, gather_tp(shard)):
        whole = put(whole, block, me ^ j)
    return whole.reshape(-1, shard.shape[-1])


def scatter_tp(parts):
    near = parts[0].astype(F32) + swap_tp(parts[1], 1).astype(F32)
    return near[0] + swap_tp(near[1].astype(BF), 2).astype(F32)


def scatter_tp_rows(parts):
    me = lax.axis_index("tp")
    far = at(parts, me ^ 2).astype(F32) + swap_tp(at(parts, me ^ 3).astype(BF), 1).astype(F32)
    far = swap_tp(far.astype(BF), 2)
    near = swap_tp(at(parts, me ^ 1).astype(BF), 1)
    return at(parts, me).astype(F32) + near.astype(F32) + far.astype(F32)


def scatter_tp_rows_start(parts):
    me = lax.axis_index("tp")
    far = at(parts, me ^ 2).astype(F32) + swap_tp(at(parts, me ^ 3).astype(BF), 1).astype(F32)
    return at(parts, me), swap_tp(at(parts, me ^ 1).astype(BF), 1), swap_tp(far.astype(BF), 2)


def sum_tp(value):
    value = value + swap_tp(value, 1)
    return value + swap_tp(value, 2)


def rms_scale(values):
    return lax.rsqrt(jnp.mean(values * values, axis=-1, keepdims=True) + EPS)


def norm_back(grad, values, scale, gain):
    weighted = grad * gain
    inner = jnp.mean(values * weighted, axis=-1, keepdims=True)
    return (scale * weighted - values * scale**3 * inner, jnp.sum(grad * values * scale, axis=0))


def gated_back(grad_hidden, gate_val, up_val):
    squash = jax.nn.sigmoid(gate_val)
    grad_gate = grad_hidden * up_val * squash * (1.0 + gate_val * (1.0 - squash))
    grad_up = grad_hidden * gate_val * squash
    return (grad_gate.astype(BF), grad_up.astype(BF))


def unit_coefs(gates, score, units, routed):
    return jnp.where(jnp.arange(units.shape[1]) < routed, gates, score)


def expert_forward(act, coef, units):
    gate_val, up_val = nt(act, units[0]), nt(act, units[1])
    return gate_val, up_val, (jax.nn.silu(gate_val) * up_val * coef).astype(BF)


def expert_back(gout, coef, score, kept, units, routed):
    grad_plain = nt(gout, units[2])
    plain = (jax.nn.silu(kept[0]) * kept[1])[:, routed:] * grad_plain[:, routed:]
    gscore = score * (1.0 - score) * jnp.sum(plain, axis=1, keepdims=True)
    return gated_back(grad_plain * coef, kept[0], kept[1]), gscore


def score_of(act, logit32):
    return jax.nn.sigmoid(jnp.sum(act.astype(F32) * logit32, axis=1, keepdims=True))


def grads_to_rows(grads, gscore, logit32, units):
    total = nn(grads[0], units[0]) + nn(grads[1], units[1])
    return (total + gscore * logit32).astype(BF)


def expert_step(act, gout, gates, logit32, units, routed):
    score = score_of(act, logit32)
    coef = unit_coefs(gates, score, units, routed)
    kept = expert_forward(act, coef, units)
    out = nn(kept[2], units[2]).astype(BF)
    grads, gscore = expert_back(gout, coef, score, kept, units, routed)
    gact = grads_to_rows(grads, gscore, logit32, units)
    logit_part = jnp.sum(act.astype(F32) * gscore, axis=0)
    return out, gact, (logit_part, tn(grads[0], act), tn(grads[1], act), tn(kept[2], gout))


def experts_in_blocks(act, gout, gates, logit32, units, routed, steps):
    rows, width = act.shape

    def step(totals, block):
        out, gact, sums = expert_step(*block, logit32, units, routed)
        return tuple(t + s for t, s in zip(totals, sums)), (out, gact)

    blocks = tuple(x.reshape(steps, rows // steps, -1) for x in (act, gout, gates))
    totals = tuple(jnp.zeros(size, F32) for size in [(width,)] + 3 * [units.shape[1:]])
    sums, (out, gact) = lax.scan(step, totals, blocks)
    return out.reshape(rows, width), gact.reshape(rows, width), sums[0], sums[1:]


def place(units, parts, offset):
    for i, part in parts:
        start = (0, offset + i * part.shape[1], 0)
        units = lax.dynamic_update_slice(units, part, start)
    return units


def columns(array, head):
    return array[:, head * HD : (head + 1) * HD]


def on_device(
    tokens,
    first_gain,
    query_weight,
    key_weight,
    value_weight,
    output_weight,
    second_gain,
    shared_logit,
    shared_gate,
    shared_up,
    shared_down,
    routed_gate_weight,
    routed_up_weight,
    expert_down,
    route_ids,
    route_gates,
    piece_start,
    piece_length,
    block_grad,
):
    groups = lax.axis_size("ep")
    quarters = lax.axis_size("tp")
    me_ep = lax.axis_index("ep")
    me_tp = lax.axis_index("tp")
    count, width = tokens.shape
    part = count // quarters
    local_heads = query_weight.shape[1] // HD
    wide = local_heads * HD
    factor = HD ** (-0.5)

    def own(array):
        return lax.dynamic_slice_in_dim(array, me_tp * part, part, 0)

    dense = jnp.sum(
        own(route_gates)[:, :, None]
        * (own(route_ids)[:, :, None] == jnp.arange(groups, dtype=jnp.int32)).astype(F32),
        axis=1,
    )
    shard_rows = query_weight.shape[0]
    high = dense.astype(BF)
    low = (dense - high.astype(F32)).astype(BF)
    packed = jnp.concatenate([high.reshape(-1), low.reshape(-1)]).reshape(-1, shard_rows)
    first = jnp.pad(first_gain[:, None], ((0, 0), (0, 127)))
    projection = jnp.concatenate([query_weight, key_weight, value_weight, first], axis=1)

    routed_gate, routed_up, routed_down = lax.optimization_barrier(
        (routed_gate_weight[0], routed_up_weight[0], expert_down[0], projection)
    )[:3]
    own_units = jnp.stack([routed_gate.T, routed_up.T, routed_down])
    rows = own_units.shape[1]
    routed = quarters * rows
    units_dev = shared_down.shape[0]
    piece = units_dev // groups
    x_units = swap_tp(own_units, 2)
    core_units = swap_tp(own_units, 1)

    def near_units(block):
        own_part, units = lax.optimization_barrier(
            (own_units, jnp.zeros((3, routed + quarters * piece, width), BF), block)
        )[:2]
        return place(units, [(0, own_part), (2, core_units)], 0)

    def nothing(block):
        return ()

    qkv_blocks, done = gather_ep(projection, [nothing, nothing, near_units])
    units = done[2]
    first = stack_absolute([block[:, 3 * wide :] for block in qkv_blocks])
    gain_one32 = first[:, :, 0].reshape(1, width).astype(F32)
    w_qkv = stack_absolute([block[:, : 3 * wide] for block in qkv_blocks]).reshape(width, -1)

    inputs32 = tokens.astype(F32)
    scale_one = rms_scale(inputs32)
    act1 = (inputs32 * scale_one * gain_one32).astype(BF)
    positions = jnp.arange(count, dtype=jnp.int32)
    start = piece_start[0]
    inside = (positions >= start) & (positions < start + piece_length[0])
    visible = (positions[None, :] <= positions[:, None]) | inside[:, None] & inside[None, :]
    all_lse, mixes, projected = [], [], []

    def project(block):
        projected.append(nn(after(act1, block), w_qkv).astype(BF))
        return projected[0]

    def attend(heads):
        def run(block):
            done = []
            for h in heads:
                query_h = after(columns(projected[0], h), block)
                key_h = columns(projected[0], local_heads + h)
                value_h = columns(projected[0], 2 * local_heads + h)
                scores = jnp.where(visible, nt(query_h, key_h) * factor, -1e30)
                highest = jnp.max(scores, axis=-1, keepdims=True)
                total = jnp.sum(jnp.exp(scores - highest), axis=-1, keepdims=True)
                all_lse.append(highest + jnp.log(total))
                probs = jnp.exp(scores - all_lse[h]).astype(BF)
                mixes.append(nn(probs, value_h).astype(BF))
                done += [all_lse[h], mixes[h]]
            return done

        return run

    spare = jnp.concatenate([jnp.stack([second_gain, shared_logit]), packed]).T
    spare = jnp.pad(spare, ((0, 0), (0, -spare.shape[1] % 128)))
    half = local_heads // 2

    shared = jnp.stack([shared_gate.T, shared_up.T, shared_down]).reshape(3, groups, piece, -1)
    shared = lax.all_to_all(
        after(shared, qkv_blocks[-1]), "ep", split_axis=1, concat_axis=1, tiled=True
    )

    def attend_last(block):
        done = attend(range(half, local_heads))(block)
        return done, after(shared.transpose(0, 2, 1, 3).reshape(3, piece, width), block)

    blocks, done = gather_ep(
        after(jnp.concatenate([output_weight.T, spare], axis=1), qkv_blocks[-1]),
        [project, attend(range(half)), attend_last],
    )
    shared = done[2][1]
    x_shared = swap_tp(shared, 2)
    qkv = projected[0]
    query, key, value = qkv[:, :wide], qkv[:, wide : 2 * wide], qkv[:, 2 * wide :]
    spare = stack_absolute([block[:, wide:] for block in blocks])
    w_out = stack_absolute([block[:, :wide] for block in blocks]).reshape(width, -1)
    vectors = spare[:, :, :2].reshape(width, 2).T.astype(F32)
    gain_two32, logit32 = vectors[0:1], vectors[1:2]
    packed = spare[:, :, 2 : 2 + packed.shape[0]].transpose(0, 2, 1)
    packed = packed.reshape(groups, 2, part, groups).astype(F32).sum(axis=1)
    chosen = jnp.arange(groups, dtype=jnp.int32)
    gates = jnp.sum(jnp.where(chosen == me_ep, packed, 0.0), axis=2)
    order = jnp.stack(relative_to_absolute())
    gates = jnp.sum(jnp.where((order[:, None] == chosen)[:, :, None], gates[None], 0.0), axis=1)
    gates = gates.reshape(groups * part, 1)

    attn_mix = jnp.concatenate(mixes, axis=1)
    branch = nt(attn_mix, w_out).reshape(quarters, part, width)
    attn_branch = scatter_tp_rows(branch)
    inputs_own = own(tokens).astype(F32)
    resid = inputs_own + attn_branch
    scale_two = rms_scale(resid)
    act2 = (resid * scale_two * gain_two32).astype(BF)

    def far_units(block):
        x_part = after(x_units, block)
        return place(units, [(1, x_part), (3, swap_tp(x_part, 1))], 0)

    def shared_units(block):
        x_part = after(x_shared, block)
        return [(0, shared), (1, x_part), (2, swap_tp(shared, 1)), (3, swap_tp(x_part, 1))]

    act_blocks, done = gather_ep(act2, [far_units])
    units = place(done[0], shared_units(act_blocks[4 if len(act_blocks) > 4 else -1]), routed)
    act_all = stack_static(act_blocks).reshape(groups * part, width)
    gout_own = after(own(block_grad), act_blocks[-2])

    def tokens_back(block):
        return block.reshape(groups, part, width)

    def prepare_shared(total):
        total = total.astype(BF).reshape(3, piece, groups, -1).transpose(0, 2, 1, 3)
        return lax.optimization_barrier(total)

    steps = -(-groups * part // 768)
    if steps == 1:
        score = score_of(act_all, logit32)
        coef = unit_coefs(gates, score, units, routed)

        def forward_gate(token):
            return nt(after(act_all, token), units[0])

        kept = []

        def forward_up(token):
            up_val = nt(after(act_all, token), units[1])
            hidden = (jax.nn.silu(kept[0]) * up_val * coef).astype(BF)
            return up_val, hidden

        def output(token):
            return nn(after(kept[2], token), units[2]).astype(BF)

        def keep_up(token):
            kept.extend(forward_up(token))
            return kept[1:]

        def keep_gate(token):
            kept.append(forward_gate(token))
            return kept[0]

        blocks, done = gather_ep(
            gout_own, [keep_gate, keep_up, output]
        )
        gate_val = done[0]
        up_val, hidden = done[1]
        ffn_part = done[2]
        gout_all = stack_static(blocks).reshape(groups * part, width)
        ffn_part = tokens_back(ffn_part)
        back = {}

        def backward(token):
            back["grads"], back["gscore"] = expert_back(
                gout_all, coef, score, (gate_val, up_val), units, routed
            )
            return back["grads"], back["gscore"]

        def rows_gate(token):
            back["rows"] = nn(after(back["grads"][0], token), units[0])
            return back["rows"]

        def rows_up(token):
            total = back["rows"] + nn(after(back["grads"][1], token), units[1])
            return (total + back["gscore"] * logit32).astype(BF)

        state = {"sum": [], "got": [], "x": None}

        def weight_grad(j, token, first, last):
            left = (hidden if j == 2 else back["grads"][j])[:, first:last]
            return tn(left, after(gout_all if j == 2 else act_all, token)).astype(BF)

        def shared_work(token):
            full = jnp.stack([weight_grad(j, token, routed, None) for j in range(3)])
            state["shared"] = full
            away = full[:, 2 * piece :]
            state["shared_got"] = swap_tp(away, 1)
            return away

        def routed_grad(j, token):
            full = weight_grad(j, token, 0, routed)
            away = full[2 * rows :]
            state["sum"].append(full)
            state["got"].append(swap_tp(away, 1))
            return full, away

        def shared_sum(index):
            span = slice(index * piece, (index + 1) * piece)
            return state["shared"][:, span].astype(F32) + state["shared_got"][:, span].astype(F32)

        def summed(j, index):
            span = slice(index * rows, (index + 1) * rows)
            return state["sum"][j][span].astype(F32) + state["got"][j][span].astype(F32)

        def routed_ready(js, token):
            along_x = jnp.concatenate([summed(j, 1) for j in js]).astype(BF)
            state["ready"] = after(along_x, token)
            return state["ready"]

        def routed_x(js, token):
            if "ready" not in state:
                routed_ready(js, token)
            along_x = after(state.pop("ready"), token)
            arrived = swap_tp(along_x, 2)
            state["x"] = arrived if state["x"] is None else jnp.concatenate([state["x"], arrived])
            return along_x

        def gate_work(token):
            along_x = after(shared_sum(1).astype(BF), token)
            state["shared_x"] = swap_tp(along_x, 2)
            return routed_grad(0, token), along_x

        def up_work(token):
            state["logit"] = jnp.sum(after(act_all, token).astype(F32) * back["gscore"], axis=0)
            return routed_grad(1, token), state["logit"]

        def last_work(token):
            return routed_grad(2, token)

        def total_work(token):
            state["total"] = prepare_shared(shared_sum(0) + state["shared_x"].astype(F32))
            return state["total"]

        ffn_branch, done = scatter_ep(
            lambda r: ffn_part[r], [backward, rows_gate, rows_up, shared_work]
        )
        gact_part = tokens_back(done[2])
        gact2, _ = scatter_ep(lambda r: gact_part[r], [gate_work, up_work, nothing, total_work])
        logit_part = state["logit"]

        def shared_total():
            return state["total"]

        def expert_grads():
            arrived = state["x"].reshape(3, rows, width).astype(F32)
            return [summed(j, 0) + arrived[j] for j in range(3)]

    else:
        gout_all = stack_static(gather_ep(gout_own)).reshape(groups * part, width)
        ffn_part, gact_part, logit_part, sums = experts_in_blocks(
            act_all, gout_all, gates, logit32, units, routed, steps
        )
        ffn_part, gact_part = tokens_back(ffn_part), tokens_back(gact_part)
        gact2 = scatter_ep(lambda r: gact_part[r])
        ffn_branch = scatter_ep(lambda r: ffn_part[r])

        def relative(j, first, last):
            parts = sums[j][first:last].reshape(2, 2, -1, width)
            return scatter_tp(parts.astype(BF))

        def last_work(token):
            return ()

        def routed_ready(js, token):
            return ()

        def routed_x(js, token):
            return ()

        def expert_grads():
            return [relative(j, 0, routed) for j in range(3)]

        def shared_total():
            return prepare_shared(jnp.stack([relative(j, routed, None) for j in range(3)]))

    block_sum = resid + ffn_branch
    squares = jnp.stack(
        [
            jnp.sum(attn_branch * attn_branch),
            jnp.sum(ffn_branch * ffn_branch),
            jnp.sum(block_sum * block_sum),
        ]
    )

    resid_part, gain_two_part = norm_back(gact2, resid, scale_two, gain_two32)
    gresid = own(block_grad).astype(F32) + resid_part
    tail = {"shared": shared_total()}
    gresid = after(gresid, tail["shared"])
    gattn = after(gather_tp_rows(gresid.astype(BF)), *jax.tree.leaves(last_work(gresid)))
    block_out = gather_tp_rows(after(block_sum.astype(BF), gattn))
    vectors = jnp.stack([gain_two_part, logit_part], axis=1).reshape(groups, -1, 2)
    vectors = jnp.pad(vectors, ((0, 0), (0, 0), (0, 126))).astype(BF)
    out_grads = tn(gattn, attn_mix).astype(BF).reshape(groups, -1, wide)
    gmix = nn(gattn, w_out).astype(BF)

    def head_back(h):
        def run(token):
            gmix_h = columns(gmix, h)
            if token is not None:
                gmix_h = after(gmix_h, token)
            query_h, key_h = columns(query, h), columns(key, h)
            scores = jnp.where(visible, nt(query_h, key_h) * factor, -1e30)
            probs = jnp.exp(scores - all_lse[h])
            gprob = nt(gmix_h, columns(value, h))
            gvalue = tn(probs.astype(BF), gmix_h).astype(BF)
            inner = jnp.sum(probs * gprob, axis=-1, keepdims=True)
            gscores = (probs * (gprob - inner)).astype(BF)
            gquery = (nn(gscores, key_h) * factor).astype(BF)
            gkey = (tn(gscores, query_h) * factor).astype(BF)
            return gquery, gkey, gvalue

        return run

    def heads_back(first, last):
        def run(token):
            sent = routed_x([0], gattn) if first == 0 else (routed_x([1], token), routed_ready([2], token))
            if first == 0:
                tail["squares"] = sum_tp(after(squares, gattn))
            return [head_back(h)(token) for h in range(first, last)], sent

        return run

    out_grads, heads = scatter_absolute(
        jnp.concatenate([out_grads, vectors], axis=2), [heads_back(0, half), heads_back(half, local_heads)]
    )
    heads = heads[0][0] + heads[1][0]
    output_grad = out_grads[:, :wide].T
    early = sum_tp(out_grads[:, wide : wide + 2])
    gqkv = jnp.concatenate([head[i] for i in range(3) for head in heads], axis=1)
    gqkv_grad = tn(act1, gqkv).astype(BF).reshape(groups, -1, 3 * wide)

    def gact1_work(token):
        shared = lax.all_to_all(tail["shared"], "ep", split_axis=1, concat_axis=1, tiled=True)
        gact1 = nt(after(gqkv, gqkv_grad), w_qkv).astype(BF).reshape(quarters, part, width)
        tail["gact1"] = scatter_tp_rows_start(gact1)
        return gact1, shared

    def tokens_work(token):
        gact1 = sum(part.astype(F32) for part in after(tail["gact1"], token))
        input_part, _ = norm_back(gact1, inputs_own, own(scale_one), gain_one32)
        tail["tokens"] = (gresid + input_part).astype(BF)
        return tail["tokens"], routed_x([2], gact1)

    qkv_grad, done = scatter_absolute(
        gqkv_grad, [gact1_work, tokens_work]
    )
    shared_grads, squares = done[0][1], tail["squares"]
    rms_values = jnp.sqrt(squares / (count * width))[None, :]
    tokens_grad = gather_tp_rows(tail["tokens"]).astype(F32)

    shared_grads = shared_grads.reshape(3, units_dev, -1)
    sgate_grad = shared_grads[0].T.astype(F32)
    sup_grad = shared_grads[1].T.astype(F32)
    sdown_grad = shared_grads[2].astype(F32)
    gate_grad, up_grad, down_grad = expert_grads()

    own_qkv = jnp.concatenate([query_weight, key_weight, value_weight], axis=1).astype(F32)
    late = sum_tp(jnp.sum(own_qkv * qkv_grad, axis=1) / first_gain.astype(F32))
    return (
        block_out,
        tokens_grad,
        late,
        qkv_grad[:, :wide],
        qkv_grad[:, wide : 2 * wide],
        qkv_grad[:, 2 * wide :],
        output_grad,
        early[:, 0],
        early[:, 1],
        sgate_grad,
        sup_grad,
        sdown_grad,
        gate_grad.T[None],
        up_grad.T[None],
        down_grad[None],
        rms_values,
    )


def solution(mesh):
    in_specs = (
        P("ep", None),
        P("ep"),
        P("ep", "tp"),
        P("ep", "tp"),
        P("ep", "tp"),
        P("tp", "ep"),
        P("ep"),
        P("ep"),
        P("ep", "tp"),
        P("ep", "tp"),
        P("tp", "ep"),
        P("ep", None, "tp"),
        P("ep", None, "tp"),
        P("ep", "tp", None),
        P("ep", None),
        P("ep", None),
        P("ep"),
        P("ep"),
        P("ep", None),
    )
    out_specs = (
        P("ep", None),
        P("ep", None),
        P("ep"),
        P("ep", "tp"),
        P("ep", "tp"),
        P("ep", "tp"),
        P("tp", "ep"),
        P("ep"),
        P("ep"),
        P("ep", "tp"),
        P("ep", "tp"),
        P("tp", "ep"),
        P("ep", None, "tp"),
        P("ep", None, "tp"),
        P("ep", "tp", None),
        P("ep", None),
    )
    return jax.shard_map(
        on_device, mesh=mesh, in_specs=in_specs, out_specs=out_specs, check_vma=False
    )
```

time: 1250 us -> 722 us (0.58)
  local copies, waits for them, and re-layouts: 535 us -> 162 us
  waiting for transfers between devices: 368 us -> 222 us
    dynamic_update_slice x18 -> x42, local copies, waits for them, and re-layouts: 395 us -> 43.4 us  [put(): return lax.dynamic_update_index_in_dim(array, value, index, 0)]
    ppermute x35, waiting for transfers between devices: 160 us -> 67.6 us  [swap_tp(): return lax.ppermute(value, 'tp', [(i, i ^ mask) for i in range(size)])]
    ppermute x21 -> x24, waiting for transfers between devices: 76.4 us -> 40.8 us  [ring_outer(): return lax.ppermute(value, 'ep', [(i, (i + 2) % size) for i in range(size)])]
    broadcast_in_dim x8 -> x30, local copies, waits for them, and re-layouts: 49.1 us -> 16.7 us  [put(): return lax.dynamic_update_index_in_dim(array, value, index, 0)]
    dynamic_update_slice x0 -> x8, local copies, waits for them, and re-layouts: none -> 30.9 us  [place(): units = lax.dynamic_update_slice(units, part, start)]
    ppermute x28 -> x32, waiting for transfers between devices: 131 us -> 114 us  [swap_inner(): return lax.ppermute(value, 'ep', [(i, i ^ 1) for i in range(size)])]
    unnamed x287 -> x181, local copies, waits for them, and re-layouts: 28.9 us -> 12.7 us
    dot_general x19 -> x13, matrix products: 59.7 us -> 47.3 us  [nn(): lax.dot_general(left, right, (((1,), (0,)), ((), ())), preferred_element_...]
  transfers between devices with their start and end apart: 86 -> 93, of which waited for: 33 -> 36; matrix products, arithmetic and copies ran while one was open for 58% -> 50% of each run, Pallas kernels for 0% -> 0%
where the time goes in v4:
time: 722 us; the launch traced here: 712 us
  waiting for transfers between devices  222 us (31%)
  local copies, waits for them, and re-layouts  162 us (22%)
  matrix products  143 us (20%)
  starting transfers between devices  97.7 us (14%)
  other arithmetic  82.4 us (11%)
    ppermute x32, waiting for transfers between devices, swap_inner(): return lax.ppermute(value, 'ep', [(i, i ^ 1) for i in range(size)])  114 us
    ppermute x35, waiting for transfers between devices, swap_tp(): return lax.ppermute(value, 'tp', [(i, i ^ mask) for i in range(size)])  67.6 us
    dot_general x17, matrix products, nt(): lax.dot_general(left, right, (((1,), (1,)), ((), ())), preferred_element_...  53.9 us
    dot_general x13, matrix products, nn(): lax.dot_general(left, right, (((1,), (0,)), ((), ())), preferred_element_...  47.3 us
    dynamic_update_slice x42, local copies, waits for them, and re-layouts, put(): return lax.dynamic_update_index_in_dim(array, value, index, 0)  43.4 us
    dot_general x16, matrix products, tn(): lax.dot_general(left, right, (((0,), (0,)), ((), ())), preferred_element_...  41.5 us
    ppermute x24, waiting for transfers between devices, ring_outer(): return lax.ppermute(value, 'ep', [(i, (i + 2) % size) for i in range(size)])  40.8 us
    ppermute x24, starting transfers between devices, ring_outer(): return lax.ppermute(value, 'ep', [(i, (i + 2) % size) for i in range(size)])  38.4 us
  transfers between devices with their start and end apart: 93, of which 36 were waited for; matrix products, arithmetic and copies ran while one was open for 50% of the time, Pallas kernels for 0%

profile of v4, /device:TPU:0, one launch (start us, length us, event | category | flops | bytes accessed | tf_op | source)
XLA Modules:
  0.0 711.5 jit_solution(2845711319285061588)
XLA Ops:
  8.3 3.7 pad_maximum_fusion.1
  39.2 11.9 %collective-permute-done.2 = bf16[256,1664]{1,0:T(8,128)(2,1)} collective-permute-done((bf16[256,1664]{1,0:T(8,128)(2,1)}, bf16[256,1664]{1,0:T(8,128)(2,1)}, u32[]{:S(2)}, u32[]{:S(2)}) %collective-permute-start.2) | collective-permute-done | bytes 852000 | tf_op jit(solution)/shard_map/ppermute | solution.py:44
  59.9 8.9 %broadcast_in_dim.256 = bf16[3,2112,2048]{2,1,0:T(8,128)(2,1)} broadcast(bf16[]{:T(256)} %constant.748.clone.1), dimensions={} | broadcast | bytes 25952258 | tf_op jit(solution)/shard_map/broadcast_in_dim | solution.py:298
  68.8 4.8 constant_dynamic-update-slice_fusion.33
  73.7 4.9 constant_dynamic-update-slice_fusion.32
  86.5 12.8 %collective-permute-done.7 = bf16[256,1664]{1,0:T(8,128)(2,1)S(1)} collective-permute-done((bf16[256,1664]{1,0:T(8,128)(2,1)}, bf16[256,1664]{1,0:T(8,128)(2,1)S(1)}, u32[]{:S(2)}, u32[]{:S(2)}) %collective-permute-start.7) | collective-permute-done | bytes 852000 | tf_op jit(solution)/shard_map/ppermute | solution.py:44
  107.2 5.1 all-to-all-start
  113.4 5.9 convolution_convert_fusion.9
  144.7 11.3 %collective-permute-done.10 = bf16[256,640]{0,1:T(8,128)(2,1)} collective-permute-done((bf16[256,640]{0,1:T(8,128)(2,1)}, bf16[256,640]{0,1:T(8,128)(2,1)}, u32[]{:S(2)}, u32[]{:S(2)}) %collective-permute-start.10) | collective-permute-done | bytes 327712 | tf_op jit(solution)/shard_map/ppermute | solution.py:49
  157.3 9.4 %collective-permute-start.13 = (bf16[256,640]{0,1:T(8,128)(2,1)}, bf16[256,640]{0,1:T(8,128)(2,1)}, u32[]{:S(2)}, u32[]{:S(2)}) collective-permute-start(bf16[256,640]{0,1:T(8,128)(2,1)} %collective-permute-done.10), channel_id=1, source_target_pairs={{0,8},{4,12},{8,16},{12,20},{16,24},{20,28},{24,0},{28,4},{1,9},{5... | collective-permute-start | bytes 983048 | tf_op jit(solution)/shard_map/ppermute | solution.py:49
  197.8 10.8 %collective-permute-done.17 = bf16[96,2048]{1,0:T(8,128)(2,1)S(1)} collective-permute-done((bf16[96,2048]{1,0:T(8,128)(2,1)S(1)}, bf16[96,2048]{1,0:T(8,128)(2,1)S(1)}, u32[]{:S(2)}, u32[]{:S(2)}) %collective-permute-start.17) | collective-permute-done | bytes 393248 | tf_op jit(solution)/shard_map/ppermute | solution.py:54
  218.7 4.8 constant_dynamic-update-slice_fusion.20
  224.0 5.0 constant_dynamic-update-slice_fusion.19
  233.2 8.3 %collective-permute-done.22 = bf16[96,2048]{1,0:T(8,128)(2,1)S(1)} collective-permute-done((bf16[96,2048]{1,0:T(8,128)(2,1)S(1)}, bf16[96,2048]{1,0:T(8,128)(2,1)S(1)}, u32[]{:S(2)}, u32[]{:S(2)}) %collective-permute-start.22) | collective-permute-done | bytes 393248 | tf_op jit(solution)/shard_map/ppermute | solution.py:49
  243.2 19.5 %collective-permute-done.29 = bf16[3,176,2048]{2,1,0:T(8,128)(2,1)} collective-permute-done((bf16[3,176,2048]{2,1,0:T(8,128)(2,1)}, bf16[3,176,2048]{2,1,0:T(8,128)(2,1)}, u32[]{:S(2)}, u32[]{:S(2)}) %collective-permute-start.29) | collective-permute-done | bytes 2162720 | tf_op jit(solution)/shard_map/ppermute | solution.py:54
  275.9 5.3 collective-permute-done.28
  285.2 9.5 %fusion.1 = f32[768,2112]{0,1:T(8,128)S(1)} fusion(bf16[768,2048]{1,0:T(8,128)(2,1)S(1)} %bitcast.362, bf16[3,2112,2048]{2,1,0:T(8,128)(2,1)} %constant_dynamic-update-slice_fusion.15), kind=kOutput, calls=%fused_computation.7 | convolution fusion | flops 6643777536 | bytes 18284544 | tf_op jit(solution)/shard_map/dot_general | solution.py:17
  299.7 12.1 %fusion.6 = (bf16[768,2112]{0,1:T(8,128)(2,1)S(1)}, f32[768,2112]{0,1:T(8,128)}) fusion(f32[768,2112]{0,1:T(8,128)S(1)} %fusion.1, f32[768]{0:T(1024)S(1)} %div.65, f32[768]{0:T(1024)S(1)} %copy-done.71, pred[2112]{0:T(1024)(128)(4,1)S(1)} %copy-done.72, bf16[768,2048]{1,0:T(8,128)(2,1)S(1)} %bitcast.363, ...), kind=kOutput, calls=%fused_computation.16 | convolution fusion | flops 6656753664 | bytes 28024896 | tf_op jit(solution)/shard_map/dot_general | solution.py:17
  315.9 10.0 %fusion.8 = bf16[768,2048]{1,0:T(8,128)(2,1)S(1)} fusion(bf16[768,2112]{0,1:T(8,128)(2,1)S(1)} %get-tuple-element.367, bf16[3,2112,2048]{2,1,0:T(8,128)(2,1)} %constant_dynamic-update-slice_fusion.15), kind=kOutput, calls=%fused_computation.31 | convolution fusion | flops 6645350400 | bytes 15040512 | tf_op jit(solution)/shard_map/dot_general | solution.py:13
  332.4 8.2 %collective-permute-done.37 = bf16[96,2048]{1,0:T(8,128)(2,1)S(1)} collective-permute-done((bf16[96,2048]{1,0:T(8,128)(2,1)S(1)}, bf16[96,2048]{1,0:T(8,128)(2,1)S(1)}, u32[]{:S(2)}, u32[]{:S(2)}) %collective-permute-start.37) | collective-permute-done | bytes 393248 | tf_op jit(solution)/shard_map/ppermute | solution.py:44
  341.4 18.1 %multiply_convert_fusion = (bf16[768,2112]{0,1:T(8,128)(2,1)}, bf16[768,2112]{0,1:T(8,128)(2,1)}, f32[768,2112]{0,1:T(8,128)}, f32[768,2112]{0,1:T(8,128)}) fusion(f32[768,2112]{0,1:T(8,128)} %copy-done.35, f32[768]{0:T(1024)S(1)} %div.65, f32[768]{0:T(1024)S(1)} %copy-done.71, pred[2112]{0:T(1024)(128)(4,1)} %iota_compare_fusion.4, ...), kind=kOutput, calls=%fused_computation.17 | convolution fusion | flops 6668107776 | bytes 44246016 | tf_op jit(solution)/shard_map/dot_general | solution.py:17
  360.8 11.2 %fusion = f32[768,2048]{1,0:T(8,128)S(1)} fusion(bf16[768,2112]{0,1:T(8,128)(2,1)} %get-tuple-element.360, bf16[3,2112,2048]{2,1,0:T(8,128)(2,1)} %constant_dynamic-update-slice_fusion.15), kind=kOutput, calls=%fused_computation.6 | convolution fusion | flops 6643777536 | bytes 18186240 | tf_op jit(solution)/shard_map/dot_general | solution.py:13
  372.7 4.1 fusion.21
  376.8 4.2 collective-permute-done.38
  384.2 11.7 %add_convert_fusion = bf16[768,2048]{1,0:T(8,128)(2,1)} fusion(f32[768,2048]{1,0:T(8,128)S(1)} %fusion, bf16[768,2112]{0,1:T(8,128)(2,1)S(1)} %copy-done.80, bf16[3,2112,2048]{2,1,0:T(8,128)(2,1)} %constant_dynamic-update-slice_fusion.15, f32[2048]{0:T(1024)S(1)} %bitcast.399, f32[768]{0:T(1024)S(1)} %fusion.117), kind=kOutput, calls=%fused_computation.21 | convolution fusion | flops 6650068992 | bytes 21343232 | tf_op jit(solution)/shard_map/dot_general | solution.py:13
  397.9 3.7 fusion.12
  404.0 5.7 fusion.14
  412.1 6.5 convolution_convert_fusion.3
  419.6 4.3 collective-permute-start.43
  426.9 9.0 %collective-permute-done.41 = bf16[96,2048]{1,0:T(8,128)(2,1)S(1)} collective-permute-done((bf16[96,2048]{1,0:T(8,128)(2,1)S(1)}, bf16[96,2048]{1,0:T(8,128)(2,1)S(1)}, u32[]{:S(2)}, u32[]{:S(2)}) %collective-permute-start.41) | collective-permute-done | bytes 393248 | tf_op jit(solution)/shard_map/ppermute | solution.py:44
  439.0 4.4 collective-permute-done.44
  445.7 6.5 convolution_convert_fusion.2
  461.2 4.5 collective-permute-done.47
  470.8 15.5 %collective-permute-done.49 = bf16[3,176,2048]{2,1,0:T(8,128)(2,1)} collective-permute-done((bf16[3,176,2048]{2,1,0:T(8,128)(2,1)}, bf16[3,176,2048]{2,1,0:T(8,128)(2,1)}, u32[]{:S(2)}, u32[]{:S(2)}) %collective-permute-start.49) | collective-permute-done | bytes 2162720 | tf_op jit(solution)/shard_map/ppermute | solution.py:54
  486.3 3.9 add_convert_fusion.1
  497.1 4.8 all-to-all-start.1
  501.9 7.2 %convolution_convert_fusion.1 = bf16[1408,2048]{1,0:T(8,128)(2,1)S(1)} fusion(bf16[768,2048]{1,0:T(8,128)(2,1)} %bitcast.93, bf16[768,2112]{0,1:T(8,128)(2,1)} %copy-done.79), kind=kOutput, calls=%fused_computation.13 | convolution fusion | flops 4432068608 | bytes 11075584 | tf_op jit(solution)/shard_map/dot_general | solution.py:21
  545.6 5.3 collective-permute-done.59
  565.8 3.7 convolution_convert_fusion
  572.9 5.4 convolution_convert_fusion.8
  584.5 4.1 collective-permute-done.80
  597.8 10.5 %collective-permute-done.85 = f32[256,2]{0,1:T(2,128)S(1)} collective-permute-done((f32[256,2]{0,1:T(2,128)S(1)}, f32[256,2]{0,1:T(2,128)S(1)}, u32[]{:S(2)}, u32[]{:S(2)}) %collective-permute-start.85) | collective-permute-done | bytes 2080 | tf_op jit(solution)/shard_map/ppermute | solution.py:54
  613.7 4.0 collective-permute-done.66
  635.3 17.4 %collective-permute-done.71 = bf16[256,1536]{1,0:T(8,128)(2,1)S(1)} collective-permute-done((bf16[256,1536]{1,0:T(8,128)(2,1)}, bf16[256,1536]{1,0:T(8,128)(2,1)S(1)}, u32[]{:S(2)}, u32[]{:S(2)}) %collective-permute-start.71) | collective-permute-done | bytes 786464 | tf_op jit(solution)/shard_map/ppermute | solution.py:44
  659.5 13.2 %collective-permute-done.72 = bf16[256,1536]{1,0:T(8,128)(2,1)S(1)} collective-permute-done((bf16[256,1536]{1,0:T(8,128)(2,1)S(1)}, bf16[256,1536]{1,0:T(8,128)(2,1)S(1)}, u32[]{:S(2)}, u32[]{:S(2)}) %collective-permute-start.72) | collective-permute-done | bytes 786464 | tf_op jit(solution)/shard_map/ppermute | solution.py:44
  681.4 10.3 %collective-permute-done.73 = bf16[256,1536]{1,0:T(8,128)(2,1)S(1)} collective-permute-done((bf16[256,1536]{1,0:T(8,128)(2,1)S(1)}, bf16[256,1536]{1,0:T(8,128)(2,1)S(1)}, u32[]{:S(2)}, u32[]{:S(2)}) %collective-permute-start.73) | collective-permute-done | bytes 786464 | tf_op jit(solution)/shard_map/ppermute | solution.py:44
  691.7 7.6 %collective-permute-done.76 = bf16[256,1536]{1,0:T(8,128)(2,1)S(1)} collective-permute-done((bf16[256,1536]{1,0:T(8,128)(2,1)S(1)}, bf16[256,1536]{1,0:T(8,128)(2,1)S(1)}, u32[]{:S(2)}, u32[]{:S(2)}) %collective-permute-start.76) | collective-permute-done | bytes 786464 | tf_op jit(solution)/shard_map/ppermute | solution.py:49
  701.0 6.1 fusion.15
  (598 shorter events, 322.5 us)
Async XLA Ops:
  3.7 26.1 %collective-permute-start = (bf16[256,1664]{1,0:T(8,128)(2,1)}, bf16[256,1664]{1,0:T(8,128)(2,1)}, u32[]{:S(2)}, u32[]{:S(2)}) collective-permute-start(bf16[256,1664]{1,0:T(8,128)(2,1)} %pad_maximum_fusion.3), channel_id=1, source_target_pairs={{0,4},{4,0},{8,12},{12,8},{16,20},{20,16},{24,28},{28,24},{1,5},{5... | collective-permute-start | bytes 2555912 | tf_op jit(solution)/shard_map/ppermute | solution.py:44
  6.7 23.1 %collective-permute-start.1 = (bf16[256,1664]{1,0:T(8,128)(2,1)}, bf16[256,1664]{1,0:T(8,128)(2,1)}, u32[]{:S(2)}, u32[]{:S(2)}) collective-permute-start(bf16[256,1664]{1,0:T(8,128)(2,1)} %pad_maximum_fusion.3), channel_id=1, source_target_pairs={{0,8},{4,12},{8,16},{12,20},{16,24},{20,28},{24,0},{28,4},{1,9},{5... | collective-permute-start | bytes 2555912 | tf_op jit(solution)/shard_map/ppermute | solution.py:49
  12.0 61.7 %collective-permute-start.5 = (bf16[3,352,2048]{2,1,0:T(8,128)(2,1)}, bf16[3,352,2048]{2,1,0:T(8,128)(2,1)}, u32[]{:S(2)}, u32[]{:S(2)}) collective-permute-start(bf16[3,352,2048]{2,1,0:T(8,128)(2,1)} %pad_maximum_fusion.1), channel_id=1, source_target_pairs={{0,1},{1,0},{2,3},{3,2},{4,5},{5,4},{6,7},{7,6},{8,9},{9,8},{10,11... | collective-permute-start | bytes 12976136 | tf_op jit(solution)/shard_map/ppermute | solution.py:54
  12.0 199.0 %collective-permute-start.20 = (bf16[3,352,2048]{2,1,0:T(8,128)(2,1)}, bf16[3,352,2048]{2,1,0:T(8,128)(2,1)}, u32[]{:S(2)}, u32[]{:S(2)}) collective-permute-start(bf16[3,352,2048]{2,1,0:T(8,128)(2,1)} %pad_maximum_fusion.1), channel_id=1, source_target_pairs={{0,2},{1,3},{2,0},{3,1},{4,6},{5,7},{6,4},{7,5},{8,10},{9,11},{10,... | collective-permute-start | bytes 12976136 | tf_op jit(solution)/shard_map/ppermute | solution.py:54
  29.8 21.3 %collective-permute-start.2 = (bf16[256,1664]{1,0:T(8,128)(2,1)}, bf16[256,1664]{1,0:T(8,128)(2,1)}, u32[]{:S(2)}, u32[]{:S(2)}) collective-permute-start(bf16[256,1664]{1,0:T(8,128)(2,1)} %collective-permute-done.1), channel_id=1, source_target_pairs={{0,4},{4,0},{8,12},{12,8},{16,20},{20,16},{24,28},{28,24},{1,5},{5... | collective-permute-start | bytes 2555912 | tf_op jit(solution)/shard_map/ppermute | solution.py:44
  30.3 22.7 %collective-permute-start.3 = (bf16[256,1664]{1,0:T(8,128)(2,1)}, bf16[256,1664]{1,0:T(8,128)(2,1)S(1)}, u32[]{:S(2)}, u32[]{:S(2)}) collective-permute-start(bf16[256,1664]{1,0:T(8,128)(2,1)} %collective-permute-done.1), channel_id=1, source_target_pairs={{0,8},{4,12},{8,16},{12,20},{16,24},{20,28},{24,0},{28,4},{1,9},{5... | collective-permute-start | bytes 2555912 | tf_op jit(solution)/shard_map/ppermute | solution.py:49
  53.0 25.6 %collective-permute-start.4 = (bf16[256,1664]{1,0:T(8,128)(2,1)S(1)}, bf16[256,1664]{1,0:T(8,128)(2,1)}, u32[]{:S(2)}, u32[]{:S(2)}) collective-permute-start(bf16[256,1664]{1,0:T(8,128)(2,1)S(1)} %collective-permute-done.3), channel_id=1, source_target_pairs={{0,4},{4,0},{8,12},{12,8},{16,20},{20,16},{24,28},{28,24},{1,5},{5... | collective-permute-start | bytes 2555912 | tf_op jit(solution)/shard_map/ppermute | solution.py:44
  54.6 24.9 %collective-permute-start.6 = (bf16[256,1664]{1,0:T(8,128)(2,1)S(1)}, bf16[256,1664]{1,0:T(8,128)(2,1)}, u32[]{:S(2)}, u32[]{:S(2)}) collective-permute-start(bf16[256,1664]{1,0:T(8,128)(2,1)S(1)} %collective-permute-done.3), channel_id=1, source_target_pairs={{0,8},{4,12},{8,16},{12,20},{16,24},{20,28},{24,0},{28,4},{1,9},{5... | collective-permute-start | bytes 2555912 | tf_op jit(solution)/shard_map/ppermute | solution.py:49
  79.4 19.8 %collective-permute-start.7 = (bf16[256,1664]{1,0:T(8,128)(2,1)}, bf16[256,1664]{1,0:T(8,128)(2,1)S(1)}, u32[]{:S(2)}, u32[]{:S(2)}) collective-permute-start(bf16[256,1664]{1,0:T(8,128)(2,1)} %collective-permute-done.6), channel_id=1, source_target_pairs={{0,4},{4,0},{8,12},{12,8},{16,20},{20,16},{24,28},{28,24},{1,5},{5... | collective-permute-start | bytes 2555912 | tf_op jit(solution)/shard_map/ppermute | solution.py:44
  99.2 23.1 %collective-permute-start.9 = (bf16[256,640]{0,1:T(8,128)(2,1)S(1)}, bf16[256,640]{0,1:T(8,128)(2,1)}, u32[]{:S(2)}, u32[]{:S(2)}) collective-permute-start(bf16[256,640]{0,1:T(8,128)(2,1)S(1)} %fusion.78), channel_id=1, source_target_pairs={{0,4},{4,0},{8,12},{12,8},{16,20},{20,16},{24,28},{28,24},{1,5},{5... | collective-permute-start | bytes 983048 | tf_op jit(solution)/shard_map/ppermute | solution.py:44
  99.7 22.7 %collective-permute-start.8 = (bf16[256,640]{0,1:T(8,128)(2,1)S(1)}, bf16[256,640]{0,1:T(8,128)(2,1)}, u32[]{:S(2)}, u32[]{:S(2)}) collective-permute-start(bf16[256,640]{0,1:T(8,128)(2,1)S(1)} %fusion.78), channel_id=1, source_target_pairs={{0,8},{4,12},{8,16},{12,20},{16,24},{20,28},{24,0},{28,4},{1,9},{5... | collective-permute-start | bytes 983048 | tf_op jit(solution)/shard_map/ppermute | solution.py:49
  107.2 70.6 %all-to-all-start = ((bf16[3,8,176,256]{3,2,0,1:T(8,128)(2,1)}), bf16[3,8,176,256]{3,2,0,1:T(8,128)(2,1)}, u32[]{:S(2)}, u32[]{:S(2)}) async-start(bf16[3,8,176,256]{3,2,0,1:T(8,128)(2,1)} %copy.190), calls=%async_computation | async-start | bytes 4325376 | tf_op jit(solution)/shard_map/all_to_all | solution.py:347
  122.4 22.3 %collective-permute-start.11 = (bf16[256,640]{0,1:T(8,128)(2,1)}, bf16[256,640]{0,1:T(8,128)(2,1)}, u32[]{:S(2)}, u32[]{:S(2)}) collective-permute-start(bf16[256,640]{0,1:T(8,128)(2,1)} %collective-permute-done.8), channel_id=1, source_target_pairs={{0,4},{4,0},{8,12},{12,8},{16,20},{20,16},{24,28},{28,24},{1,5},{5... | collective-permute-start | bytes 983048 | tf_op jit(solution)/shard_map/ppermute | solution.py:44
  124.5 31.5 %collective-permute-start.10 = (bf16[256,640]{0,1:T(8,128)(2,1)}, bf16[256,640]{0,1:T(8,128)(2,1)}, u32[]{:S(2)}, u32[]{:S(2)}) collective-permute-start(bf16[256,640]{0,1:T(8,128)(2,1)} %collective-permute-done.8), channel_id=1, source_target_pairs={{0,8},{4,12},{8,16},{12,20},{16,24},{20,28},{24,0},{28,4},{1,9},{5... | collective-permute-start | bytes 983048 | tf_op jit(solution)/shard_map/ppermute | solution.py:49
  156.0 25.1 %collective-permute-start.12 = (bf16[256,640]{0,1:T(8,128)(2,1)}, bf16[256,640]{0,1:T(8,128)(2,1)}, u32[]{:S(2)}, u32[]{:S(2)}) collective-permute-start(bf16[256,640]{0,1:T(8,128)(2,1)} %collective-permute-done.10), channel_id=1, source_target_pairs={{0,4},{4,0},{8,12},{12,8},{16,20},{20,16},{24,28},{28,24},{1,5},{5... | collective-permute-start | bytes 983048 | tf_op jit(solution)/shard_map/ppermute | solution.py:44
  157.3 23.8 %collective-permute-start.13 = (bf16[256,640]{0,1:T(8,128)(2,1)}, bf16[256,640]{0,1:T(8,128)(2,1)}, u32[]{:S(2)}, u32[]{:S(2)}) collective-permute-start(bf16[256,640]{0,1:T(8,128)(2,1)} %collective-permute-done.10), channel_id=1, source_target_pairs={{0,8},{4,12},{8,16},{12,20},{16,24},{20,28},{24,0},{28,4},{1,9},{5... | collective-permute-start | bytes 983048 | tf_op jit(solution)/shard_map/ppermute | solution.py:49
  212.8 49.8 %collective-permute-start.29 = (bf16[3,176,2048]{2,1,0:T(8,128)(2,1)}, bf16[3,176,2048]{2,1,0:T(8,128)(2,1)}, u32[]{:S(2)}, u32[]{:S(2)}) collective-permute-start(bf16[3,176,2048]{2,1,0:T(8,128)(2,1)} %bitcast.369), channel_id=1, source_target_pairs={{0,2},{1,3},{2,0},{3,1},{4,6},{5,7},{6,4},{7,5},{8,10},{9,11},{10,... | collective-permute-start | bytes 6488072 | tf_op jit(solution)/shard_map/ppermute | solution.py:54
  213.2 52.8 %collective-permute-start.30 = (bf16[3,176,2048]{2,1,0:T(8,128)(2,1)}, bf16[3,176,2048]{2,1,0:T(8,128)(2,1)}, u32[]{:S(2)}, u32[]{:S(2)}) collective-permute-start(bf16[3,176,2048]{2,1,0:T(8,128)(2,1)} %bitcast.370), channel_id=1, source_target_pairs={{0,1},{1,0},{2,3},{3,2},{4,5},{5,4},{6,7},{7,6},{8,9},{9,8},{10,11... | collective-permute-start | bytes 6488072 | tf_op jit(solution)/shard_map/ppermute | solution.py:54
  241.4 27.8 %collective-permute-start.25 = (bf16[96,2048]{1,0:T(8,128)(2,1)S(1)}, bf16[96,2048]{1,0:T(8,128)(2,1)S(1)}, u32[]{:S(2)}, u32[]{:S(2)}) collective-permute-start(bf16[96,2048]{1,0:T(8,128)(2,1)S(1)} %collective-permute-done.22), channel_id=1, source_target_pairs={{0,4},{4,0},{8,12},{12,8},{16,20},{20,16},{24,28},{28,24},{1,5},{5... | collective-permute-start | bytes 1179656 | tf_op jit(solution)/shard_map/ppermute | solution.py:44
  243.2 26.0 %collective-permute-start.24 = (bf16[96,2048]{1,0:T(8,128)(2,1)S(1)}, bf16[96,2048]{1,0:T(8,128)(2,1)S(1)}, u32[]{:S(2)}, u32[]{:S(2)}) collective-permute-start(bf16[96,2048]{1,0:T(8,128)(2,1)S(1)} %collective-permute-done.22), channel_id=1, source_target_pairs={{0,8},{4,12},{8,16},{12,20},{16,24},{20,28},{24,0},{28,4},{1,9},{5... | collective-permute-start | bytes 1179656 | tf_op jit(solution)/shard_map/ppermute | solution.py:49
  262.6 19.4 %collective-permute-start.31 = (bf16[3,176,2048]{2,1,0:T(8,128)(2,1)}, bf16[3,176,2048]{2,1,0:T(8,128)(2,1)}, u32[]{:S(2)}, u32[]{:S(2)}) collective-permute-start(bf16[3,176,2048]{2,1,0:T(8,128)(2,1)} %collective-permute-done.29), channel_id=1, source_target_pairs={{0,1},{1,0},{2,3},{3,2},{4,5},{5,4},{6,7},{7,6},{8,9},{9,8},{10,11... | collective-permute-start | bytes 6488072 | tf_op jit(solution)/shard_map/ppermute | solution.py:54
  269.5 25.2 %collective-permute-start.27 = (bf16[96,2048]{1,0:T(8,128)(2,1)S(1)}, bf16[96,2048]{1,0:T(8,128)(2,1)}, u32[]{:S(2)}, u32[]{:S(2)}) collective-permute-start(bf16[96,2048]{1,0:T(8,128)(2,1)S(1)} %constant_dynamic-slice_fusion), channel_id=1, source_target_pairs={{0,4},{4,0},{8,12},{12,8},{16,20},{20,16},{24,28},{28,24},{1,5},{5... | collective-permute-start | bytes 1179656 | tf_op jit(solution)/shard_map/ppermute | solution.py:44
  271.2 23.5 %collective-permute-start.26 = (bf16[96,2048]{1,0:T(8,128)(2,1)S(1)}, bf16[96,2048]{1,0:T(8,128)(2,1)}, u32[]{:S(2)}, u32[]{:S(2)}) collective-permute-start(bf16[96,2048]{1,0:T(8,128)(2,1)S(1)} %constant_dynamic-slice_fusion), channel_id=1, source_target_pairs={{0,8},{4,12},{8,16},{12,20},{16,24},{20,28},{24,0},{28,4},{1,9},{5... | collective-permute-start | bytes 1179656 | tf_op jit(solution)/shard_map/ppermute | solution.py:49
  330.2 29.3 %collective-permute-start.35 = (bf16[96,2048]{1,0:T(8,128)(2,1)}, bf16[96,2048]{1,0:T(8,128)(2,1)}, u32[]{:S(2)}, u32[]{:S(2)}) collective-permute-start(bf16[96,2048]{1,0:T(8,128)(2,1)} %get-tuple-element.535), channel_id=1, source_target_pairs={{0,4},{4,0},{8,12},{12,8},{16,20},{20,16},{24,28},{28,24},{1,5},{5... | collective-permute-start | bytes 1179656 | tf_op jit(solution)/shard_map/ppermute | solution.py:44
  360.7 20.3 %collective-permute-start.40 = (bf16[96,2048]{1,0:T(8,128)(2,1)S(1)}, bf16[96,2048]{1,0:T(8,128)(2,1)S(1)}, u32[]{:S(2)}, u32[]{:S(2)}) collective-permute-start(bf16[96,2048]{1,0:T(8,128)(2,1)S(1)} %add_convert_fusion.11), channel_id=1, source_target_pairs={{0,8},{4,12},{8,16},{12,20},{16,24},{20,28},{24,0},{28,4},{1,9},{5... | collective-permute-start | bytes 1179656 | tf_op jit(solution)/shard_map/ppermute | solution.py:49
  411.3 24.6 %collective-permute-start.45 = (bf16[3,352,2048]{2,1,0:T(8,128)(2,1)S(1)}, bf16[3,352,2048]{2,1,0:T(8,128)(2,1)S(1)}, u32[]{:S(2)}, u32[]{:S(2)}) collective-permute-start(bf16[3,352,2048]{2,1,0:T(8,128)(2,1)S(1)} %slice.850), channel_id=1, source_target_pairs={{0,1},{1,0},{2,3},{3,2},{4,5},{5,4},{6,7},{7,6},{8,9},{9,8},{10,11... | collective-permute-start | bytes 12976136 | tf_op jit(solution)/shard_map/ppermute | solution.py:54
  419.0 39.0 %collective-permute-start.60 = (bf16[704,2048]{1,0:T(8,128)(2,1)S(1)}, bf16[704,2048]{1,0:T(8,128)(2,1)}, u32[]{:S(2)}, u32[]{:S(2)}) collective-permute-start(bf16[704,2048]{1,0:T(8,128)(2,1)S(1)} %slice.852), channel_id=1, source_target_pairs={{0,1},{1,0},{2,3},{3,2},{4,5},{5,4},{6,7},{7,6},{8,9},{9,8},{10,11... | collective-permute-start | bytes 8650760 | tf_op jit(solution)/shard_map/ppermute | solution.py:54
  419.6 72.2 %collective-permute-start.43 = (bf16[96,2048]{1,0:T(8,128)(2,1)}, bf16[96,2048]{1,0:T(8,128)(2,1)}, u32[]{:S(2)}, u32[]{:S(2)}) collective-permute-start(bf16[96,2048]{1,0:T(8,128)(2,1)} %add_convert_fusion.9), channel_id=1, source_target_pairs={{0,8},{4,12},{8,16},{12,20},{16,24},{20,28},{24,0},{28,4},{1,9},{5... | collective-permute-start | bytes 1179656 | tf_op jit(solution)/shard_map/ppermute | solution.py:49
  438.7 47.6 %collective-permute-start.49 = (bf16[3,176,2048]{2,1,0:T(8,128)(2,1)}, bf16[3,176,2048]{2,1,0:T(8,128)(2,1)}, u32[]{:S(2)}, u32[]{:S(2)}) collective-permute-start(bf16[3,176,2048]{2,1,0:T(8,128)(2,1)} %add_convert_fusion.2), channel_id=1, source_target_pairs={{0,2},{1,3},{2,0},{3,1},{4,6},{5,7},{6,4},{7,5},{8,10},{9,11},{10,... | collective-permute-start | bytes 6488072 | tf_op jit(solution)/shard_map/ppermute | solution.py:54
  461.1 56.0 %collective-permute-start.62 = (bf16[704,2048]{1,0:T(8,128)(2,1)}, bf16[704,2048]{1,0:T(8,128)(2,1)}, u32[]{:S(2)}, u32[]{:S(2)}) collective-permute-start(bf16[704,2048]{1,0:T(8,128)(2,1)} %slice.855), channel_id=1, source_target_pairs={{0,1},{1,0},{2,3},{3,2},{4,5},{5,4},{6,7},{7,6},{8,9},{9,8},{10,11... | collective-permute-start | bytes 8650760 | tf_op jit(solution)/shard_map/ppermute | solution.py:54
  465.6 26.1 %collective-permute-start.48 = (bf16[96,2048]{1,0:T(8,128)(2,1)S(1)}, bf16[96,2048]{1,0:T(8,128)(2,1)S(1)}, u32[]{:S(2)}, u32[]{:S(2)}) collective-permute-start(bf16[96,2048]{1,0:T(8,128)(2,1)S(1)} %copy-done.36), channel_id=1, source_target_pairs={{0,4},{4,0},{8,12},{12,8},{16,20},{20,16},{24,28},{28,24},{1,5},{5... | collective-permute-start | bytes 1179656 | tf_op jit(solution)/shard_map/ppermute | solution.py:44
  470.8 21.0 %collective-permute-start.52 = (bf16[96,2048]{1,0:T(8,128)(2,1)S(1)}, bf16[96,2048]{1,0:T(8,128)(2,1)S(1)}, u32[]{:S(2)}, u32[]{:S(2)}) collective-permute-start(bf16[96,2048]{1,0:T(8,128)(2,1)S(1)} %add_convert_fusion.6), channel_id=1, source_target_pairs={{0,8},{4,12},{8,16},{12,20},{16,24},{20,28},{24,0},{28,4},{1,9},{5... | collective-permute-start | bytes 1179656 | tf_op jit(solution)/shard_map/ppermute | solution.py:49
  496.8 19.1 %collective-permute-start.53 = (bf16[96,2048]{1,0:T(8,128)(2,1)}, bf16[96,2048]{1,0:T(8,128)(2,1)S(1)}, u32[]{:S(2)}, u32[]{:S(2)}) collective-permute-start(bf16[96,2048]{1,0:T(8,128)(2,1)} %get-tuple-element.513), channel_id=1, source_target_pairs={{0,2},{1,3},{2,0},{3,1},{4,6},{5,7},{6,4},{7,5},{8,10},{9,11},{10,... | collective-permute-start | bytes 1179656 | tf_op jit(solution)/shard_map/ppermute | solution.py:54
  497.1 112.8 %all-to-all-start.1 = ((bf16[3,8,176,256]{3,2,0,1:T(8,128)(2,1)}), bf16[3,8,176,256]{3,2,0,1:T(8,128)(2,1)}, u32[]{:S(2)}, u32[]{:S(2)}) async-start(bf16[3,8,176,256]{3,2,0,1:T(8,128)(2,1)} %bitcast.358), calls=%async_computation.1 | async-start | bytes 4325376 | tf_op jit(solution)/shard_map/all_to_all | solution.py:609
  513.5 48.1 %collective-permute-start.63 = (bf16[704,2048]{1,0:T(8,128)(2,1)}, bf16[704,2048]{1,0:T(8,128)(2,1)}, u32[]{:S(2)}, u32[]{:S(2)}) collective-permute-start(bf16[704,2048]{1,0:T(8,128)(2,1)} %slice.857), channel_id=1, source_target_pairs={{0,1},{1,0},{2,3},{3,2},{4,5},{5,4},{6,7},{7,6},{8,9},{9,8},{10,11... | collective-permute-start | bytes 8650760 | tf_op jit(solution)/shard_map/ppermute | solution.py:54
  531.5 25.2 %collective-permute-start.56 = (bf16[96,2048]{1,0:T(8,128)(2,1)S(1)}, bf16[96,2048]{1,0:T(8,128)(2,1)}, u32[]{:S(2)}, u32[]{:S(2)}) collective-permute-start(bf16[96,2048]{1,0:T(8,128)(2,1)S(1)} %get-tuple-element.381), channel_id=1, source_target_pairs={{0,2},{1,3},{2,0},{3,1},{4,6},{5,7},{6,4},{7,5},{8,10},{9,11},{10,... | collective-permute-start | bytes 1179656 | tf_op jit(solution)/shard_map/ppermute | solution.py:54
  533.3 25.3 %collective-permute-start.57 = (bf16[96,2048]{1,0:T(8,128)(2,1)S(1)}, bf16[96,2048]{1,0:T(8,128)(2,1)}, u32[]{:S(2)}, u32[]{:S(2)}) collective-permute-start(bf16[96,2048]{1,0:T(8,128)(2,1)S(1)} %get-tuple-element.381), channel_id=1, source_target_pairs={{0,1},{1,0},{2,3},{3,2},{4,5},{5,4},{6,7},{7,6},{8,9},{9,8},{10,11... | collective-permute-start | bytes 1179656 | tf_op jit(solution)/shard_map/ppermute | solution.py:54
  544.8 134.0 %collective-permute-start.86 = (bf16[352,2048]{1,0:T(8,128)(2,1)}, bf16[352,2048]{1,0:T(8,128)(2,1)}, u32[]{:S(2)}, u32[]{:S(2)}) collective-permute-start(bf16[352,2048]{1,0:T(8,128)(2,1)} %add_convert_fusion.5), channel_id=1, source_target_pairs={{0,2},{1,3},{2,0},{3,1},{4,6},{5,7},{6,4},{7,5},{8,10},{9,11},{10,... | collective-permute-start | bytes 4325384 | tf_op jit(solution)/shard_map/ppermute | solution.py:54
  552.2 19.2 %collective-permute-start.81 = (bf16[256,640]{0,1:T(8,128)(2,1)S(1)}, bf16[256,640]{0,1:T(8,128)(2,1)S(1)}, u32[]{:S(2)}, u32[]{:S(2)}) collective-permute-start(bf16[256,640]{0,1:T(8,128)(2,1)S(1)} %fusion.72), channel_id=1, source_target_pairs={{0,8},{4,12},{8,16},{12,20},{16,24},{20,28},{24,0},{28,4},{1,9},{5... | collective-permute-start | bytes 983048 | tf_op jit(solution)/shard_map/ppermute | solution.py:49
  560.5 118.2 %collective-permute-start.87 = (bf16[352,2048]{1,0:T(8,128)(2,1)}, bf16[352,2048]{1,0:T(8,128)(2,1)}, u32[]{:S(2)}, u32[]{:S(2)}) collective-permute-start(bf16[352,2048]{1,0:T(8,128)(2,1)} %add_convert_fusion.4), channel_id=1, source_target_pairs={{0,2},{1,3},{2,0},{3,1},{4,6},{5,7},{6,4},{7,5},{8,10},{9,11},{10,... | collective-permute-start | bytes 4325384 | tf_op jit(solution)/shard_map/ppermute | solution.py:54
  588.6 21.2 %collective-permute-start.67 = (bf16[256,1536]{1,0:T(8,128)(2,1)S(1)}, bf16[256,1536]{1,0:T(8,128)(2,1)}, u32[]{:S(2)}, u32[]{:S(2)}) collective-permute-start(bf16[256,1536]{1,0:T(8,128)(2,1)S(1)} %get-tuple-element.527), channel_id=1, source_target_pairs={{0,4},{4,0},{8,12},{12,8},{16,20},{20,16},{24,28},{28,24},{1,5},{5... | collective-permute-start | bytes 2359304 | tf_op jit(solution)/shard_map/ppermute | solution.py:44
  593.5 20.3 %collective-permute-start.64 = (bf16[96,2048]{1,0:T(8,128)(2,1)S(1)}, bf16[96,2048]{1,0:T(8,128)(2,1)}, u32[]{:S(2)}, u32[]{:S(2)}) collective-permute-start(bf16[96,2048]{1,0:T(8,128)(2,1)S(1)} %get-tuple-element.550), channel_id=1, source_target_pairs={{0,1},{1,0},{2,3},{3,2},{4,5},{5,4},{6,7},{7,6},{8,9},{9,8},{10,11... | collective-permute-start | bytes 1179656 | tf_op jit(solution)/shard_map/ppermute | solution.py:54
  612.3 40.4 %collective-permute-start.74 = (bf16[256,1536]{1,0:T(8,128)(2,1)}, bf16[256,1536]{1,0:T(8,128)(2,1)}, u32[]{:S(2)}, u32[]{:S(2)}) collective-permute-start(bf16[256,1536]{1,0:T(8,128)(2,1)} %fusion.28), channel_id=1, source_target_pairs={{0,8},{4,12},{8,16},{12,20},{16,24},{20,28},{24,0},{28,4},{1,9},{5... | collective-permute-start | bytes 2359304 | tf_op jit(solution)/shard_map/ppermute | solution.py:49
  632.6 20.2 %collective-permute-start.71 = (bf16[256,1536]{1,0:T(8,128)(2,1)}, bf16[256,1536]{1,0:T(8,128)(2,1)S(1)}, u32[]{:S(2)}, u32[]{:S(2)}) collective-permute-start(bf16[256,1536]{1,0:T(8,128)(2,1)} %get-tuple-element.408), channel_id=1, source_target_pairs={{0,4},{4,0},{8,12},{12,8},{16,20},{20,16},{24,28},{28,24},{1,5},{5... | collective-permute-start | bytes 2359304 | tf_op jit(solution)/shard_map/ppermute | solution.py:44
  633.9 44.8 %collective-permute-start.88 = (bf16[352,2048]{1,0:T(8,128)(2,1)S(1)}, bf16[352,2048]{1,0:T(8,128)(2,1)S(1)}, u32[]{:S(2)}, u32[]{:S(2)}) collective-permute-start(bf16[352,2048]{1,0:T(8,128)(2,1)S(1)} %copy-done.27), channel_id=1, source_target_pairs={{0,2},{1,3},{2,0},{3,1},{4,6},{5,7},{6,4},{7,5},{8,10},{9,11},{10,... | collective-permute-start | bytes 4325384 | tf_op jit(solution)/shard_map/ppermute | solution.py:54
  652.7 20.0 %collective-permute-start.72 = (bf16[256,1536]{1,0:T(8,128)(2,1)S(1)}, bf16[256,1536]{1,0:T(8,128)(2,1)S(1)}, u32[]{:S(2)}, u32[]{:S(2)}) collective-permute-start(bf16[256,1536]{1,0:T(8,128)(2,1)S(1)} %copy-done.34), channel_id=1, source_target_pairs={{0,4},{4,0},{8,12},{12,8},{16,20},{20,16},{24,28},{28,24},{1,5},{5... | collective-permute-start | bytes 2359304 | tf_op jit(solution)/shard_map/ppermute | solution.py:44
  655.8 21.5 %collective-permute-start.75 = (bf16[256,1536]{1,0:T(8,128)(2,1)S(1)}, bf16[256,1536]{1,0:T(8,128)(2,1)S(1)}, u32[]{:S(2)}, u32[]{:S(2)}) collective-permute-start(bf16[256,1536]{1,0:T(8,128)(2,1)S(1)} %fusion.24), channel_id=1, source_target_pairs={{0,8},{4,12},{8,16},{12,20},{16,24},{20,28},{24,0},{28,4},{1,9},{5... | collective-permute-start | bytes 2359304 | tf_op jit(solution)/shard_map/ppermute | solution.py:49
  678.7 20.6 %collective-permute-start.76 = (bf16[256,1536]{1,0:T(8,128)(2,1)S(1)}, bf16[256,1536]{1,0:T(8,128)(2,1)S(1)}, u32[]{:S(2)}, u32[]{:S(2)}) collective-permute-start(bf16[256,1536]{1,0:T(8,128)(2,1)S(1)} %fusion.26), channel_id=1, source_target_pairs={{0,8},{4,12},{8,16},{12,20},{16,24},{20,28},{24,0},{28,4},{1,9},{5... | collective-permute-start | bytes 2359304 | tf_op jit(solution)/shard_map/ppermute | solution.py:49
  (126 other events, 1576.8 us)

commit v5 on v4

--- a/solution.py
+++ b/solution.py
@@ -279,6 +279,8 @@
     high = dense.astype(BF)
     low = (dense - high.astype(F32)).astype(BF)
     packed = jnp.concatenate([high.reshape(-1), low.reshape(-1)]).reshape(-1, shard_rows)
+    spare = jnp.concatenate([jnp.stack([second_gain, shared_logit]), packed])
+    spare = jnp.pad(spare, ((0, -spare.shape[0] % 16), (0, 0)))
     first = jnp.pad(first_gain[:, None], ((0, 0), (0, 127)))
     projection = jnp.concatenate([query_weight, key_weight, value_weight, first], axis=1)
 
@@ -339,8 +341,6 @@
 
         return run
 
-    spare = jnp.concatenate([jnp.stack([second_gain, shared_logit]), packed]).T
-    spare = jnp.pad(spare, ((0, 0), (0, -spare.shape[1] % 128)))
     half = local_heads // 2
 
     shared = jnp.stack([shared_gate.T, shared_up.T, shared_down]).reshape(3, groups, piece, -1)
@@ -353,18 +353,19 @@
         return done, after(shared.transpose(0, 2, 1, 3).reshape(3, piece, width), block)
 
     blocks, done = gather_ep(
-        after(jnp.concatenate([output_weight.T, spare], axis=1), qkv_blocks[-1]),
+        after(jnp.concatenate([output_weight, spare]), qkv_blocks[-1]),
         [project, attend(range(half)), attend_last],
     )
     shared = done[2][1]
     x_shared = swap_tp(shared, 2)
     qkv = projected[0]
     query, key, value = qkv[:, :wide], qkv[:, wide : 2 * wide], qkv[:, 2 * wide :]
-    spare = stack_absolute([block[:, wide:] for block in blocks])
-    w_out = stack_absolute([block[:, :wide] for block in blocks]).reshape(width, -1)
-    vectors = spare[:, :, :2].reshape(width, 2).T.astype(F32)
-    gain_two32, logit32 = vectors[0:1], vectors[1:2]
-    packed = spare[:, :, 2 : 2 + packed.shape[0]].transpose(0, 2, 1)
+    spare = stack_absolute([block[wide:] for block in blocks])
+    w_out = stack_absolute([block[:wide] for block in blocks])
+    w_out = w_out.transpose(0, 2, 1).reshape(width, wide)
+    gain_two32 = spare[:, 0].reshape(1, width).astype(F32)
+    logit32 = spare[:, 1].reshape(1, width).astype(F32)
+    packed = spare[:, 2 : 2 + packed.shape[0]]
     packed = packed.reshape(groups, 2, part, groups).astype(F32).sum(axis=1)
     chosen = jnp.arange(groups, dtype=jnp.int32)
     gates = jnp.sum(jnp.where(chosen == me_ep, packed, 0.0), axis=2)
@@ -389,7 +390,7 @@
         return [(0, shared), (1, x_part), (2, swap_tp(shared, 1)), (3, swap_tp(x_part, 1))]
 
     act_blocks, done = gather_ep(act2, [far_units])
-    units = place(done[0], shared_units(act_blocks[4 if len(act_blocks) > 4 else -1]), routed)
+    units = place(done[0], shared_units(act_blocks[-1]), routed)
     act_all = stack_static(act_blocks).reshape(groups * part, width)
     gout_own = after(own(block_grad), act_blocks[-2])
 

time: 722 us -> 713 us (0.988)
  waiting for transfers between devices: 222 us -> 201 us
    ppermute x35, waiting for transfers between devices: 67.6 us -> 51.1 us  [swap_tp(): return lax.ppermute(value, 'tp', [(i, i ^ mask) for i in range(size)])]
    ppermute x32, waiting for transfers between devices: 114 us -> 99.1 us  [swap_inner(): return lax.ppermute(value, 'ep', [(i, i ^ 1) for i in range(size)])]
    ppermute x24, waiting for transfers between devices: 40.8 us -> 50.9 us  [ring_outer(): return lax.ppermute(value, 'ep', [(i, (i + 2) % size) for i in range(size)])]
    broadcast_in_dim x30 -> x32, local copies, waits for them, and re-layouts: 16.7 us -> 19.1 us  [put(): return lax.dynamic_update_index_in_dim(array, value, index, 0)]
  transfers between devices with their start and end apart: 93 -> 93, of which waited for: 36 -> 36; matrix products, arithmetic and copies ran while one was open for 50% -> 52% of each run, Pallas kernels for 0% -> 0%
where the time goes in v5:
time: 713 us; the launch traced here: 701 us
  waiting for transfers between devices  201 us (28%)
  local copies, waits for them, and re-layouts  166 us (23%)
  matrix products  143 us (20%)
  starting transfers between devices  101 us (14%)
  other arithmetic  85.9 us (12%)
    ppermute x32, waiting for transfers between devices, swap_inner(): return lax.ppermute(value, 'ep', [(i, i ^ 1) for i in range(size)])  99.1 us
    dot_general x17, matrix products, nt(): lax.dot_general(left, right, (((1,), (1,)), ((), ())), preferred_element_...  53.8 us
    ppermute x35, waiting for transfers between devices, swap_tp(): return lax.ppermute(value, 'tp', [(i, i ^ mask) for i in range(size)])  51.1 us
    ppermute x24, waiting for transfers between devices, ring_outer(): return lax.ppermute(value, 'ep', [(i, (i + 2) % size) for i in range(size)])  50.9 us
    dynamic_update_slice x42, local copies, waits for them, and re-layouts, put(): return lax.dynamic_update_index_in_dim(array, value, index, 0)  47.4 us
    dot_general x13, matrix products, nn(): lax.dot_general(left, right, (((1,), (0,)), ((), ())), preferred_element_...  47.3 us
    dot_general x16, matrix products, tn(): lax.dot_general(left, right, (((0,), (0,)), ((), ())), preferred_element_...  41.5 us
    ppermute x32, starting transfers between devices, swap_inner(): return lax.ppermute(value, 'ep', [(i, i ^ 1) for i in range(size)])  38.3 us
  transfers between devices with their start and end apart: 93, of which 36 were waited for; matrix products, arithmetic and copies ran while one was open for 52% of the time, Pallas kernels for 0%

profile of v5, /device:TPU:0, one launch (start us, length us, event | category | flops | bytes accessed | tf_op | source)
XLA Modules:
  0.0 701.2 jit_solution(10730170315965935781)
XLA Ops:
  8.3 3.7 pad_maximum_fusion.1
  44.2 9.6 %collective-permute-done.2 = bf16[256,1664]{1,0:T(8,128)(2,1)} collective-permute-done((bf16[256,1664]{1,0:T(8,128)(2,1)}, bf16[256,1664]{1,0:T(8,128)(2,1)}, u32[]{:S(2)}, u32[]{:S(2)}) %collective-permute-start.2) | collective-permute-done | bytes 852000 | tf_op jit(solution)/shard_map/ppermute | solution.py:44
  64.9 8.9 %broadcast_in_dim.264 = bf16[3,2112,2048]{2,1,0:T(8,128)(2,1)} broadcast(bf16[]{:T(256)} %constant.751.clone.1), dimensions={} | broadcast | bytes 25952258 | tf_op jit(solution)/shard_map/broadcast_in_dim | solution.py:300
  73.8 4.8 constant_dynamic-update-slice_fusion.38
  78.6 4.9 constant_dynamic-update-slice_fusion.37
  95.2 9.0 %collective-permute-done.7 = bf16[256,1664]{1,0:T(8,128)(2,1)S(1)} collective-permute-done((bf16[256,1664]{1,0:T(8,128)(2,1)}, bf16[256,1664]{1,0:T(8,128)(2,1)S(1)}, u32[]{:S(2)}, u32[]{:S(2)}) %collective-permute-start.7) | collective-permute-done | bytes 852000 | tf_op jit(solution)/shard_map/ppermute | solution.py:44
  113.6 5.1 all-to-all-start
  119.8 5.9 convolution_convert_fusion.9
  150.4 10.7 %collective-permute-done.10 = bf16[528,256]{1,0:T(8,128)(2,1)} collective-permute-done((bf16[528,256]{1,0:T(8,128)(2,1)}, bf16[528,256]{1,0:T(8,128)(2,1)}, u32[]{:S(2)}, u32[]{:S(2)}) %collective-permute-start.10) | collective-permute-done | bytes 270368 | tf_op jit(solution)/shard_map/ppermute | solution.py:49
  162.4 9.2 %collective-permute-start.13 = (bf16[528,256]{1,0:T(8,128)(2,1)}, bf16[528,256]{1,0:T(8,128)(2,1)}, u32[]{:S(2)}, u32[]{:S(2)}) collective-permute-start(bf16[528,256]{1,0:T(8,128)(2,1)} %collective-permute-done.10), channel_id=1, source_target_pairs={{0,8},{4,12},{8,16},{12,20},{16,24},{20,28},{24,0},{28,4},{1,9},{5... | collective-permute-start | bytes 811016 | tf_op jit(solution)/shard_map/ppermute | solution.py:49
  187.6 4.1 collective-permute-done.14
  198.7 9.9 %collective-permute-done.17 = bf16[96,2048]{1,0:T(8,128)(2,1)S(1)} collective-permute-done((bf16[96,2048]{1,0:T(8,128)(2,1)S(1)}, bf16[96,2048]{1,0:T(8,128)(2,1)S(1)}, u32[]{:S(2)}, u32[]{:S(2)}) %collective-permute-start.17) | collective-permute-done | bytes 393248 | tf_op jit(solution)/shard_map/ppermute | solution.py:54
  219.0 4.9 constant_dynamic-update-slice_fusion.20
  224.2 5.0 constant_dynamic-update-slice_fusion.19
  233.5 8.3 %collective-permute-done.22 = bf16[96,2048]{1,0:T(8,128)(2,1)S(1)} collective-permute-done((bf16[96,2048]{1,0:T(8,128)(2,1)S(1)}, bf16[96,2048]{1,0:T(8,128)(2,1)S(1)}, u32[]{:S(2)}, u32[]{:S(2)}) %collective-permute-start.22) | collective-permute-done | bytes 393248 | tf_op jit(solution)/shard_map/ppermute | solution.py:49
  243.5 9.8 %collective-permute-done.24 = bf16[96,2048]{1,0:T(8,128)(2,1)S(1)} collective-permute-done((bf16[96,2048]{1,0:T(8,128)(2,1)S(1)}, bf16[96,2048]{1,0:T(8,128)(2,1)S(1)}, u32[]{:S(2)}, u32[]{:S(2)}) %collective-permute-start.24) | collective-permute-done | bytes 393248 | tf_op jit(solution)/shard_map/ppermute | solution.py:49
  255.8 6.9 collective-permute-done.29
  278.0 9.5 %fusion.1 = f32[768,2112]{0,1:T(8,128)S(1)} fusion(bf16[768,2048]{1,0:T(8,128)(2,1)S(1)} %bitcast.358, bf16[3,2112,2048]{2,1,0:T(8,128)(2,1)} %constant_dynamic-update-slice_fusion.15), kind=kOutput, calls=%fused_computation.7 | convolution fusion | flops 6643777536 | bytes 18284544 | tf_op jit(solution)/shard_map/dot_general | solution.py:17
  291.3 12.1 %fusion.6 = (bf16[768,2112]{0,1:T(8,128)(2,1)S(1)}, f32[768,2112]{0,1:T(8,128)}) fusion(f32[768,2112]{0,1:T(8,128)S(1)} %fusion.1, f32[768]{0:T(1024)S(1)} %div.65, f32[768]{0:T(1024)S(1)} %copy-done.73, pred[2112]{0:T(1024)(128)(4,1)S(1)} %copy-done.74, bf16[768,2048]{1,0:T(8,128)(2,1)S(1)} %bitcast.359, ...), kind=kOutput, calls=%fused_computation.16 | convolution fusion | flops 6656753664 | bytes 28024896 | tf_op jit(solution)/shard_map/dot_general | solution.py:17
  306.2 10.0 %fusion.8 = bf16[768,2048]{1,0:T(8,128)(2,1)S(1)} fusion(bf16[768,2112]{0,1:T(8,128)(2,1)S(1)} %get-tuple-element.367, bf16[3,2112,2048]{2,1,0:T(8,128)(2,1)} %constant_dynamic-update-slice_fusion.15), kind=kOutput, calls=%fused_computation.31 | convolution fusion | flops 6645350400 | bytes 15040512 | tf_op jit(solution)/shard_map/dot_general | solution.py:13
  323.9 8.1 %collective-permute-done.37 = bf16[96,2048]{1,0:T(8,128)(2,1)S(1)} collective-permute-done((bf16[96,2048]{1,0:T(8,128)(2,1)S(1)}, bf16[96,2048]{1,0:T(8,128)(2,1)S(1)}, u32[]{:S(2)}, u32[]{:S(2)}) %collective-permute-start.37) | collective-permute-done | bytes 393248 | tf_op jit(solution)/shard_map/ppermute | solution.py:44
  332.8 18.1 %multiply_convert_fusion = (bf16[768,2112]{0,1:T(8,128)(2,1)}, bf16[768,2112]{0,1:T(8,128)(2,1)}, f32[768,2112]{0,1:T(8,128)}, f32[768,2112]{0,1:T(8,128)}) fusion(f32[768,2112]{0,1:T(8,128)} %copy-done.36, f32[768]{0:T(1024)S(1)} %div.65, f32[768]{0:T(1024)S(1)} %copy-done.73, pred[2112]{0:T(1024)(128)(4,1)} %iota_compare_fusion.4, ...), kind=kOutput, calls=%fused_computation.17 | convolution fusion | flops 6668107776 | bytes 44246016 | tf_op jit(solution)/shard_map/dot_general | solution.py:17
  353.3 11.2 %fusion = f32[768,2048]{1,0:T(8,128)S(1)} fusion(bf16[768,2112]{0,1:T(8,128)(2,1)} %get-tuple-element.360, bf16[3,2112,2048]{2,1,0:T(8,128)(2,1)} %constant_dynamic-update-slice_fusion.15), kind=kOutput, calls=%fused_computation.6 | convolution fusion | flops 6643777536 | bytes 18186240 | tf_op jit(solution)/shard_map/dot_general | solution.py:13
  366.3 4.1 fusion.21
  377.6 11.7 %add_convert_fusion = bf16[768,2048]{1,0:T(8,128)(2,1)} fusion(f32[768,2048]{1,0:T(8,128)S(1)} %fusion, bf16[768,2112]{0,1:T(8,128)(2,1)S(1)} %copy-done.82, bf16[3,2112,2048]{2,1,0:T(8,128)(2,1)} %constant_dynamic-update-slice_fusion.15, f32[2048]{0:T(1024)S(1)} %bitcast.394, f32[768]{0:T(1024)S(1)} %fusion.121), kind=kOutput, calls=%fused_computation.21 | convolution fusion | flops 6650068992 | bytes 21343232 | tf_op jit(solution)/shard_map/dot_general | solution.py:13
  391.2 3.7 fusion.12
  397.4 5.7 fusion.14
  405.5 6.5 convolution_convert_fusion.3
  417.7 8.4 %collective-permute-done.41 = bf16[96,2048]{1,0:T(8,128)(2,1)S(1)} collective-permute-done((bf16[96,2048]{1,0:T(8,128)(2,1)S(1)}, bf16[96,2048]{1,0:T(8,128)(2,1)S(1)}, u32[]{:S(2)}, u32[]{:S(2)}) %collective-permute-start.41) | collective-permute-done | bytes 393248 | tf_op jit(solution)/shard_map/ppermute | solution.py:44
  435.2 6.5 convolution_convert_fusion.2
  455.5 3.4 collective-permute-done.51
  460.4 15.8 %collective-permute-done.49 = bf16[3,176,2048]{2,1,0:T(8,128)(2,1)} collective-permute-done((bf16[3,176,2048]{2,1,0:T(8,128)(2,1)}, bf16[3,176,2048]{2,1,0:T(8,128)(2,1)}, u32[]{:S(2)}, u32[]{:S(2)}) %collective-permute-start.49) | collective-permute-done | bytes 2162720 | tf_op jit(solution)/shard_map/ppermute | solution.py:54
  476.1 3.9 add_convert_fusion.1
  488.1 4.6 all-to-all-start.1
  492.7 7.2 %convolution_convert_fusion.1 = bf16[1408,2048]{1,0:T(8,128)(2,1)S(1)} fusion(bf16[768,2048]{1,0:T(8,128)(2,1)} %bitcast.87, bf16[768,2112]{0,1:T(8,128)(2,1)} %copy-done.81), kind=kOutput, calls=%fused_computation.13 | convolution fusion | flops 4432068608 | bytes 11075584 | tf_op jit(solution)/shard_map/dot_general | solution.py:21
  508.0 3.5 add_convert_fusion.4
  536.6 4.0 collective-permute-done.59
  552.7 3.6 add_convert_fusion.3
  556.7 3.7 convolution_convert_fusion
  564.1 5.4 convolution_convert_fusion.8
  575.6 4.2 collective-permute-done.80
  587.7 10.7 %collective-permute-done.85 = f32[256,2]{0,1:T(2,128)S(1)} collective-permute-done((f32[256,2]{0,1:T(2,128)S(1)}, f32[256,2]{0,1:T(2,128)S(1)}, u32[]{:S(2)}, u32[]{:S(2)}) %collective-permute-start.85) | collective-permute-done | bytes 2080 | tf_op jit(solution)/shard_map/ppermute | solution.py:54
  604.3 3.7 collective-permute-done.66
  625.9 16.6 %collective-permute-done.71 = bf16[256,1536]{1,0:T(8,128)(2,1)S(1)} collective-permute-done((bf16[256,1536]{1,0:T(8,128)(2,1)}, bf16[256,1536]{1,0:T(8,128)(2,1)S(1)}, u32[]{:S(2)}, u32[]{:S(2)}) %collective-permute-start.71) | collective-permute-done | bytes 786464 | tf_op jit(solution)/shard_map/ppermute | solution.py:44
  648.7 13.7 %collective-permute-done.72 = bf16[256,1536]{1,0:T(8,128)(2,1)S(1)} collective-permute-done((bf16[256,1536]{1,0:T(8,128)(2,1)S(1)}, bf16[256,1536]{1,0:T(8,128)(2,1)S(1)}, u32[]{:S(2)}, u32[]{:S(2)}) %collective-permute-start.72) | collective-permute-done | bytes 786464 | tf_op jit(solution)/shard_map/ppermute | solution.py:44
  670.9 10.6 %collective-permute-done.73 = bf16[256,1536]{1,0:T(8,128)(2,1)S(1)} collective-permute-done((bf16[256,1536]{1,0:T(8,128)(2,1)S(1)}, bf16[256,1536]{1,0:T(8,128)(2,1)S(1)}, u32[]{:S(2)}, u32[]{:S(2)}) %collective-permute-start.73) | collective-permute-done | bytes 786464 | tf_op jit(solution)/shard_map/ppermute | solution.py:44
  681.5 7.3 %collective-permute-done.76 = bf16[256,1536]{1,0:T(8,128)(2,1)S(1)} collective-permute-done((bf16[256,1536]{1,0:T(8,128)(2,1)S(1)}, bf16[256,1536]{1,0:T(8,128)(2,1)S(1)}, u32[]{:S(2)}, u32[]{:S(2)}) %collective-permute-start.76) | collective-permute-done | bytes 786464 | tf_op jit(solution)/shard_map/ppermute | solution.py:49
  690.5 6.1 fusion.15
  (603 shorter events, 332.4 us)
Async XLA Ops:
  3.7 28.8 %collective-permute-start = (bf16[256,1664]{1,0:T(8,128)(2,1)}, bf16[256,1664]{1,0:T(8,128)(2,1)}, u32[]{:S(2)}, u32[]{:S(2)}) collective-permute-start(bf16[256,1664]{1,0:T(8,128)(2,1)} %pad_maximum_fusion.3), channel_id=1, source_target_pairs={{0,4},{4,0},{8,12},{12,8},{16,20},{20,16},{24,28},{28,24},{1,5},{5... | collective-permute-start | bytes 2555912 | tf_op jit(solution)/shard_map/ppermute | solution.py:44
  6.7 25.8 %collective-permute-start.1 = (bf16[256,1664]{1,0:T(8,128)(2,1)}, bf16[256,1664]{1,0:T(8,128)(2,1)}, u32[]{:S(2)}, u32[]{:S(2)}) collective-permute-start(bf16[256,1664]{1,0:T(8,128)(2,1)} %pad_maximum_fusion.3), channel_id=1, source_target_pairs={{0,8},{4,12},{8,16},{12,20},{16,24},{20,28},{24,0},{28,4},{1,9},{5... | collective-permute-start | bytes 2555912 | tf_op jit(solution)/shard_map/ppermute | solution.py:49
  12.0 66.6 %collective-permute-start.5 = (bf16[3,352,2048]{2,1,0:T(8,128)(2,1)}, bf16[3,352,2048]{2,1,0:T(8,128)(2,1)}, u32[]{:S(2)}, u32[]{:S(2)}) collective-permute-start(bf16[3,352,2048]{2,1,0:T(8,128)(2,1)} %pad_maximum_fusion.1), channel_id=1, source_target_pairs={{0,1},{1,0},{2,3},{3,2},{4,5},{5,4},{6,7},{7,6},{8,9},{9,8},{10,11... | collective-permute-start | bytes 12976136 | tf_op jit(solution)/shard_map/ppermute | solution.py:54
  12.0 199.1 %collective-permute-start.20 = (bf16[3,352,2048]{2,1,0:T(8,128)(2,1)}, bf16[3,352,2048]{2,1,0:T(8,128)(2,1)}, u32[]{:S(2)}, u32[]{:S(2)}) collective-permute-start(bf16[3,352,2048]{2,1,0:T(8,128)(2,1)} %pad_maximum_fusion.1), channel_id=1, source_target_pairs={{0,2},{1,3},{2,0},{3,1},{4,6},{5,7},{6,4},{7,5},{8,10},{9,11},{10,... | collective-permute-start | bytes 12976136 | tf_op jit(solution)/shard_map/ppermute | solution.py:54
  32.5 21.3 %collective-permute-start.2 = (bf16[256,1664]{1,0:T(8,128)(2,1)}, bf16[256,1664]{1,0:T(8,128)(2,1)}, u32[]{:S(2)}, u32[]{:S(2)}) collective-permute-start(bf16[256,1664]{1,0:T(8,128)(2,1)} %collective-permute-done.1), channel_id=1, source_target_pairs={{0,4},{4,0},{8,12},{12,8},{16,20},{20,16},{24,28},{28,24},{1,5},{5... | collective-permute-start | bytes 2555912 | tf_op jit(solution)/shard_map/ppermute | solution.py:44
  33.0 22.7 %collective-permute-start.3 = (bf16[256,1664]{1,0:T(8,128)(2,1)}, bf16[256,1664]{1,0:T(8,128)(2,1)S(1)}, u32[]{:S(2)}, u32[]{:S(2)}) collective-permute-start(bf16[256,1664]{1,0:T(8,128)(2,1)} %collective-permute-done.1), channel_id=1, source_target_pairs={{0,8},{4,12},{8,16},{12,20},{16,24},{20,28},{24,0},{28,4},{1,9},{5... | collective-permute-start | bytes 2555912 | tf_op jit(solution)/shard_map/ppermute | solution.py:49
  55.7 27.8 %collective-permute-start.4 = (bf16[256,1664]{1,0:T(8,128)(2,1)S(1)}, bf16[256,1664]{1,0:T(8,128)(2,1)}, u32[]{:S(2)}, u32[]{:S(2)}) collective-permute-start(bf16[256,1664]{1,0:T(8,128)(2,1)S(1)} %collective-permute-done.3), channel_id=1, source_target_pairs={{0,4},{4,0},{8,12},{12,8},{16,20},{20,16},{24,28},{28,24},{1,5},{5... | collective-permute-start | bytes 2555912 | tf_op jit(solution)/shard_map/ppermute | solution.py:44
  57.3 27.2 %collective-permute-start.6 = (bf16[256,1664]{1,0:T(8,128)(2,1)S(1)}, bf16[256,1664]{1,0:T(8,128)(2,1)}, u32[]{:S(2)}, u32[]{:S(2)}) collective-permute-start(bf16[256,1664]{1,0:T(8,128)(2,1)S(1)} %collective-permute-done.3), channel_id=1, source_target_pairs={{0,8},{4,12},{8,16},{12,20},{16,24},{20,28},{24,0},{28,4},{1,9},{5... | collective-permute-start | bytes 2555912 | tf_op jit(solution)/shard_map/ppermute | solution.py:49
  84.4 19.8 %collective-permute-start.7 = (bf16[256,1664]{1,0:T(8,128)(2,1)}, bf16[256,1664]{1,0:T(8,128)(2,1)S(1)}, u32[]{:S(2)}, u32[]{:S(2)}) collective-permute-start(bf16[256,1664]{1,0:T(8,128)(2,1)} %collective-permute-done.6), channel_id=1, source_target_pairs={{0,4},{4,0},{8,12},{12,8},{16,20},{20,16},{24,28},{28,24},{1,5},{5... | collective-permute-start | bytes 2555912 | tf_op jit(solution)/shard_map/ppermute | solution.py:44
  104.2 24.5 %collective-permute-start.9 = (bf16[528,256]{1,0:T(8,128)(2,1)S(1)}, bf16[528,256]{1,0:T(8,128)(2,1)}, u32[]{:S(2)}, u32[]{:S(2)}) collective-permute-start(bf16[528,256]{1,0:T(8,128)(2,1)S(1)} %pad_maximum_fusion.5), channel_id=1, source_target_pairs={{0,4},{4,0},{8,12},{12,8},{16,20},{20,16},{24,28},{28,24},{1,5},{5... | collective-permute-start | bytes 811016 | tf_op jit(solution)/shard_map/ppermute | solution.py:44
  104.7 24.0 %collective-permute-start.8 = (bf16[528,256]{1,0:T(8,128)(2,1)S(1)}, bf16[528,256]{1,0:T(8,128)(2,1)}, u32[]{:S(2)}, u32[]{:S(2)}) collective-permute-start(bf16[528,256]{1,0:T(8,128)(2,1)S(1)} %pad_maximum_fusion.5), channel_id=1, source_target_pairs={{0,8},{4,12},{8,16},{12,20},{16,24},{20,28},{24,0},{28,4},{1,9},{5... | collective-permute-start | bytes 811016 | tf_op jit(solution)/shard_map/ppermute | solution.py:49
  113.6 66.8 %all-to-all-start = ((bf16[3,8,176,256]{3,2,0,1:T(8,128)(2,1)}), bf16[3,8,176,256]{3,2,0,1:T(8,128)(2,1)}, u32[]{:S(2)}, u32[]{:S(2)}) async-start(bf16[3,8,176,256]{3,2,0,1:T(8,128)(2,1)} %copy.187), calls=%async_computation | async-start | bytes 4325376 | tf_op jit(solution)/shard_map/all_to_all | solution.py:347
  128.8 21.7 %collective-permute-start.11 = (bf16[528,256]{1,0:T(8,128)(2,1)}, bf16[528,256]{1,0:T(8,128)(2,1)}, u32[]{:S(2)}, u32[]{:S(2)}) collective-permute-start(bf16[528,256]{1,0:T(8,128)(2,1)} %collective-permute-done.8), channel_id=1, source_target_pairs={{0,4},{4,0},{8,12},{12,8},{16,20},{20,16},{24,28},{28,24},{1,5},{5... | collective-permute-start | bytes 811016 | tf_op jit(solution)/shard_map/ppermute | solution.py:44
  130.8 30.3 %collective-permute-start.10 = (bf16[528,256]{1,0:T(8,128)(2,1)}, bf16[528,256]{1,0:T(8,128)(2,1)}, u32[]{:S(2)}, u32[]{:S(2)}) collective-permute-start(bf16[528,256]{1,0:T(8,128)(2,1)} %collective-permute-done.8), channel_id=1, source_target_pairs={{0,8},{4,12},{8,16},{12,20},{16,24},{20,28},{24,0},{28,4},{1,9},{5... | collective-permute-start | bytes 811016 | tf_op jit(solution)/shard_map/ppermute | solution.py:49
  161.1 22.5 %collective-permute-start.12 = (bf16[528,256]{1,0:T(8,128)(2,1)}, bf16[528,256]{1,0:T(8,128)(2,1)}, u32[]{:S(2)}, u32[]{:S(2)}) collective-permute-start(bf16[528,256]{1,0:T(8,128)(2,1)} %collective-permute-done.10), channel_id=1, source_target_pairs={{0,4},{4,0},{8,12},{12,8},{16,20},{20,16},{24,28},{28,24},{1,5},{5... | collective-permute-start | bytes 811016 | tf_op jit(solution)/shard_map/ppermute | solution.py:44
  162.4 21.2 %collective-permute-start.13 = (bf16[528,256]{1,0:T(8,128)(2,1)}, bf16[528,256]{1,0:T(8,128)(2,1)}, u32[]{:S(2)}, u32[]{:S(2)}) collective-permute-start(bf16[528,256]{1,0:T(8,128)(2,1)} %collective-permute-done.10), channel_id=1, source_target_pairs={{0,8},{4,12},{8,16},{12,20},{16,24},{20,28},{24,0},{28,4},{1,9},{5... | collective-permute-start | bytes 811016 | tf_op jit(solution)/shard_map/ppermute | solution.py:49
  212.9 49.8 %collective-permute-start.29 = (bf16[3,176,2048]{2,1,0:T(8,128)(2,1)}, bf16[3,176,2048]{2,1,0:T(8,128)(2,1)}, u32[]{:S(2)}, u32[]{:S(2)}) collective-permute-start(bf16[3,176,2048]{2,1,0:T(8,128)(2,1)} %bitcast.365), channel_id=1, source_target_pairs={{0,2},{1,3},{2,0},{3,1},{4,6},{5,7},{6,4},{7,5},{8,10},{9,11},{10,... | collective-permute-start | bytes 6488072 | tf_op jit(solution)/shard_map/ppermute | solution.py:54
  213.5 58.1 %collective-permute-start.30 = (bf16[3,176,2048]{2,1,0:T(8,128)(2,1)}, bf16[3,176,2048]{2,1,0:T(8,128)(2,1)}, u32[]{:S(2)}, u32[]{:S(2)}) collective-permute-start(bf16[3,176,2048]{2,1,0:T(8,128)(2,1)} %bitcast.366), channel_id=1, source_target_pairs={{0,1},{1,0},{2,3},{3,2},{4,5},{5,4},{6,7},{7,6},{8,9},{9,8},{10,11... | collective-permute-start | bytes 6488072 | tf_op jit(solution)/shard_map/ppermute | solution.py:54
  255.0 32.4 %collective-permute-start.27 = (bf16[96,2048]{1,0:T(8,128)(2,1)S(1)}, bf16[96,2048]{1,0:T(8,128)(2,1)}, u32[]{:S(2)}, u32[]{:S(2)}) collective-permute-start(bf16[96,2048]{1,0:T(8,128)(2,1)S(1)} %constant_dynamic-slice_fusion), channel_id=1, source_target_pairs={{0,4},{4,0},{8,12},{12,8},{16,20},{20,16},{24,28},{28,24},{1,5},{5... | collective-permute-start | bytes 1179656 | tf_op jit(solution)/shard_map/ppermute | solution.py:44
  255.4 32.0 %collective-permute-start.26 = (bf16[96,2048]{1,0:T(8,128)(2,1)S(1)}, bf16[96,2048]{1,0:T(8,128)(2,1)}, u32[]{:S(2)}, u32[]{:S(2)}) collective-permute-start(bf16[96,2048]{1,0:T(8,128)(2,1)S(1)} %constant_dynamic-slice_fusion), channel_id=1, source_target_pairs={{0,8},{4,12},{8,16},{12,20},{16,24},{20,28},{24,0},{28,4},{1,9},{5... | collective-permute-start | bytes 1179656 | tf_op jit(solution)/shard_map/ppermute | solution.py:49
  287.5 17.9 %collective-permute-start.33 = (bf16[96,2048]{1,0:T(8,128)(2,1)}, bf16[96,2048]{1,0:T(8,128)(2,1)S(1)}, u32[]{:S(2)}, u32[]{:S(2)}) collective-permute-start(bf16[96,2048]{1,0:T(8,128)(2,1)} %collective-permute-done.26), channel_id=1, source_target_pairs={{0,4},{4,0},{8,12},{12,8},{16,20},{20,16},{24,28},{28,24},{1,5},{5... | collective-permute-start | bytes 1179656 | tf_op jit(solution)/shard_map/ppermute | solution.py:44
  322.1 28.8 %collective-permute-start.35 = (bf16[96,2048]{1,0:T(8,128)(2,1)}, bf16[96,2048]{1,0:T(8,128)(2,1)}, u32[]{:S(2)}, u32[]{:S(2)}) collective-permute-start(bf16[96,2048]{1,0:T(8,128)(2,1)} %get-tuple-element.535), channel_id=1, source_target_pairs={{0,4},{4,0},{8,12},{12,8},{16,20},{20,16},{24,28},{28,24},{1,5},{5... | collective-permute-start | bytes 1179656 | tf_op jit(solution)/shard_map/ppermute | solution.py:44
  352.1 20.2 %collective-permute-start.40 = (bf16[96,2048]{1,0:T(8,128)(2,1)S(1)}, bf16[96,2048]{1,0:T(8,128)(2,1)S(1)}, u32[]{:S(2)}, u32[]{:S(2)}) collective-permute-start(bf16[96,2048]{1,0:T(8,128)(2,1)S(1)} %add_convert_fusion.11), channel_id=1, source_target_pairs={{0,8},{4,12},{8,16},{12,20},{16,24},{20,28},{24,0},{28,4},{1,9},{5... | collective-permute-start | bytes 1179656 | tf_op jit(solution)/shard_map/ppermute | solution.py:49
  404.7 21.5 %collective-permute-start.45 = (bf16[3,352,2048]{2,1,0:T(8,128)(2,1)S(1)}, bf16[3,352,2048]{2,1,0:T(8,128)(2,1)S(1)}, u32[]{:S(2)}, u32[]{:S(2)}) collective-permute-start(bf16[3,352,2048]{2,1,0:T(8,128)(2,1)S(1)} %slice.845), channel_id=1, source_target_pairs={{0,1},{1,0},{2,3},{3,2},{4,5},{5,4},{6,7},{7,6},{8,9},{9,8},{10,11... | collective-permute-start | bytes 12976136 | tf_op jit(solution)/shard_map/ppermute | solution.py:54
  412.4 37.0 %collective-permute-start.60 = (bf16[704,2048]{1,0:T(8,128)(2,1)S(1)}, bf16[704,2048]{1,0:T(8,128)(2,1)}, u32[]{:S(2)}, u32[]{:S(2)}) collective-permute-start(bf16[704,2048]{1,0:T(8,128)(2,1)S(1)} %slice.847), channel_id=1, source_target_pairs={{0,1},{1,0},{2,3},{3,2},{4,5},{5,4},{6,7},{7,6},{8,9},{9,8},{10,11... | collective-permute-start | bytes 8650760 | tf_op jit(solution)/shard_map/ppermute | solution.py:54
  413.0 68.6 %collective-permute-start.43 = (bf16[96,2048]{1,0:T(8,128)(2,1)}, bf16[96,2048]{1,0:T(8,128)(2,1)}, u32[]{:S(2)}, u32[]{:S(2)}) collective-permute-start(bf16[96,2048]{1,0:T(8,128)(2,1)} %add_convert_fusion.9), channel_id=1, source_target_pairs={{0,8},{4,12},{8,16},{12,20},{16,24},{20,28},{24,0},{28,4},{1,9},{5... | collective-permute-start | bytes 1179656 | tf_op jit(solution)/shard_map/ppermute | solution.py:49
  429.0 47.2 %collective-permute-start.49 = (bf16[3,176,2048]{2,1,0:T(8,128)(2,1)}, bf16[3,176,2048]{2,1,0:T(8,128)(2,1)}, u32[]{:S(2)}, u32[]{:S(2)}) collective-permute-start(bf16[3,176,2048]{2,1,0:T(8,128)(2,1)} %add_convert_fusion.2), channel_id=1, source_target_pairs={{0,2},{1,3},{2,0},{3,1},{4,6},{5,7},{6,4},{7,5},{8,10},{9,11},{10,... | collective-permute-start | bytes 6488072 | tf_op jit(solution)/shard_map/ppermute | solution.py:54
  452.3 55.7 %collective-permute-start.62 = (bf16[704,2048]{1,0:T(8,128)(2,1)}, bf16[704,2048]{1,0:T(8,128)(2,1)}, u32[]{:S(2)}, u32[]{:S(2)}) collective-permute-start(bf16[704,2048]{1,0:T(8,128)(2,1)} %slice.850), channel_id=1, source_target_pairs={{0,1},{1,0},{2,3},{3,2},{4,5},{5,4},{6,7},{7,6},{8,9},{9,8},{10,11... | collective-permute-start | bytes 8650760 | tf_op jit(solution)/shard_map/ppermute | solution.py:54
  454.7 26.8 %collective-permute-start.48 = (bf16[96,2048]{1,0:T(8,128)(2,1)S(1)}, bf16[96,2048]{1,0:T(8,128)(2,1)S(1)}, u32[]{:S(2)}, u32[]{:S(2)}) collective-permute-start(bf16[96,2048]{1,0:T(8,128)(2,1)S(1)} %copy-done.37), channel_id=1, source_target_pairs={{0,4},{4,0},{8,12},{12,8},{16,20},{20,16},{24,28},{28,24},{1,5},{5... | collective-permute-start | bytes 1179656 | tf_op jit(solution)/shard_map/ppermute | solution.py:44
  460.3 21.3 %collective-permute-start.52 = (bf16[96,2048]{1,0:T(8,128)(2,1)S(1)}, bf16[96,2048]{1,0:T(8,128)(2,1)S(1)}, u32[]{:S(2)}, u32[]{:S(2)}) collective-permute-start(bf16[96,2048]{1,0:T(8,128)(2,1)S(1)} %add_convert_fusion.6), channel_id=1, source_target_pairs={{0,8},{4,12},{8,16},{12,20},{16,24},{20,28},{24,0},{28,4},{1,9},{5... | collective-permute-start | bytes 1179656 | tf_op jit(solution)/shard_map/ppermute | solution.py:49
  486.6 20.2 %collective-permute-start.53 = (bf16[96,2048]{1,0:T(8,128)(2,1)}, bf16[96,2048]{1,0:T(8,128)(2,1)S(1)}, u32[]{:S(2)}, u32[]{:S(2)}) collective-permute-start(bf16[96,2048]{1,0:T(8,128)(2,1)} %get-tuple-element.513), channel_id=1, source_target_pairs={{0,2},{1,3},{2,0},{3,1},{4,6},{5,7},{6,4},{7,5},{8,10},{9,11},{10,... | collective-permute-start | bytes 1179656 | tf_op jit(solution)/shard_map/ppermute | solution.py:54
  488.1 18.9 %collective-permute-start.54 = (bf16[96,2048]{1,0:T(8,128)(2,1)}, bf16[96,2048]{1,0:T(8,128)(2,1)}, u32[]{:S(2)}, u32[]{:S(2)}) collective-permute-start(bf16[96,2048]{1,0:T(8,128)(2,1)} %get-tuple-element.513), channel_id=1, source_target_pairs={{0,1},{1,0},{2,3},{3,2},{4,5},{5,4},{6,7},{7,6},{8,9},{9,8},{10,11... | collective-permute-start | bytes 1179656 | tf_op jit(solution)/shard_map/ppermute | solution.py:54
  488.1 112.2 %all-to-all-start.1 = ((bf16[3,8,176,256]{3,2,0,1:T(8,128)(2,1)}), bf16[3,8,176,256]{3,2,0,1:T(8,128)(2,1)}, u32[]{:S(2)}, u32[]{:S(2)}) async-start(bf16[3,8,176,256]{3,2,0,1:T(8,128)(2,1)} %bitcast.354), calls=%async_computation.1 | async-start | bytes 4325376 | tf_op jit(solution)/shard_map/all_to_all | solution.py:610
  504.3 48.4 %collective-permute-start.63 = (bf16[704,2048]{1,0:T(8,128)(2,1)}, bf16[704,2048]{1,0:T(8,128)(2,1)}, u32[]{:S(2)}, u32[]{:S(2)}) collective-permute-start(bf16[704,2048]{1,0:T(8,128)(2,1)} %slice.852), channel_id=1, source_target_pairs={{0,1},{1,0},{2,3},{3,2},{4,5},{5,4},{6,7},{7,6},{8,9},{9,8},{10,11... | collective-permute-start | bytes 8650760 | tf_op jit(solution)/shard_map/ppermute | solution.py:54
  522.5 24.1 %collective-permute-start.56 = (bf16[96,2048]{1,0:T(8,128)(2,1)S(1)}, bf16[96,2048]{1,0:T(8,128)(2,1)}, u32[]{:S(2)}, u32[]{:S(2)}) collective-permute-start(bf16[96,2048]{1,0:T(8,128)(2,1)S(1)} %get-tuple-element.381), channel_id=1, source_target_pairs={{0,2},{1,3},{2,0},{3,1},{4,6},{5,7},{6,4},{7,5},{8,10},{9,11},{10,... | collective-permute-start | bytes 1179656 | tf_op jit(solution)/shard_map/ppermute | solution.py:54
  523.0 25.4 %collective-permute-start.57 = (bf16[96,2048]{1,0:T(8,128)(2,1)S(1)}, bf16[96,2048]{1,0:T(8,128)(2,1)}, u32[]{:S(2)}, u32[]{:S(2)}) collective-permute-start(bf16[96,2048]{1,0:T(8,128)(2,1)S(1)} %get-tuple-element.381), channel_id=1, source_target_pairs={{0,1},{1,0},{2,3},{3,2},{4,5},{5,4},{6,7},{7,6},{8,9},{9,8},{10,11... | collective-permute-start | bytes 1179656 | tf_op jit(solution)/shard_map/ppermute | solution.py:54
  534.6 133.7 %collective-permute-start.86 = (bf16[352,2048]{1,0:T(8,128)(2,1)}, bf16[352,2048]{1,0:T(8,128)(2,1)}, u32[]{:S(2)}, u32[]{:S(2)}) collective-permute-start(bf16[352,2048]{1,0:T(8,128)(2,1)} %add_convert_fusion.5), channel_id=1, source_target_pairs={{0,2},{1,3},{2,0},{3,1},{4,6},{5,7},{6,4},{7,5},{8,10},{9,11},{10,... | collective-permute-start | bytes 4325384 | tf_op jit(solution)/shard_map/ppermute | solution.py:54
  542.0 20.4 %collective-permute-start.81 = (bf16[256,640]{0,1:T(8,128)(2,1)S(1)}, bf16[256,640]{0,1:T(8,128)(2,1)S(1)}, u32[]{:S(2)}, u32[]{:S(2)}) collective-permute-start(bf16[256,640]{0,1:T(8,128)(2,1)S(1)} %fusion.72), channel_id=1, source_target_pairs={{0,8},{4,12},{8,16},{12,20},{16,24},{20,28},{24,0},{28,4},{1,9},{5... | collective-permute-start | bytes 983048 | tf_op jit(solution)/shard_map/ppermute | solution.py:49
  550.4 117.9 %collective-permute-start.87 = (bf16[352,2048]{1,0:T(8,128)(2,1)}, bf16[352,2048]{1,0:T(8,128)(2,1)}, u32[]{:S(2)}, u32[]{:S(2)}) collective-permute-start(bf16[352,2048]{1,0:T(8,128)(2,1)} %add_convert_fusion.4), channel_id=1, source_target_pairs={{0,2},{1,3},{2,0},{3,1},{4,6},{5,7},{6,4},{7,5},{8,10},{9,11},{10,... | collective-permute-start | bytes 4325384 | tf_op jit(solution)/shard_map/ppermute | solution.py:54
  579.8 20.5 %collective-permute-start.67 = (bf16[256,1536]{1,0:T(8,128)(2,1)S(1)}, bf16[256,1536]{1,0:T(8,128)(2,1)}, u32[]{:S(2)}, u32[]{:S(2)}) collective-permute-start(bf16[256,1536]{1,0:T(8,128)(2,1)S(1)} %get-tuple-element.527), channel_id=1, source_target_pairs={{0,4},{4,0},{8,12},{12,8},{16,20},{20,16},{24,28},{28,24},{1,5},{5... | collective-permute-start | bytes 2359304 | tf_op jit(solution)/shard_map/ppermute | solution.py:44
  584.5 19.8 %collective-permute-start.64 = (bf16[96,2048]{1,0:T(8,128)(2,1)S(1)}, bf16[96,2048]{1,0:T(8,128)(2,1)}, u32[]{:S(2)}, u32[]{:S(2)}) collective-permute-start(bf16[96,2048]{1,0:T(8,128)(2,1)S(1)} %get-tuple-element.550), channel_id=1, source_target_pairs={{0,1},{1,0},{2,3},{3,2},{4,5},{5,4},{6,7},{7,6},{8,9},{9,8},{10,11... | collective-permute-start | bytes 1179656 | tf_op jit(solution)/shard_map/ppermute | solution.py:54
  602.7 39.8 %collective-permute-start.74 = (bf16[256,1536]{1,0:T(8,128)(2,1)}, bf16[256,1536]{1,0:T(8,128)(2,1)}, u32[]{:S(2)}, u32[]{:S(2)}) collective-permute-start(bf16[256,1536]{1,0:T(8,128)(2,1)} %fusion.28), channel_id=1, source_target_pairs={{0,8},{4,12},{8,16},{12,20},{16,24},{20,28},{24,0},{28,4},{1,9},{5... | collective-permute-start | bytes 2359304 | tf_op jit(solution)/shard_map/ppermute | solution.py:49
  622.3 20.2 %collective-permute-start.71 = (bf16[256,1536]{1,0:T(8,128)(2,1)}, bf16[256,1536]{1,0:T(8,128)(2,1)S(1)}, u32[]{:S(2)}, u32[]{:S(2)}) collective-permute-start(bf16[256,1536]{1,0:T(8,128)(2,1)} %get-tuple-element.408), channel_id=1, source_target_pairs={{0,4},{4,0},{8,12},{12,8},{16,20},{20,16},{24,28},{28,24},{1,5},{5... | collective-permute-start | bytes 2359304 | tf_op jit(solution)/shard_map/ppermute | solution.py:44
  623.4 44.8 %collective-permute-start.88 = (bf16[352,2048]{1,0:T(8,128)(2,1)S(1)}, bf16[352,2048]{1,0:T(8,128)(2,1)S(1)}, u32[]{:S(2)}, u32[]{:S(2)}) collective-permute-start(bf16[352,2048]{1,0:T(8,128)(2,1)S(1)} %copy-done.27), channel_id=1, source_target_pairs={{0,2},{1,3},{2,0},{3,1},{4,6},{5,7},{6,4},{7,5},{8,10},{9,11},{10,... | collective-permute-start | bytes 4325384 | tf_op jit(solution)/shard_map/ppermute | solution.py:54
  642.5 20.0 %collective-permute-start.72 = (bf16[256,1536]{1,0:T(8,128)(2,1)S(1)}, bf16[256,1536]{1,0:T(8,128)(2,1)S(1)}, u32[]{:S(2)}, u32[]{:S(2)}) collective-permute-start(bf16[256,1536]{1,0:T(8,128)(2,1)S(1)} %copy-done.35), channel_id=1, source_target_pairs={{0,4},{4,0},{8,12},{12,8},{16,20},{20,16},{24,28},{28,24},{1,5},{5... | collective-permute-start | bytes 2359304 | tf_op jit(solution)/shard_map/ppermute | solution.py:44
  645.3 21.5 %collective-permute-start.75 = (bf16[256,1536]{1,0:T(8,128)(2,1)S(1)}, bf16[256,1536]{1,0:T(8,128)(2,1)S(1)}, u32[]{:S(2)}, u32[]{:S(2)}) collective-permute-start(bf16[256,1536]{1,0:T(8,128)(2,1)S(1)} %fusion.24), channel_id=1, source_target_pairs={{0,8},{4,12},{8,16},{12,20},{16,24},{20,28},{24,0},{28,4},{1,9},{5... | collective-permute-start | bytes 2359304 | tf_op jit(solution)/shard_map/ppermute | solution.py:49
  662.5 19.0 %collective-permute-start.73 = (bf16[256,1536]{1,0:T(8,128)(2,1)S(1)}, bf16[256,1536]{1,0:T(8,128)(2,1)S(1)}, u32[]{:S(2)}, u32[]{:S(2)}) collective-permute-start(bf16[256,1536]{1,0:T(8,128)(2,1)S(1)} %copy-done.34), channel_id=1, source_target_pairs={{0,4},{4,0},{8,12},{12,8},{16,20},{20,16},{24,28},{28,24},{1,5},{5... | collective-permute-start | bytes 2359304 | tf_op jit(solution)/shard_map/ppermute | solution.py:44
  668.2 20.6 %collective-permute-start.76 = (bf16[256,1536]{1,0:T(8,128)(2,1)S(1)}, bf16[256,1536]{1,0:T(8,128)(2,1)S(1)}, u32[]{:S(2)}, u32[]{:S(2)}) collective-permute-start(bf16[256,1536]{1,0:T(8,128)(2,1)S(1)} %fusion.26), channel_id=1, source_target_pairs={{0,8},{4,12},{8,16},{12,20},{16,24},{20,28},{24,0},{28,4},{1,9},{5... | collective-permute-start | bytes 2359304 | tf_op jit(solution)/shard_map/ppermute | solution.py:49
  (128 other events, 1334.7 us)
